TPU v7x, 768 devices: a whole 4x8x12 slice. The times are simulated.
768 devices in a mesh: ew: 16 (over z_hi, y), ns: 48 (over z_lo, x, core).
Axes of the slice: x: 4, y: 8, z: 12 (z_hi: 2, z_lo: 6; z = z_hi * 6 + z_lo), core: 2. Of those that a mesh axis runs over, the one named last changes fastest.
Arguments:
- tokens: bfloat16 [48, 16, 2, 64, 768], P('ns', 'ew'), may hold values from -6 to 6
- vis_index: int32 [48, 16, 2, 64], P('ns', 'ew'), may hold values from 0 to 255, as said below
- counts: int32 [48, 16, 2], P('ns', 'ew'), may hold values from 32 to 64
- owners: int32 [48, 16, 2, 64, 1], P('ns', 'ew'), may hold values from 0 to 47; in each aligned block of 128 rows (0 to 127, 128 to 255, ..., all dimensions but the last counted through in order) at most 4 rows name the same one
- mask_token: bfloat16 [768], replicated, may hold values from -6 to 6
- proj_weight: bfloat16 [768, 64], replicated, may hold values from -0.21875 to 0.21875
- up_first: bfloat16 [4, 4, 64, 64], replicated, may hold values from -0.375 to 0.375
- up_second: bfloat16 [4, 4, 12, 64], replicated, may hold values from -0.375 to 0.375
- saved_pre: bfloat16 [2, 64, 384, 2048], P(None, None, 'ns', 'ew'), may hold values from -6 to 6
- cotangent: bfloat16 [2, 12, 768, 4096], P(None, None, 'ns', 'ew'), may hold values from -6 to 6
Outputs:
- token_grad: bfloat16 [48, 16, 192, 768], P('ns', 'ew')
- grad_proj: float32 [768, 64], replicated
- grad_first: float32 [4, 4, 64, 64], replicated
- grad_second: float32 [4, 4, 12, 64], replicated
- grad_mask: float32 [768], replicated
Inputs may be any that keep to these rules, and one draw needn't show every extreme that they name: `vis_index`: each entry is a patch number of its tile, patches numbered row by row with 64 to a row; the 64 entries of one tile and date are distinct; the live ones are the first counts entries. `owners`: among the 128 slots of one tile, live or not, at most 4 name the same owner.
All inputs are finite; a program needn't handle non-finite values.
Results may differ from a plain program's by a relative error of at most 0.0057.
Values may be sent and summed in bfloat16 or wider, within the bound.
A program may use at most 32 MiB of HBM per device.

v0:
```python
import jax
import jax.numpy as jnp
from jax import lax
from jax.sharding import PartitionSpec as P


def padded_2(block, sides, width):
    for axis, dim in sides:
        count = lax.axis_size(axis)
        forward = [(i, i + 1) for i in range(count - 1)]
        backward = [(target, source) for source, target in forward]
        low = lax.ppermute(
            lax.slice_in_dim(block, block.shape[dim] - width, None, axis=dim), axis, forward
        )
        high = lax.ppermute(lax.slice_in_dim(block, 0, width, axis=dim), axis, backward)
        block = jnp.concatenate([low, block, high], axis=dim)
    return block


def gelu_value(preact):
    return preact * jax.nn.sigmoid(1.702 * preact)


def gelu_slope(preact):
    sigmoid_value = jax.nn.sigmoid(1.702 * preact)
    return sigmoid_value + 1.702 * preact * sigmoid_value * (1.0 - sigmoid_value)


def transpose_back(inputs, padded, kernel):
    height = inputs.shape[2]
    breadth = inputs.shape[3]
    grad_inputs = None
    grad_taps = []
    for tap_y in range(4):
        for tap_x in range(4):
            window = padded[:, :, tap_y : tap_y + 2 * height : 2, tap_x : tap_x + 2 * breadth : 2]
            partial_term = jnp.einsum(
                "oi,fohw->fihw", kernel[tap_y, tap_x], window, preferred_element_type=jnp.float32
            )
            grad_inputs = partial_term if grad_inputs is None else grad_inputs + partial_term
            grad_taps.append(
                jnp.einsum("fihw,fohw->oi", inputs, window, preferred_element_type=jnp.float32)
            )
    grad_kernel = jnp.stack(grad_taps).reshape((4, 4) + kernel.shape[2:])
    return (grad_inputs, grad_kernel)


def per_device(
    tokens,
    vis_index,
    counts,
    owners,
    mask_token,
    proj_weight,
    up_first,
    up_second,
    saved_pre,
    cotangent,
):
    tile_tokens = tokens[0, 0]
    tile_index = vis_index[0, 0]
    tile_counts = counts[0, 0]
    tile_owners = owners[0, 0, :, :, 0]
    frames, slots, features = tile_tokens.shape
    channels = proj_weight.shape[1]
    tok_rows = saved_pre.shape[2] // 2
    tok_cols = saved_pre.shape[3] // 2
    patches = tok_rows * tok_cols
    is_live = jnp.arange(slots, dtype=jnp.int32)[None, :] < tile_counts[:, None]
    picks = (
        tile_index[:, :, None] == jnp.arange(patches, dtype=jnp.int32)[None, None, :]
    ) & is_live[:, :, None]
    picks_half = picks.astype(jnp.bfloat16)
    hidden_mask = 1.0 - jnp.sum(picks.astype(jnp.float32), axis=1)
    token_proj = jnp.einsum(
        "fvd,dc->fvc", tile_tokens, proj_weight, preferred_element_type=jnp.float32
    ).astype(jnp.bfloat16)
    mask_proj = jnp.dot(
        mask_token[None, :], proj_weight, preferred_element_type=jnp.float32
    ).astype(jnp.bfloat16)[0]
    placed = jnp.einsum("fvp,fvc->fcp", picks_half, token_proj, preferred_element_type=jnp.float32)
    placed = placed + hidden_mask[:, None, :] * mask_proj.astype(jnp.float32)[None, :, None]
    first_in = placed.astype(jnp.bfloat16).reshape(frames, channels, tok_rows, tok_cols)
    padded_cot = padded_2(cotangent, (("ew", 3), ("ns", 2)), 1)
    pre_wide = saved_pre.astype(jnp.float32)
    hidden = gelu_value(pre_wide).astype(jnp.bfloat16)
    grad_hidden, grad_second = transpose_back(hidden, padded_cot, up_second)
    deltas = (grad_hidden * gelu_slope(pre_wide)).astype(jnp.bfloat16)
    padded_deltas = padded_2(deltas, (("ew", 3), ("ns", 2)), 1)
    grad_grid, grad_first = transpose_back(first_in, padded_deltas, up_first)
    grad_grid = grad_grid.astype(jnp.bfloat16).reshape(frames, channels, patches)
    chosen = jnp.einsum(
        "fvp,fcp->fvc", picks_half, grad_grid, preferred_element_type=jnp.float32
    ).astype(jnp.bfloat16)
    mask_sum = jnp.einsum(
        "fp,fcp->c", hidden_mask, grad_grid.astype(jnp.float32), precision=lax.Precision.HIGHEST
    )
    grad_proj = jnp.einsum("fvd,fvc->dc", tile_tokens, chosen, preferred_element_type=jnp.float32)
    grad_proj = grad_proj + mask_token.astype(jnp.float32)[:, None] * mask_sum[None, :]
    grad_proj, grad_first, grad_second, mask_sum = lax.psum(
        (grad_proj, grad_first, grad_second, mask_sum), ("ew", "ns")
    )
    grad_mask = jnp.dot(proj_weight.astype(jnp.float32), mask_sum, precision=lax.Precision.HIGHEST)
    owner_count = lax.axis_size("ns")
    row_count = frames * slots
    capacity = 3 * row_count // (2 * owner_count)
    owner_rows = tile_owners.reshape(row_count)
    live_rows = is_live.reshape(row_count)
    owner_hits = (
        (owner_rows[:, None] == jnp.arange(owner_count, dtype=jnp.int32)[None, :])
        & live_rows[:, None]
    ).astype(jnp.int32)
    earlier = jnp.cumsum(owner_hits, axis=0, dtype=jnp.int32) - owner_hits
    place = jnp.sum(earlier * owner_hits, axis=1, dtype=jnp.int32)
    target = jnp.where(live_rows, owner_rows * capacity + place, owner_count * capacity)
    token_rows = jnp.einsum(
        "fvc,dc->fvd", chosen, proj_weight, preferred_element_type=jnp.float32
    ).astype(jnp.bfloat16)
    outgoing = jnp.zeros((owner_count * capacity, features), jnp.bfloat16)
    outgoing = outgoing.at[target].set(token_rows.reshape(row_count, features), mode="drop")
    arrived = lax.all_to_all(
        outgoing.reshape(owner_count, capacity, features),
        "ns",
        split_axis=0,
        concat_axis=0,
        tiled=True,
    )
    token_grad = arrived.reshape(owner_count * capacity, features)
    return (token_grad[None, None], grad_proj, grad_first, grad_second, grad_mask)


def solution(mesh):
    return jax.shard_map(
        per_device,
        mesh=mesh,
        in_specs=(
            P("ns", "ew", None, None, None),
            P("ns", "ew", None, None),
            P("ns", "ew", None),
            P("ns", "ew", None, None, None),
            P(),
            P(),
            P(),
            P(),
            P(None, None, "ns", "ew"),
            P(None, None, "ns", "ew"),
        ),
        out_specs=(P("ns", "ew", None, None), P(), P(), P(), P()),
        check_vma=False,
    )
```

profile of v0, /device:TPU:1, one launch (start us, length us, event | category | flops | bytes accessed | tf_op | source)
XLA Modules:
  0.0 742.3 jit_solution(12657122075901382665)
XLA Ops:
  8.4 4.0 collective-permute-start
  13.7 3.6 slice.230
  23.9 3.6 slice.228
  27.5 3.7 slice.234
  31.2 4.0 collective-permute-start.2
  35.2 7.0 collective-permute-start.3
  42.7 3.7 slice.232
  48.2 6.7 slice.220
  55.0 3.6 slice.222
  58.6 3.7 slice.224
  62.3 3.7 slice.226
  66.0 6.7 slice.236
  72.7 6.7 slice.238
  79.4 6.7 slice.240
  86.1 6.7 slice.242
  92.8 6.7 slice.244
  99.6 6.7 slice.246
  106.3 4.0 slice.248
  110.3 4.1 slice.250
  126.8 4.3 collective-permute-start.4
  137.2 4.1 collective-permute-done.5
  158.6 3.0 slice.262
  161.5 3.0 slice.260
  164.5 3.0 slice.258
  170.4 3.0 slice.276
  179.2 3.1 slice.286
  182.3 3.1 slice.284
  185.4 3.1 slice.282
  188.6 3.1 slice.280
  206.2 12.7 %all-to-all-start = ((bf16[48,4,768]{2,1,0:T(4,128)(2,1)}), bf16[48,4,768]{2,1,0:T(4,128)(2,1)S(1)}, u32[]{:S(2)}, u32[]{:S(2)}) async-start(bf16[48,4,768]{2,1,0:T(4,128)(2,1)} %reshape.132), calls=%async_computation | async-start | bytes 589824 | tf_op jit(solution)/shard_map/all_to_all | solution.py:121
  221.1 142.9 %all-reduce = (f32[4,4,12,64]{3,1,2,0:T(4,128)}, f32[64]{0:T(128)S(1)}) all-reduce(f32[4,4,12,64]{3,1,2,0:T(4,128)S(1)} %copy.70, f32[64]{0:T(128)S(1)} %convolution_bitcast_fusion.33), channel_id=1, replica_groups=mesh['ew'=16,'ns'=48] {'ew','ns'}, use_global_device_ids=true, to_apply=%region_6.7 | all-reduce | flops 12352 | bytes 98816 | tf_op jit(solution)/shard_map/psum | solution.py:100
  365.5 366.4 %all-reduce.4.cloned.1.call-done = (f32[768,64]{0,1:T(8,128)}, f32[4,4,64,64]{3,2,1,0:T(8,128)}) async-done(((f32[768,64]{0,1:T(8,128)}, f32[4,4,64,64]{3,2,1,0:T(8,128)}), (f32[768,64]{0,1:T(8,128)}, f32[4,4,64,64]{3,2,1,0:T(8,128)})) %all-reduce.4.cloned.1.call-update) | async-done | bytes 458768 | tf_op jit(solution)/shard_map/psum | solution.py:100
  (224 shorter events, 76.8 us)
Async XLA Ops:
  7.2 14.3 %copy-start = (bf16[1,1,2,64,768]{4,3,2,1,0:T(8,128)(2,1)S(1)}, bf16[1,1,2,64,768]{4,3,2,1,0:T(8,128)(2,1)}, u32[]{:S(2)}) copy-start(bf16[1,1,2,64,768]{4,3,2,1,0:T(8,128)(2,1)} %param.10) | copy-start | bytes 589828
  7.2 10.2 %copy-start.48 = (s32[1,1,2]{2,1,0:T(1,128)S(1)}, s32[1,1,2]{2,1,0:T(1,128)}, u32[]{:S(2)}) copy-start(s32[1,1,2]{2,1,0:T(1,128)} %param.12) | copy-start | bytes 28
  7.2 10.5 %copy-start.1 = (bf16[2,64,8,128]{3,2,1,0:T(8,128)(2,1)S(1)}, bf16[2,64,8,128]{3,2,1,0:T(8,128)(2,1)}, u32[]{:S(2)}) copy-start(bf16[2,64,8,128]{3,2,1,0:T(8,128)(2,1)} %param.18) | copy-start | bytes 786436
  8.2 9.6 %copy-start.25 = (bf16[4,4,12,64]{3,1,2,0:T(4,128)(2,1)S(1)}, bf16[4,4,12,64]{3,1,2,0:T(4,128)(2,1)}, u32[]{:S(2)}) copy-start(bf16[4,4,12,64]{3,1,2,0:T(4,128)(2,1)} %param.17) | copy-start | bytes 73732
  8.3 10.3 %copy-start.44 = (s32[1,1,2,64]{3,2,1,0:T(2,128)S(1)}, s32[1,1,2,64]{3,2,1,0:T(2,128)}, u32[]{:S(2)}) copy-start(s32[1,1,2,64]{3,2,1,0:T(2,128)} %param.11) | copy-start | bytes 1540
  8.3 11.0 %copy-start.42 = (bf16[768]{0:T(1024)(128)(2,1)S(1)}, bf16[768]{0:T(1024)(128)(2,1)}, u32[]{:S(2)}) copy-start(bf16[768]{0:T(1024)(128)(2,1)} %param.14) | copy-start | bytes 4612
  8.3 11.5 %copy-start.43 = (s32[1,1,2,64,1]{3,4,2,1,0:T(1,128)S(1)}, s32[1,1,2,64,1]{3,4,2,1,0:T(1,128)}, u32[]{:S(2)}) copy-start(s32[1,1,2,64,1]{3,4,2,1,0:T(1,128)} %param.13) | copy-start | bytes 1540
  8.4 14.8 %collective-permute-start = (bf16[2,12,16,1]{3,1,2,0:T(8,128)(2,1)S(1)}, bf16[2,12,16,1]{3,1,2,0:T(8,128)(2,1)S(1)}, u32[]{:S(2)}, u32[]{:S(2)}) collective-permute-start(bf16[2,12,16,1]{3,1,2,0:T(8,128)(2,1)S(1)} %get-tuple-element.17), channel_id=1, source_target_pairs={{0,48},{48,96},{96,144},{144,192},{192,240},{240,288},{288,336},{3... | collective-permute-start | bytes 2312 | tf_op jit(solution)/shard_map/ppermute | solution.py:12
  12.4 10.8 %collective-permute-start.1 = (bf16[2,12,16,1]{3,1,2,0:T(8,128)(2,1)S(1)}, bf16[2,12,16,1]{3,1,2,0:T(8,128)(2,1)S(1)}, u32[]{:S(2)}, u32[]{:S(2)}) collective-permute-start(bf16[2,12,16,1]{3,1,2,0:T(8,128)(2,1)S(1)} %get-tuple-element.18), channel_id=1, source_target_pairs={{48,0},{96,48},{144,96},{192,144},{240,192},{288,240},{336,288},{3... | collective-permute-start | bytes 2312 | tf_op jit(solution)/shard_map/ppermute | solution.py:15
  17.5 4.0 copy-start.46
  17.8 3.5 copy-start.23
  23.2 19.2 %copy-start.22 = (bf16[2,12,16,1]{3,1,2,0:T(8,128)(2,1)}, bf16[2,12,16,1]{3,1,2,0:T(8,128)(2,1)S(1)}, u32[]{:S(2)}) copy-start(bf16[2,12,16,1]{3,1,2,0:T(8,128)(2,1)S(1)} %collective-permute-done.1) | copy-start | bytes 2308
  31.2 15.2 %collective-permute-start.2 = (bf16[2,12,1,258]{3,1,2,0:T(8,128)(2,1)S(1)}, bf16[2,12,1,258]{3,1,2,0:T(8,128)(2,1)S(1)}, u32[]{:S(2)}, u32[]{:S(2)}) collective-permute-start(bf16[2,12,1,258]{3,1,2,0:T(8,128)(2,1)S(1)} %get-tuple-element.13), channel_id=1, source_target_pairs={{0,1},{1,2},{2,3},{3,4},{4,5},{5,6},{6,7},{7,8},{8,9},{9,10},{10,1... | collective-permute-start | bytes 37160 | tf_op jit(solution)/shard_map/ppermute | solution.py:12
  35.2 11.8 %collective-permute-start.3 = (bf16[2,12,1,258]{3,1,2,0:T(8,128)(2,1)S(1)}, bf16[2,12,1,258]{3,1,2,0:T(8,128)(2,1)}, u32[]{:S(2)}, u32[]{:S(2)}) collective-permute-start(bf16[2,12,1,258]{3,1,2,0:T(8,128)(2,1)S(1)} %get-tuple-element.14), channel_id=1, source_target_pairs={{1,0},{2,1},{3,2},{4,3},{5,4},{6,5},{7,6},{8,7},{9,8},{10,9},{11,1... | collective-permute-start | bytes 37160 | tf_op jit(solution)/shard_map/ppermute | solution.py:15
  58.6 57.8 %copy-start.18 = (bf16[2,12,8,128]{3,1,2,0:T(8,128)(2,1)}, bf16[2,12,8,128]{3,1,2,0:T(8,128)(2,1)S(1)}, u32[]{:S(2)}) copy-start(bf16[2,12,8,128]{3,1,2,0:T(8,128)(2,1)S(1)} %slice.222) | copy-start | bytes 147460
  62.3 53.1 %copy-start.16 = (bf16[2,12,8,128]{3,1,2,0:T(8,128)(2,1)}, bf16[2,12,8,128]{3,1,2,0:T(8,128)(2,1)S(1)}, u32[]{:S(2)}) copy-start(bf16[2,12,8,128]{3,1,2,0:T(8,128)(2,1)S(1)} %slice.224) | copy-start | bytes 147460
  114.4 2.0 copy-start.39
  121.0 3.3 copy-start.19
  121.2 3.3 copy-start.17
  126.8 10.3 %collective-permute-start.4 = (bf16[2,64,8,1]{3,1,2,0:T(8,128)(2,1)S(1)}, bf16[2,64,8,1]{3,1,2,0:T(8,128)(2,1)S(1)}, u32[]{:S(2)}, u32[]{:S(2)}) collective-permute-start(bf16[2,64,8,1]{3,1,2,0:T(8,128)(2,1)S(1)} %get-tuple-element.15), channel_id=1, source_target_pairs={{0,48},{48,96},{96,144},{144,192},{192,240},{240,288},{288,336},{3... | collective-permute-start | bytes 6152 | tf_op jit(solution)/shard_map/ppermute | solution.py:12
  131.1 10.1 %collective-permute-start.5 = (bf16[2,64,8,1]{3,1,2,0:T(8,128)(2,1)S(1)}, bf16[2,64,8,1]{3,1,2,0:T(8,128)(2,1)S(1)}, u32[]{:S(2)}, u32[]{:S(2)}) collective-permute-start(bf16[2,64,8,1]{3,1,2,0:T(8,128)(2,1)S(1)} %get-tuple-element.16), channel_id=1, source_target_pairs={{48,0},{96,48},{144,96},{192,144},{240,192},{288,240},{336,288},{3... | collective-permute-start | bytes 6152 | tf_op jit(solution)/shard_map/ppermute | solution.py:15
  134.3 2.9 copy-start.26
  147.5 10.7 %collective-permute-start.6 = (bf16[2,64,1,130]{3,1,2,0:T(8,128)(2,1)S(1)}, bf16[2,64,1,130]{3,1,2,0:T(8,128)(2,1)S(1)}, u32[]{:S(2)}, u32[]{:S(2)}) collective-permute-start(bf16[2,64,1,130]{3,1,2,0:T(8,128)(2,1)S(1)} %get-tuple-element.11), channel_id=1, source_target_pairs={{0,1},{1,2},{2,3},{3,4},{4,5},{5,6},{6,7},{7,8},{8,9},{9,10},{10,1... | collective-permute-start | bytes 99848 | tf_op jit(solution)/shard_map/ppermute | solution.py:12
  149.4 8.8 %collective-permute-start.7 = (bf16[2,64,1,130]{3,1,2,0:T(8,128)(2,1)S(1)}, bf16[2,64,1,130]{3,1,2,0:T(8,128)(2,1)S(1)}, u32[]{:S(2)}, u32[]{:S(2)}) collective-permute-start(bf16[2,64,1,130]{3,1,2,0:T(8,128)(2,1)S(1)} %get-tuple-element.12), channel_id=1, source_target_pairs={{1,0},{2,1},{3,2},{4,3},{5,4},{6,5},{7,6},{8,7},{9,8},{10,9},{11,1... | collective-permute-start | bytes 99848 | tf_op jit(solution)/shard_map/ppermute | solution.py:15
  194.6 1.9 copy-start.24
  200.5 1.5 copy-start.2
  200.5 1.5 copy-start.3
  205.4 13.5 %copy-start.41 = (f32[2,256,1]{1,0,2:T(2,128)S(1)}, f32[2,256,1]{1,0,2:T(2,128)}, u32[]{:S(2)}) copy-start(f32[2,256,1]{1,0,2:T(2,128)} %get-tuple-element.36) | copy-start | bytes 6148
  206.2 13.7 %copy-start.40 = (f32[768]{0:T(1024)S(1)}, f32[768]{0:T(1024)}, u32[]{:S(2)}) copy-start(f32[768]{0:T(1024)} %convert_element_type.51) | copy-start | bytes 9220
  206.2 158.6 %all-to-all-start = ((bf16[48,4,768]{2,1,0:T(4,128)(2,1)}), bf16[48,4,768]{2,1,0:T(4,128)(2,1)S(1)}, u32[]{:S(2)}, u32[]{:S(2)}) async-start(bf16[48,4,768]{2,1,0:T(4,128)(2,1)} %reshape.132), calls=%async_computation | async-start | bytes 589824 | tf_op jit(solution)/shard_map/all_to_all | solution.py:121
  218.9 513.0 %all-reduce.4.cloned.1.call-start = ((), (), s32[]{:S(2)}) async-start(), calls=%async_computation.1 | async-start | bytes 1441792 | tf_op jit(solution)/shard_map/psum | solution.py:100
  219.1 1.7 copy-start.27
  (27 other events, 22.5 us)
Sparse Core Ops, SparseCore 0:
  226.0 505.8 all-reduce.3
where the time goes:
time: 745 us; the launch traced here: 742 us
  waiting for transfers between devices  373 us (50%)
  blocking collectives  143 us (19%)
  local copies, waits for them, and re-layouts  142 us (19%)
  starting transfers between devices  39.1 us (5%)
  matrix products  24.1 us (3%)
  between operations  15.2 us (2%)
    psum x1, waiting for transfers between devices, per_device(): lax.psum((grad_proj, grad_first, grad_second, mask_sum), ('ew', 'ns'))  366 us
    psum x1, blocking collectives, per_device(): lax.psum((grad_proj, grad_first, grad_second, mask_sum), ('ew', 'ns'))  143 us
    slice x32, local copies, waits for them, and re-layouts, transpose_back(): padded[:, :, tap_y:tap_y + 2 * height:2, tap_x:tap_x + 2 * breadth:2]  128 us
    dot_general x32, matrix products, transpose_back(): jnp.einsum('oi,fohw->fihw', kernel[tap_y, tap_x], window, preferred_eleme...  15.2 us
  transfers between devices with their start and end apart: 10, of which 3 were waited for; matrix products, arithmetic and copies ran while one was open for 3% of the time, Pallas kernels for 0%

commit v1 on v0

--- a/solution.py
+++ b/solution.py
@@ -1,7 +1,17 @@
+import functools
+
 import jax
 import jax.numpy as jnp
 from jax import lax
+from jax.experimental import pallas as pl
+from jax.experimental.pallas import tpu as pltpu
 from jax.sharding import PartitionSpec as P
+
+MESH = pl.DeviceIdType.MESH
+GROUP_A = 8
+GROUP_Y = 8
+Z_LOW = 6
+Z_HIGH = 2
 
 
 def padded_2(block, sides, width):
@@ -43,6 +53,225 @@
             )
     grad_kernel = jnp.stack(grad_taps).reshape((4, 4) + kernel.shape[2:])
     return (grad_inputs, grad_kernel)
+
+
+def exchange_kernel(
+    payload,
+    rows_out,
+    total_out,
+    rows_in,
+    buf_a,
+    red_a,
+    buf_b,
+    buf_c,
+    buf_d,
+    buf_s,
+    tok_z,
+    tok_s,
+    send_a,
+    recv_a,
+    send_b,
+    recv_b,
+    send_c,
+    recv_c,
+    send_d,
+    recv_d,
+    send_e,
+    recv_e,
+    send_z,
+    recv_z,
+    send_t,
+    recv_t,
+    local_sem,
+):
+    n = lax.axis_index("ns")
+    e = lax.axis_index("ew")
+    g = lax.rem(n, GROUP_A)
+    zl = lax.div(n, GROUP_A)
+    zh = lax.div(e, GROUP_Y)
+    y = lax.rem(e, GROUP_Y)
+    zi = zh * Z_LOW + zl
+    z_count = Z_LOW * Z_HIGH
+
+    def peer_a(k):
+        other = lax.rem(g + k, GROUP_A)
+        return other, {"ew": e, "ns": zl * GROUP_A + other}
+
+    def peer_b(k):
+        other = lax.rem(y + k, GROUP_Y)
+        return other, {"ew": zh * GROUP_Y + other, "ns": n}
+
+    def peer_c(k):
+        other = lax.rem(zi + k, z_count)
+        return other, {
+            "ew": lax.div(other, Z_LOW) * GROUP_Y + y,
+            "ns": lax.rem(other, Z_LOW) * GROUP_A + g,
+        }
+
+    def peer_z(k):
+        other = lax.rem(zl + k, Z_LOW)
+        return other, {"ew": e, "ns": other * GROUP_A + g}
+
+    barrier = pltpu.get_barrier_semaphore()
+    for count, peer in ((GROUP_A, peer_a), (GROUP_Y, peer_b), (z_count, peer_c)):
+        for k in range(1, count):
+            pl.semaphore_signal(barrier, inc=1, device_id=peer(k)[1], device_id_type=MESH)
+    pl.semaphore_wait(barrier, GROUP_A + GROUP_Y + z_count - 3)
+
+    def remote(src, dst, send, recv, target):
+        return pltpu.make_async_remote_copy(
+            src_ref=src,
+            dst_ref=dst,
+            send_sem=send,
+            recv_sem=recv,
+            device_id=target,
+            device_id_type=MESH,
+        )
+
+    copies_a = []
+    for k in range(1, GROUP_A):
+        other, target = peer_a(k)
+        copies_a.append(
+            remote(payload.at[other], buf_a.at[k - 1], send_a.at[k - 1], recv_a.at[k - 1], target)
+        )
+    for copy in copies_a:
+        copy.start()
+    copies_z = []
+    for k in range(1, Z_LOW):
+        other, target = peer_z(k)
+        copies_z.append(
+            remote(rows_out.at[other], tok_z.at[zl], send_z.at[k - 1], recv_z.at[k - 1], target)
+        )
+    for copy in copies_z:
+        copy.start()
+    tok_z[zl] = rows_out[zl]
+
+    for copy in copies_a:
+        copy.wait()
+    summed = payload[g]
+    for k in range(1, GROUP_A):
+        summed = summed + buf_a[k - 1]
+    red_a[...] = summed
+
+    copies_b = []
+    for k in range(1, GROUP_Y):
+        other, target = peer_b(k)
+        copies_b.append(
+            remote(red_a.at[other], buf_b.at[k - 1], send_b.at[k - 1], recv_b.at[k - 1], target)
+        )
+    for copy in copies_b:
+        copy.start()
+
+    for copy in copies_z:
+        copy.wait()
+    stacked = tok_z[...].reshape(Z_LOW * 16, 128)
+    picked = lax.broadcasted_iota(jnp.int32, (GROUP_A * 16, Z_LOW * 16), 0)
+    column = lax.broadcasted_iota(jnp.int32, (GROUP_A * 16, Z_LOW * 16), 1)
+    wanted = ((picked % 16) // 2) * 16 + (picked // 16) * 2 + picked % 2
+    choose = jnp.where(column == wanted, 1.0, 0.0).astype(jnp.bfloat16)
+    sorted_rows = jnp.dot(choose, stacked, preferred_element_type=jnp.float32)
+    tok_s[...] = sorted_rows.astype(jnp.bfloat16).reshape(GROUP_A, 16, 128)
+    copies_t = []
+    for k in range(1, GROUP_A):
+        other, target = peer_a(k)
+        copies_t.append(
+            remote(tok_s.at[other], buf_s.at[g], send_t.at[k - 1], recv_t.at[k - 1], target)
+        )
+    for copy in copies_t:
+        copy.start()
+    buf_s[g] = tok_s[g]
+
+    for copy in copies_b:
+        copy.wait()
+    summed = red_a[y]
+    for k in range(1, GROUP_Y):
+        summed = summed + buf_b[k - 1]
+    buf_c[zi] = summed
+
+    copies_c = []
+    for k in range(1, z_count):
+        _, target = peer_c(k)
+        copies_c.append(
+            remote(buf_c.at[zi], buf_c.at[zi], send_c.at[k - 1], recv_c.at[k - 1], target)
+        )
+    for copy in copies_c:
+        copy.start()
+    for copy in copies_c:
+        copy.wait()
+    summed = buf_c[0]
+    for k in range(1, z_count):
+        summed = summed + buf_c[k]
+    buf_d[y] = summed
+
+    copies_d = []
+    for k in range(1, GROUP_Y):
+        _, target = peer_b(k)
+        copies_d.append(
+            remote(buf_d.at[y], buf_d.at[y], send_d.at[k - 1], recv_d.at[k - 1], target)
+        )
+    for copy in copies_d:
+        copy.start()
+    for copy in copies_d:
+        copy.wait()
+
+    copies_e = []
+    for k in range(1, GROUP_A):
+        _, target = peer_a(k)
+        copies_e.append(
+            remote(buf_d, total_out.at[g], send_e.at[k - 1], recv_e.at[k - 1], target)
+        )
+    for copy in copies_e:
+        copy.start()
+    own = pltpu.make_async_copy(buf_d, total_out.at[g], local_sem)
+    own.start()
+    for copy in copies_t:
+        copy.wait()
+    rows_in[...] = buf_s[...]
+    own.wait()
+    for copy in copies_e:
+        copy.wait()
+
+
+def exchange(payload, rows_out):
+    dma = pltpu.SemaphoreType.DMA
+    z_count = Z_LOW * Z_HIGH
+    vmem = pl.BlockSpec(memory_space=pltpu.VMEM)
+    return pl.pallas_call(
+        exchange_kernel,
+        out_shape=(
+            jax.ShapeDtypeStruct((GROUP_A, GROUP_Y, 16, 128), jnp.float32),
+            jax.ShapeDtypeStruct((GROUP_A, 16, 128), jnp.bfloat16),
+        ),
+        in_specs=[vmem, vmem],
+        out_specs=(pl.BlockSpec(memory_space=pl.ANY), vmem),
+        scratch_shapes=[
+            pltpu.VMEM((GROUP_A - 1, GROUP_Y, 16, 128), jnp.float32),
+            pltpu.VMEM((GROUP_Y, 16, 128), jnp.float32),
+            pltpu.VMEM((GROUP_Y - 1, 16, 128), jnp.float32),
+            pltpu.VMEM((z_count, 16, 128), jnp.float32),
+            pltpu.VMEM((GROUP_Y, 16, 128), jnp.float32),
+            pltpu.VMEM((GROUP_A, 16, 128), jnp.bfloat16),
+            pltpu.VMEM((Z_LOW, 16, 128), jnp.bfloat16),
+            pltpu.VMEM((GROUP_A, 16, 128), jnp.bfloat16),
+            dma((GROUP_A - 1,)),
+            dma((GROUP_A - 1,)),
+            dma((GROUP_Y - 1,)),
+            dma((GROUP_Y - 1,)),
+            dma((z_count - 1,)),
+            dma((z_count - 1,)),
+            dma((GROUP_Y - 1,)),
+            dma((GROUP_Y - 1,)),
+            dma((GROUP_A - 1,)),
+            dma((GROUP_A - 1,)),
+            dma((Z_LOW - 1,)),
+            dma((Z_LOW - 1,)),
+            dma((GROUP_A - 1,)),
+            dma((GROUP_A - 1,)),
+            dma(()),
+        ],
+        compiler_params=pltpu.CompilerParams(collective_id=0, has_side_effects=True),
+        name="exchange",
+    )(payload, rows_out)
 
 
 def per_device(
@@ -97,10 +326,6 @@
     )
     grad_proj = jnp.einsum("fvd,fvc->dc", tile_tokens, chosen, preferred_element_type=jnp.float32)
     grad_proj = grad_proj + mask_token.astype(jnp.float32)[:, None] * mask_sum[None, :]
-    grad_proj, grad_first, grad_second, mask_sum = lax.psum(
-        (grad_proj, grad_first, grad_second, mask_sum), ("ew", "ns")
-    )
-    grad_mask = jnp.dot(proj_weight.astype(jnp.float32), mask_sum, precision=lax.Precision.HIGHEST)
     owner_count = lax.axis_size("ns")
     row_count = frames * slots
     capacity = 3 * row_count // (2 * owner_count)
@@ -113,19 +338,38 @@
     earlier = jnp.cumsum(owner_hits, axis=0, dtype=jnp.int32) - owner_hits
     place = jnp.sum(earlier * owner_hits, axis=1, dtype=jnp.int32)
     target = jnp.where(live_rows, owner_rows * capacity + place, owner_count * capacity)
-    token_rows = jnp.einsum(
-        "fvc,dc->fvd", chosen, proj_weight, preferred_element_type=jnp.float32
-    ).astype(jnp.bfloat16)
-    outgoing = jnp.zeros((owner_count * capacity, features), jnp.bfloat16)
-    outgoing = outgoing.at[target].set(token_rows.reshape(row_count, features), mode="drop")
-    arrived = lax.all_to_all(
-        outgoing.reshape(owner_count, capacity, features),
-        "ns",
-        split_axis=0,
-        concat_axis=0,
-        tiled=True,
+    slot_hot = (
+        target[:, None] == jnp.arange(owner_count * capacity, dtype=jnp.int32)[None, :]
+    ).astype(jnp.bfloat16)
+    narrow = jnp.einsum(
+        "rs,rc->sc", slot_hot, chosen.reshape(row_count, channels),
+        preferred_element_type=jnp.float32,
+    ).astype(jnp.bfloat16)
+    rows_out = narrow.reshape(Z_LOW, 16, 128)
+
+    left = grad_first.reshape(1024, channels)
+    right = jnp.concatenate(
+        [
+            grad_proj,
+            grad_second.reshape(192, channels),
+            mask_sum[None, :],
+            jnp.zeros((63, channels), jnp.float32),
+        ],
+        axis=0,
     )
-    token_grad = arrived.reshape(owner_count * capacity, features)
+    payload = jnp.concatenate([left, right], axis=1).reshape(GROUP_A, GROUP_Y, 16, 128)
+    total, rows_in = exchange(payload, rows_out)
+    total = total.reshape(1024, 128)
+    grad_first = total[:, :channels].reshape(4, 4, channels, channels)
+    grad_proj = total[:768, channels:]
+    grad_second = total[768:960, channels:].reshape(4, 4, 12, channels)
+    mask_sum = total[960, channels:]
+    grad_mask = jnp.dot(proj_weight.astype(jnp.float32), mask_sum, precision=lax.Precision.HIGHEST)
+    arrived = rows_in[:, : 2 * Z_LOW].reshape(GROUP_A, Z_LOW, 2, 128).transpose(1, 0, 2, 3)
+    arrived = arrived.reshape(owner_count * capacity, channels)
+    token_grad = jnp.einsum(
+        "rc,dc->rd", arrived, proj_weight, preferred_element_type=jnp.float32
+    ).astype(jnp.bfloat16)
     return (token_grad[None, None], grad_proj, grad_first, grad_second, grad_mask)
 
 

time: 745 us -> 288 us (0.39)
  waiting for transfers between devices: 373 us -> 4.66 us
  blocking collectives: 143 us -> 0 us
  Pallas kernels: 0 us -> 75.5 us
  between operations: 15.2 us -> 1.87 us
  starting transfers between devices: 39.1 us -> 26.3 us
  local copies, waits for them, and re-layouts: 142 us -> 150 us
    psum x1 -> x0, waiting for transfers between devices: 366 us -> none  [per_device(): lax.psum((grad_proj, grad_first, grad_second, mask_sum), ('ew', 'ns'))]
    psum x1 -> x0, blocking collectives: 143 us -> none  [per_device(): lax.psum((grad_proj, grad_first, grad_second, mask_sum), ('ew', 'ns'))]
    pallas_call x0 -> x1, Pallas kernels: none -> 75.5 us  [exchange(): pl.pallas_call(exchange_kernel, out_shape=(jax.ShapeDtypeStruct((GROUP_A,...]
    all_to_all x1 -> x0, starting transfers between devices: 12.7 us -> none  [per_device(): lax.all_to_all(outgoing.reshape(owner_count, capacity, features), 'ns', s...]
    slice x32, local copies, waits for them, and re-layouts: 128 us -> 138 us  [transpose_back(): padded[:, :, tap_y:tap_y + 2 * height:2, tap_x:tap_x + 2 * breadth:2]]
  transfers between devices with their start and end apart: 10 -> 8, of which waited for: 3 -> 2; matrix products, arithmetic and copies ran while one was open for 3% -> 8% of each run, Pallas kernels for 0% -> 0%
where the time goes in v1:
time: 288 us; the launch traced here: 287 us
  local copies, waits for them, and re-layouts  150 us (52%)
  Pallas kernels  75.5 us (26%)
  starting transfers between devices  26.3 us (9%)
  matrix products  22.7 us (8%)
  other arithmetic  6.35 us (2%)
  waiting for transfers between devices  4.66 us (2%)
    slice x32, local copies, waits for them, and re-layouts, transpose_back(): padded[:, :, tap_y:tap_y + 2 * height:2, tap_x:tap_x + 2 * breadth:2]  138 us
    pallas_call x1, Pallas kernels, exchange(): pl.pallas_call(exchange_kernel, out_shape=(jax.ShapeDtypeStruct((GROUP_A,...  75.5 us
    ppermute x4, starting transfers between devices, padded_2(): lax.ppermute(lax.slice_in_dim(block, block.shape[dim] - width, None, axis...  14.2 us
    dot_general x32, matrix products, transpose_back(): jnp.einsum('oi,fohw->fihw', kernel[tap_y, tap_x], window, preferred_eleme...  14.1 us
    ppermute x4, starting transfers between devices, padded_2(): lax.ppermute(lax.slice_in_dim(block, 0, width, axis=dim), axis, backward)  12.2 us
    unnamed x112, local copies, waits for them, and re-layouts  7.68 us
  transfers between devices with their start and end apart: 8, of which 2 were waited for; matrix products, arithmetic and copies ran while one was open for 8% of the time, Pallas kernels for 0%

profile of v1, /device:TPU:1, one launch (start us, length us, event | category | flops | bytes accessed | tf_op | source)
XLA Modules:
  0.0 287.3 jit_solution(14788321120235713682)
XLA Ops:
  1.9 4.0 %collective-permute-start = (bf16[2,12,16,1]{3,1,2,0:T(8,128)(2,1)S(1)}, bf16[2,12,16,1]{3,1,2,0:T(8,128)(2,1)S(1)}, u32[]{:S(2)}, u32[]{:S(2)}) collective-permute-start(bf16[2,12,16,1]{3,1,2,0:T(8,128)(2,1)S(1)} %get-tuple-element.20), channel_id=1, source_target_pairs={{0,48},{48,96},{96,144},{144,192},{192,240},{240,288},{288,336},{3... | collective-permute-start | bytes 2312 | tf_op jit(solution)/shard_map/ppermute | solution.py:22
  7.2 3.6 %slice.245 = bf16[2,12,8,128]{3,1,2,0:T(8,128)(2,1)S(1)} slice(bf16[2,12,16,256]{3,1,2,0:T(8,128)(2,1)S(1)} %copy.75), slice={[0:2:1], [0:12:1], [0:16:2], [0:256:2]} | slice | bytes 98304 | tf_op jit(solution)/shard_map/slice | solution.py:46
  17.8 3.6 %slice.243 = bf16[2,12,8,128]{3,1,2,0:T(8,128)(2,1)S(1)} slice(bf16[2,12,16,258]{3,1,2,0:T(8,128)(2,1)S(1)} %pad_maximum_fusion.4), slice={[0:2:1], [0:12:1], [0:16:2], [0:256:2]} | slice | bytes 98304 | tf_op jit(solution)/shard_map/slice | solution.py:46
  21.5 3.7 %slice.249 = bf16[2,12,8,128]{3,1,2,0:T(8,128)(2,1)S(1)} slice(bf16[2,12,16,258]{3,1,2,0:T(8,128)(2,1)S(1)} %pad_maximum_fusion.4), slice={[0:2:1], [0:12:1], [0:16:2], [3:258:2]} | slice | bytes 98304 | tf_op jit(solution)/shard_map/slice | solution.py:46
  25.2 4.0 %collective-permute-start.2 = (bf16[2,12,1,258]{3,1,2,0:T(8,128)(2,1)S(1)}, bf16[2,12,1,258]{3,1,2,0:T(8,128)(2,1)S(1)}, u32[]{:S(2)}, u32[]{:S(2)}) collective-permute-start(bf16[2,12,1,258]{3,1,2,0:T(8,128)(2,1)S(1)} %get-tuple-element.16), channel_id=1, source_target_pairs={{0,1},{1,2},{2,3},{3,4},{4,5},{5,6},{6,7},{7,8},{8,9},{9,10},{10,1... | collective-permute-start | bytes 37160 | tf_op jit(solution)/shard_map/ppermute | solution.py:22
  29.1 7.0 %collective-permute-start.3 = (bf16[2,12,1,258]{3,1,2,0:T(8,128)(2,1)S(1)}, bf16[2,12,1,258]{3,1,2,0:T(8,128)(2,1)}, u32[]{:S(2)}, u32[]{:S(2)}) collective-permute-start(bf16[2,12,1,258]{3,1,2,0:T(8,128)(2,1)S(1)} %get-tuple-element.17), channel_id=1, source_target_pairs={{1,0},{2,1},{3,2},{4,3},{5,4},{6,5},{7,6},{8,7},{9,8},{10,9},{11,1... | collective-permute-start | bytes 37160 | tf_op jit(solution)/shard_map/ppermute | solution.py:25
  36.7 3.7 %slice.247 = bf16[2,12,8,128]{3,1,2,0:T(8,128)(2,1)S(1)} slice(bf16[2,12,16,258]{3,1,2,0:T(8,128)(2,1)S(1)} %pad_maximum_fusion.4), slice={[0:2:1], [0:12:1], [0:16:2], [2:258:2]} | slice | bytes 98304 | tf_op jit(solution)/shard_map/slice | solution.py:46
  41.6 6.8 %slice.241 = bf16[2,12,8,128]{3,1,2,0:T(8,128)(2,1)} slice(bf16[2,12,18,258]{3,1,2,0:T(8,128)(2,1)S(1)} %pad_maximum_fusion.3), slice={[0:2:1], [0:12:1], [0:16:2], [3:258:2]} | slice | bytes 98304 | tf_op jit(solution)/shard_map/slice | solution.py:46
  48.3 6.7 %slice.239 = bf16[2,12,8,128]{3,1,2,0:T(8,128)(2,1)} slice(bf16[2,12,18,258]{3,1,2,0:T(8,128)(2,1)S(1)} %pad_maximum_fusion.3), slice={[0:2:1], [0:12:1], [0:16:2], [2:258:2]} | slice | bytes 98304 | tf_op jit(solution)/shard_map/slice | solution.py:46
  55.0 6.7 %slice.237 = bf16[2,12,8,128]{3,1,2,0:T(8,128)(2,1)} slice(bf16[2,12,18,258]{3,1,2,0:T(8,128)(2,1)S(1)} %pad_maximum_fusion.3), slice={[0:2:1], [0:12:1], [0:16:2], [1:257:2]} | slice | bytes 98304 | tf_op jit(solution)/shard_map/slice | solution.py:46
  61.8 6.7 %slice.235 = bf16[2,12,8,128]{3,1,2,0:T(8,128)(2,1)} slice(bf16[2,12,18,258]{3,1,2,0:T(8,128)(2,1)S(1)} %pad_maximum_fusion.3), slice={[0:2:1], [0:12:1], [0:16:2], [0:256:2]} | slice | bytes 98304 | tf_op jit(solution)/shard_map/slice | solution.py:46
  68.5 4.0 %slice.265 = bf16[2,12,8,128]{3,1,2,0:T(8,128)(2,1)S(1)} slice(bf16[2,12,18,258]{3,1,2,0:T(8,128)(2,1)S(1)} %pad_maximum_fusion.3), slice={[0:2:1], [0:12:1], [3:18:2], [3:258:2]} | slice | bytes 98304 | tf_op jit(solution)/shard_map/slice | solution.py:46
  72.5 4.1 %slice.263 = bf16[2,12,8,128]{3,1,2,0:T(8,128)(2,1)S(1)} slice(bf16[2,12,18,258]{3,1,2,0:T(8,128)(2,1)S(1)} %pad_maximum_fusion.3), slice={[0:2:1], [0:12:1], [3:18:2], [2:258:2]} | slice | bytes 98304 | tf_op jit(solution)/shard_map/slice | solution.py:46
  76.5 6.8 %slice.261 = bf16[2,12,8,128]{3,1,2,0:T(8,128)(2,1)} slice(bf16[2,12,18,258]{3,1,2,0:T(8,128)(2,1)S(1)} %pad_maximum_fusion.3), slice={[0:2:1], [0:12:1], [3:18:2], [1:257:2]} | slice | bytes 98304 | tf_op jit(solution)/shard_map/slice | solution.py:46
  83.3 6.7 %slice.259 = bf16[2,12,8,128]{3,1,2,0:T(8,128)(2,1)} slice(bf16[2,12,18,258]{3,1,2,0:T(8,128)(2,1)S(1)} %pad_maximum_fusion.3), slice={[0:2:1], [0:12:1], [3:18:2], [0:256:2]} | slice | bytes 98304 | tf_op jit(solution)/shard_map/slice | solution.py:46
  90.1 6.7 %slice.257 = bf16[2,12,8,128]{3,1,2,0:T(8,128)(2,1)} slice(bf16[2,12,18,258]{3,1,2,0:T(8,128)(2,1)S(1)} %pad_maximum_fusion.3), slice={[0:2:1], [0:12:1], [2:18:2], [3:258:2]} | slice | bytes 98304 | tf_op jit(solution)/shard_map/slice | solution.py:46
  96.8 6.7 %slice.255 = bf16[2,12,8,128]{3,1,2,0:T(8,128)(2,1)} slice(bf16[2,12,18,258]{3,1,2,0:T(8,128)(2,1)S(1)} %pad_maximum_fusion.3), slice={[0:2:1], [0:12:1], [2:18:2], [2:258:2]} | slice | bytes 98304 | tf_op jit(solution)/shard_map/slice | solution.py:46
  103.5 6.7 %slice.253 = bf16[2,12,8,128]{3,1,2,0:T(8,128)(2,1)} slice(bf16[2,12,18,258]{3,1,2,0:T(8,128)(2,1)S(1)} %pad_maximum_fusion.3), slice={[0:2:1], [0:12:1], [2:18:2], [1:257:2]} | slice | bytes 98304 | tf_op jit(solution)/shard_map/slice | solution.py:46
  110.2 6.7 %slice.251 = bf16[2,12,8,128]{3,1,2,0:T(8,128)(2,1)} slice(bf16[2,12,18,258]{3,1,2,0:T(8,128)(2,1)S(1)} %pad_maximum_fusion.3), slice={[0:2:1], [0:12:1], [2:18:2], [0:256:2]} | slice | bytes 98304 | tf_op jit(solution)/shard_map/slice | solution.py:46
  126.6 4.3 %collective-permute-start.4 = (bf16[2,64,8,1]{3,1,2,0:T(8,128)(2,1)S(1)}, bf16[2,64,8,1]{3,1,2,0:T(8,128)(2,1)S(1)}, u32[]{:S(2)}, u32[]{:S(2)}) collective-permute-start(bf16[2,64,8,1]{3,1,2,0:T(8,128)(2,1)S(1)} %get-tuple-element.18), channel_id=1, source_target_pairs={{0,48},{48,96},{96,144},{144,192},{192,240},{240,288},{288,336},{3... | collective-permute-start | bytes 6152 | tf_op jit(solution)/shard_map/ppermute | solution.py:22
  136.9 4.1 %collective-permute-done.5 = bf16[2,64,8,1]{3,1,2,0:T(8,128)(2,1)S(1)} collective-permute-done((bf16[2,64,8,1]{3,1,2,0:T(8,128)(2,1)S(1)}, bf16[2,64,8,1]{3,1,2,0:T(8,128)(2,1)S(1)}, u32[]{:S(2)}, u32[]{:S(2)}) %collective-permute-start.5) | collective-permute-done | bytes 2080 | tf_op jit(solution)/shard_map/ppermute | solution.py:25
  161.2 3.0 %slice.272 = bf16[2,64,4,64]{3,1,2,0:T(8,128)(2,1)S(1)} slice(bf16[2,64,10,130]{3,1,2,0:T(8,128)(2,1)S(1)} %pad_maximum_fusion), slice={[0:2:1], [0:64:1], [0:8:2], [1:129:2]} | slice | bytes 131072 | tf_op jit(solution)/shard_map/slice | solution.py:46
  164.2 3.0 %slice.273 = bf16[2,64,4,64]{3,1,2,0:T(8,128)(2,1)S(1)} slice(bf16[2,64,10,130]{3,1,2,0:T(8,128)(2,1)S(1)} %pad_maximum_fusion), slice={[0:2:1], [0:64:1], [0:8:2], [2:130:2]} | slice | bytes 131072 | tf_op jit(solution)/shard_map/slice | solution.py:46
  167.2 3.0 %slice.274 = bf16[2,64,4,64]{3,1,2,0:T(8,128)(2,1)S(1)} slice(bf16[2,64,10,130]{3,1,2,0:T(8,128)(2,1)S(1)} %pad_maximum_fusion), slice={[0:2:1], [0:64:1], [0:8:2], [3:130:2]} | slice | bytes 131072 | tf_op jit(solution)/shard_map/slice | solution.py:46
  173.0 3.0 %slice.280 = bf16[2,64,4,64]{3,1,2,0:T(8,128)(2,1)S(1)} slice(bf16[2,64,10,130]{3,1,2,0:T(8,128)(2,1)S(1)} %pad_maximum_fusion), slice={[0:2:1], [0:64:1], [2:10:2], [1:129:2]} | slice | bytes 131072 | tf_op jit(solution)/shard_map/slice | solution.py:46
  176.0 3.0 %slice.281 = bf16[2,64,4,64]{3,1,2,0:T(8,128)(2,1)S(1)} slice(bf16[2,64,10,130]{3,1,2,0:T(8,128)(2,1)S(1)} %pad_maximum_fusion), slice={[0:2:1], [0:64:1], [2:10:2], [2:130:2]} | slice | bytes 131072 | tf_op jit(solution)/shard_map/slice | solution.py:46
  179.0 3.0 %slice.282 = bf16[2,64,4,64]{3,1,2,0:T(8,128)(2,1)S(1)} slice(bf16[2,64,10,130]{3,1,2,0:T(8,128)(2,1)S(1)} %pad_maximum_fusion), slice={[0:2:1], [0:64:1], [2:10:2], [3:130:2]} | slice | bytes 131072 | tf_op jit(solution)/shard_map/slice | solution.py:46
  181.9 3.1 %slice.283 = bf16[2,64,4,64]{3,1,2,0:T(8,128)(2,1)S(1)} slice(bf16[2,64,10,130]{3,1,2,0:T(8,128)(2,1)S(1)} %pad_maximum_fusion), slice={[0:2:1], [0:64:1], [3:10:2], [0:128:2]} | slice | bytes 131072 | tf_op jit(solution)/shard_map/slice | solution.py:46
  185.0 3.1 %slice.284 = bf16[2,64,4,64]{3,1,2,0:T(8,128)(2,1)S(1)} slice(bf16[2,64,10,130]{3,1,2,0:T(8,128)(2,1)S(1)} %pad_maximum_fusion), slice={[0:2:1], [0:64:1], [3:10:2], [1:129:2]} | slice | bytes 131072 | tf_op jit(solution)/shard_map/slice | solution.py:46
  188.1 3.1 %slice.285 = bf16[2,64,4,64]{3,1,2,0:T(8,128)(2,1)S(1)} slice(bf16[2,64,10,130]{3,1,2,0:T(8,128)(2,1)S(1)} %pad_maximum_fusion), slice={[0:2:1], [0:64:1], [3:10:2], [2:130:2]} | slice | bytes 131072 | tf_op jit(solution)/shard_map/slice | solution.py:46
  191.3 3.1 %slice.286 = bf16[2,64,4,64]{3,1,2,0:T(8,128)(2,1)S(1)} slice(bf16[2,64,10,130]{3,1,2,0:T(8,128)(2,1)S(1)} %pad_maximum_fusion), slice={[0:2:1], [0:64:1], [3:10:2], [3:130:2]} | slice | bytes 131072 | tf_op jit(solution)/shard_map/slice | solution.py:46
  206.3 75.5 %exchange.1 = (f32[8,8,16,128]{3,2,1,0:T(8,128)}, bf16[8,16,128]{2,1,0:T(8,128)(2,1)}) custom-call(f32[8,8,16,128]{3,2,1,0:T(8,128)} %pad_maximum_fusion.2.payload, bf16[6,16,128]{2,1,0:T(8,128)(2,1)} %reshape.115.rows_out), custom_call_target="tpu_custom_call" | custom-call | tf_op jit(solution)/shard_map/exchange/pallas_call | solution.py:239
  (239 shorter events, 66.5 us)
Async XLA Ops:
  0.6 14.1 %copy-start = (bf16[1,1,2,64,768]{4,3,2,1,0:T(8,128)(2,1)S(1)}, bf16[1,1,2,64,768]{4,3,2,1,0:T(8,128)(2,1)}, u32[]{:S(2)}) copy-start(bf16[1,1,2,64,768]{4,3,2,1,0:T(8,128)(2,1)} %param.10) | copy-start | bytes 589828
  0.6 10.2 %copy-start.27 = (bf16[4,4,12,64]{3,1,2,0:T(4,128)(2,1)S(1)}, bf16[4,4,12,64]{3,1,2,0:T(4,128)(2,1)}, u32[]{:S(2)}) copy-start(bf16[4,4,12,64]{3,1,2,0:T(4,128)(2,1)} %param.17) | copy-start | bytes 73732
  0.7 10.9 %copy-start.52 = (s32[1,1,2]{2,1,0:T(1,128)S(1)}, s32[1,1,2]{2,1,0:T(1,128)}, u32[]{:S(2)}) copy-start(s32[1,1,2]{2,1,0:T(1,128)} %param.12) | copy-start | bytes 28
  0.7 11.1 %copy-start.46 = (s32[1,1,2,64]{3,2,1,0:T(2,128)S(1)}, s32[1,1,2,64]{3,2,1,0:T(2,128)}, u32[]{:S(2)}) copy-start(s32[1,1,2,64]{3,2,1,0:T(2,128)} %param.11) | copy-start | bytes 1540
  0.7 11.8 %copy-start.45 = (bf16[768]{0:T(1024)(128)(2,1)S(1)}, bf16[768]{0:T(1024)(128)(2,1)}, u32[]{:S(2)}) copy-start(bf16[768]{0:T(1024)(128)(2,1)} %param.14) | copy-start | bytes 4612
  0.7 11.8 %copy-start.2 = (bf16[2,64,8,128]{3,2,1,0:T(8,128)(2,1)S(1)}, bf16[2,64,8,128]{3,2,1,0:T(8,128)(2,1)}, u32[]{:S(2)}) copy-start(bf16[2,64,8,128]{3,2,1,0:T(8,128)(2,1)} %param.18) | copy-start | bytes 786436
  1.8 11.4 %copy-start.48 = (s32[1,1,2,64,1]{3,4,2,1,0:T(1,128)S(1)}, s32[1,1,2,64,1]{3,4,2,1,0:T(1,128)}, u32[]{:S(2)}) copy-start(s32[1,1,2,64,1]{3,4,2,1,0:T(1,128)} %param.13) | copy-start | bytes 1540
  1.9 15.3 %collective-permute-start = (bf16[2,12,16,1]{3,1,2,0:T(8,128)(2,1)S(1)}, bf16[2,12,16,1]{3,1,2,0:T(8,128)(2,1)S(1)}, u32[]{:S(2)}, u32[]{:S(2)}) collective-permute-start(bf16[2,12,16,1]{3,1,2,0:T(8,128)(2,1)S(1)} %get-tuple-element.20), channel_id=1, source_target_pairs={{0,48},{48,96},{96,144},{144,192},{192,240},{240,288},{288,336},{3... | collective-permute-start | bytes 2312 | tf_op jit(solution)/shard_map/ppermute | solution.py:22
  5.9 11.2 %collective-permute-start.1 = (bf16[2,12,16,1]{3,1,2,0:T(8,128)(2,1)S(1)}, bf16[2,12,16,1]{3,1,2,0:T(8,128)(2,1)S(1)}, u32[]{:S(2)}, u32[]{:S(2)}) collective-permute-start(bf16[2,12,16,1]{3,1,2,0:T(8,128)(2,1)S(1)} %get-tuple-element.21), channel_id=1, source_target_pairs={{48,0},{96,48},{144,96},{192,144},{240,192},{288,240},{336,288},{3... | collective-permute-start | bytes 2312 | tf_op jit(solution)/shard_map/ppermute | solution.py:25
  11.7 3.1 %copy-start.49 = (pred[2,64]{1,0:T(4,128)(4,1)}, pred[2,64]{1,0:T(4,128)(4,1)S(1)}, u32[]{:S(2)}) copy-start(pred[2,64]{1,0:T(4,128)(4,1)S(1)} %iota_compare_fusion.4) | copy-start | bytes 388
  12.5 2.2 copy-start.24
  17.8 18.6 %copy-start.41 = (bf16[1,1,12,64]{3,1,2,0:T(2,128)(2,1)S(1)}, bf16[1,1,12,64]{3,1,2,0:T(2,128)(2,1)}, u32[]{:S(2)}) copy-start(bf16[1,1,12,64]{3,1,2,0:T(2,128)(2,1)} %get-tuple-element.30) | copy-start | bytes 4612
  25.2 15.2 %collective-permute-start.2 = (bf16[2,12,1,258]{3,1,2,0:T(8,128)(2,1)S(1)}, bf16[2,12,1,258]{3,1,2,0:T(8,128)(2,1)S(1)}, u32[]{:S(2)}, u32[]{:S(2)}) collective-permute-start(bf16[2,12,1,258]{3,1,2,0:T(8,128)(2,1)S(1)} %get-tuple-element.16), channel_id=1, source_target_pairs={{0,1},{1,2},{2,3},{3,4},{4,5},{5,6},{6,7},{7,8},{8,9},{9,10},{10,1... | collective-permute-start | bytes 37160 | tf_op jit(solution)/shard_map/ppermute | solution.py:22
  29.1 11.2 %collective-permute-start.3 = (bf16[2,12,1,258]{3,1,2,0:T(8,128)(2,1)S(1)}, bf16[2,12,1,258]{3,1,2,0:T(8,128)(2,1)}, u32[]{:S(2)}, u32[]{:S(2)}) collective-permute-start(bf16[2,12,1,258]{3,1,2,0:T(8,128)(2,1)S(1)} %get-tuple-element.17), channel_id=1, source_target_pairs={{1,0},{2,1},{3,2},{4,3},{5,4},{6,5},{7,6},{8,7},{9,8},{10,9},{11,1... | collective-permute-start | bytes 37160 | tf_op jit(solution)/shard_map/ppermute | solution.py:25
  55.0 61.9 %copy-start.40 = (bf16[1,1,12,64]{3,1,2,0:T(2,128)(2,1)S(1)}, bf16[1,1,12,64]{3,1,2,0:T(2,128)(2,1)}, u32[]{:S(2)}) copy-start(bf16[1,1,12,64]{3,1,2,0:T(2,128)(2,1)} %get-tuple-element.33) | copy-start | bytes 4612
  83.3 34.8 %copy-start.39 = (bf16[1,1,12,64]{3,1,2,0:T(2,128)(2,1)S(1)}, bf16[1,1,12,64]{3,1,2,0:T(2,128)(2,1)}, u32[]{:S(2)}) copy-start(bf16[1,1,12,64]{3,1,2,0:T(2,128)(2,1)} %get-tuple-element.34) | copy-start | bytes 4612
  110.2 9.0 %copy-start.38 = (bf16[1,1,12,64]{3,1,2,0:T(2,128)(2,1)S(1)}, bf16[1,1,12,64]{3,1,2,0:T(2,128)(2,1)}, u32[]{:S(2)}) copy-start(bf16[1,1,12,64]{3,1,2,0:T(2,128)(2,1)} %get-tuple-element.35) | copy-start | bytes 4612
  116.9 2.3 copy-start.19
  118.1 1.5 copy-start.37
  123.5 8.7 %copy-start.22 = (bf16[2,12,8,128]{3,1,2,0:T(8,128)(2,1)S(1)}, bf16[2,12,8,128]{3,1,2,0:T(8,128)(2,1)}, u32[]{:S(2)}) copy-start(bf16[2,12,8,128]{3,1,2,0:T(8,128)(2,1)} %slice.235) | copy-start | bytes 147460
  123.5 8.9 %copy-start.20 = (bf16[2,12,8,128]{3,1,2,0:T(8,128)(2,1)S(1)}, bf16[2,12,8,128]{3,1,2,0:T(8,128)(2,1)}, u32[]{:S(2)}) copy-start(bf16[2,12,8,128]{3,1,2,0:T(8,128)(2,1)} %slice.237) | copy-start | bytes 147460
  123.7 8.9 %copy-start.18 = (bf16[2,12,8,128]{3,1,2,0:T(8,128)(2,1)S(1)}, bf16[2,12,8,128]{3,1,2,0:T(8,128)(2,1)}, u32[]{:S(2)}) copy-start(bf16[2,12,8,128]{3,1,2,0:T(8,128)(2,1)} %slice.239) | copy-start | bytes 147460
  123.7 9.1 %copy-start.17 = (bf16[2,12,8,128]{3,1,2,0:T(8,128)(2,1)S(1)}, bf16[2,12,8,128]{3,1,2,0:T(8,128)(2,1)}, u32[]{:S(2)}) copy-start(bf16[2,12,8,128]{3,1,2,0:T(8,128)(2,1)} %slice.241) | copy-start | bytes 147460
  126.6 10.3 %collective-permute-start.4 = (bf16[2,64,8,1]{3,1,2,0:T(8,128)(2,1)S(1)}, bf16[2,64,8,1]{3,1,2,0:T(8,128)(2,1)S(1)}, u32[]{:S(2)}, u32[]{:S(2)}) collective-permute-start(bf16[2,64,8,1]{3,1,2,0:T(8,128)(2,1)S(1)} %get-tuple-element.18), channel_id=1, source_target_pairs={{0,48},{48,96},{96,144},{144,192},{192,240},{240,288},{288,336},{3... | collective-permute-start | bytes 6152 | tf_op jit(solution)/shard_map/ppermute | solution.py:22
  130.9 10.1 %collective-permute-start.5 = (bf16[2,64,8,1]{3,1,2,0:T(8,128)(2,1)S(1)}, bf16[2,64,8,1]{3,1,2,0:T(8,128)(2,1)S(1)}, u32[]{:S(2)}, u32[]{:S(2)}) collective-permute-start(bf16[2,64,8,1]{3,1,2,0:T(8,128)(2,1)S(1)} %get-tuple-element.19), channel_id=1, source_target_pairs={{48,0},{96,48},{144,96},{192,144},{240,192},{288,240},{336,288},{3... | collective-permute-start | bytes 6152 | tf_op jit(solution)/shard_map/ppermute | solution.py:25
  147.2 10.7 %collective-permute-start.6 = (bf16[2,64,1,130]{3,1,2,0:T(8,128)(2,1)S(1)}, bf16[2,64,1,130]{3,1,2,0:T(8,128)(2,1)S(1)}, u32[]{:S(2)}, u32[]{:S(2)}) collective-permute-start(bf16[2,64,1,130]{3,1,2,0:T(8,128)(2,1)S(1)} %get-tuple-element.14), channel_id=1, source_target_pairs={{0,1},{1,2},{2,3},{3,4},{4,5},{5,6},{6,7},{7,8},{8,9},{9,10},{10,1... | collective-permute-start | bytes 99848 | tf_op jit(solution)/shard_map/ppermute | solution.py:22
  149.2 8.8 %collective-permute-start.7 = (bf16[2,64,1,130]{3,1,2,0:T(8,128)(2,1)S(1)}, bf16[2,64,1,130]{3,1,2,0:T(8,128)(2,1)S(1)}, u32[]{:S(2)}, u32[]{:S(2)}) collective-permute-start(bf16[2,64,1,130]{3,1,2,0:T(8,128)(2,1)S(1)} %get-tuple-element.15), channel_id=1, source_target_pairs={{1,0},{2,1},{3,2},{4,3},{5,4},{6,5},{7,6},{8,7},{9,8},{10,9},{11,1... | collective-permute-start | bytes 99848 | tf_op jit(solution)/shard_map/ppermute | solution.py:25
  194.4 1.4 copy-start.26
  199.6 1.6 copy-start.3
  203.7 1.6 copy-start.6
  206.3 76.8 %copy-start.25 = (bf16[768,64]{0,1:T(8,128)(2,1)S(1)}, bf16[768,64]{0,1:T(8,128)(2,1)}, u32[]{:S(2)}) copy-start(bf16[768,64]{0,1:T(8,128)(2,1)} %param.15) | copy-start | bytes 294916
  281.8 3.0 %copy-start.28 = (bf16[8,16,128]{2,1,0:T(8,128)(2,1)S(1)}, bf16[8,16,128]{2,1,0:T(8,128)(2,1)}, u32[]{:S(2)}) copy-start(bf16[8,16,128]{2,1,0:T(8,128)(2,1)} %get-tuple-element.7) | copy-start | bytes 98308
  (29 other events, 24.9 us)

commit v2 on v1

--- a/solution.py
+++ b/solution.py
@@ -1,7 +1,6 @@
-import functools
-
 import jax
 import jax.numpy as jnp
+import numpy as np
 from jax import lax
 from jax.experimental import pallas as pl
 from jax.experimental.pallas import tpu as pltpu
@@ -14,45 +13,473 @@
 Z_HIGH = 2
 
 
-def padded_2(block, sides, width):
-    for axis, dim in sides:
-        count = lax.axis_size(axis)
-        forward = [(i, i + 1) for i in range(count - 1)]
-        backward = [(target, source) for source, target in forward]
-        low = lax.ppermute(
-            lax.slice_in_dim(block, block.shape[dim] - width, None, axis=dim), axis, forward
-        )
-        high = lax.ppermute(lax.slice_in_dim(block, 0, width, axis=dim), axis, backward)
-        block = jnp.concatenate([low, block, high], axis=dim)
-    return block
-
-
-def gelu_value(preact):
-    return preact * jax.nn.sigmoid(1.702 * preact)
-
-
-def gelu_slope(preact):
-    sigmoid_value = jax.nn.sigmoid(1.702 * preact)
-    return sigmoid_value + 1.702 * preact * sigmoid_value * (1.0 - sigmoid_value)
-
-
-def transpose_back(inputs, padded, kernel):
-    height = inputs.shape[2]
-    breadth = inputs.shape[3]
-    grad_inputs = None
-    grad_taps = []
-    for tap_y in range(4):
-        for tap_x in range(4):
-            window = padded[:, :, tap_y : tap_y + 2 * height : 2, tap_x : tap_x + 2 * breadth : 2]
-            partial_term = jnp.einsum(
-                "oi,fohw->fihw", kernel[tap_y, tap_x], window, preferred_element_type=jnp.float32
+BANDS_PAD = 16
+LANES = 128
+
+
+def tap_select():
+    wide = np.zeros((256, 4, 256), np.float32)
+    halo = np.zeros((16, 4, 256), np.float32)
+    for tap in range(4):
+        for lane, cell in [(j, j) for j in range(128)] + [(128, 128), (255, -1)]:
+            col = 2 * cell + tap - 1
+            if col < 0:
+                halo[8 + col + 3, tap, lane] = 1
+            elif col < 256:
+                wide[col, tap, lane] = 1
+            else:
+                halo[col - 256, tap, lane] = 1
+    fine = np.zeros((256, 4, 2, 64), np.float32)
+    for tap in range(4):
+        for cell in range(64):
+            col = 2 * cell + tap - 1
+            fine[col if col >= 0 else 255, tap, :, cell] = 1
+    edge = np.zeros((2, 8, 128, 128), np.float32)
+    for frame in range(2):
+        for row in range(8):
+            spots = [row + 1] + ([0] if row == 7 else []) + ([9] if row == 0 else [])
+            for spot in spots:
+                pair = 2 * (frame * 10 + spot)
+                edge[frame, row, 0, pair] = 1
+                edge[frame, row, 127, (pair - 1) % 128] = 1
+    cols = np.zeros((16, 256), np.float32)
+    for k in range(3):
+        cols[k, k] = 1
+        cols[8 + k, 253 + k] = 1
+    half = jnp.bfloat16
+    return (
+        jnp.asarray(wide.reshape(256, 1024), half),
+        jnp.asarray(halo.reshape(16, 1024), half),
+        jnp.asarray(fine.reshape(256, 512), half),
+        jnp.asarray(edge.reshape(2048, 128), half),
+        jnp.asarray(cols, half),
+    )
+
+
+def dot_nn(a, b):
+    return jnp.dot(a, b, preferred_element_type=jnp.float32)
+
+
+def dot_nt(a, b):
+    return lax.dot_general(a, b, (((1,), (1,)), ((), ())), preferred_element_type=jnp.float32)
+
+
+def dot_tn(a, b):
+    return lax.dot_general(a, b, (((0,), (0,)), ((), ())), preferred_element_type=jnp.float32)
+
+
+def prepare_kernel(cot, pre, cols, edge, cot_rows, cot_cols, pre_rows, pre_cols, wide_c, wide_p):
+    half = jnp.bfloat16
+    for f in range(2):
+        for o in range(12):
+            for part in range(2):
+                wide_c[part, pl.ds((f * 16 + o) * 16, 16), :] = cot[
+                    f, o, :, part * 128 : part * 128 + 128
+                ].astype(jnp.float32)
+        for part in range(2):
+            wide_c[part, pl.ds((f * 16 + 12) * 16, 64), :] = jnp.zeros((64, 128), jnp.float32)
+        for r in range(16):
+            for part in range(2):
+                cot_rows[f, r, :, part * 128 : part * 128 + 128] = wide_c[
+                    part, pl.ds(f * 256 + r, 16, stride=16), :
+                ].astype(half)
+        for part in range(2):
+            block = cot_rows[f, part * 8 : part * 8 + 8].reshape(128, 256)
+            cot_cols[f, part] = dot_nt(cols[...], block).astype(half)
+    for f in range(2):
+        wide_p[pl.ds(f * 512, 512), :] = pre[f].reshape(512, 128).astype(jnp.float32)
+    packed = jnp.zeros((64, 128), jnp.float32)
+    for f in range(2):
+        for i in range(8):
+            slab = wide_p[pl.ds(f * 512 + i, 64, stride=8), :].astype(half)
+            pre_rows[f, i] = slab
+            packed = packed + dot_nn(slab, edge[pl.ds((f * 8 + i) * 128, 128), :])
+    pre_cols[...] = packed.astype(half)
+
+
+def prepare(cot, pre, cols, edge):
+    vmem = pl.BlockSpec(memory_space=pltpu.VMEM)
+    half = jnp.bfloat16
+    return pl.pallas_call(
+        prepare_kernel,
+        out_shape=(
+            jax.ShapeDtypeStruct((2, 16, 16, 256), half),
+            jax.ShapeDtypeStruct((2, 2, 16, 128), half),
+            jax.ShapeDtypeStruct((2, 8, 64, 128), half),
+            jax.ShapeDtypeStruct((64, 128), half),
+        ),
+        in_specs=[vmem] * 4,
+        out_specs=(vmem,) * 4,
+        scratch_shapes=[pltpu.VMEM((2, 512, 128), jnp.float32), pltpu.VMEM((1024, 128), jnp.float32)],
+        name="prepare",
+    )(cot, pre, cols, edge)
+
+
+SIDES = ((-1, 0), (1, 0), (0, -1), (0, 1), (-1, -1), (-1, 1), (1, -1), (1, 1))
+
+
+def halo_kernel(cot_rows, cot_cols, pre_rows, pre_cols, rows_c, rows_p, cols_c, cols_p, send, recv):
+    n = lax.axis_index("ns")
+    e = lax.axis_index("ew")
+    n_count = lax.axis_size("ns")
+    e_count = lax.axis_size("ew")
+
+    def peer(side):
+        return {
+            "ew": lax.rem(e + side[1] + e_count, e_count),
+            "ns": lax.rem(n + side[0] + n_count, n_count),
+        }
+
+    barrier = pltpu.get_barrier_semaphore()
+    for side in SIDES:
+        pl.semaphore_signal(barrier, inc=1, device_id=peer(side), device_id_type=MESH)
+    pl.semaphore_wait(barrier, len(SIDES))
+    copies = []
+
+    def put(src, dst, side):
+        slot = len(copies)
+        copy = pltpu.make_async_remote_copy(
+            src_ref=src,
+            dst_ref=dst,
+            send_sem=send.at[slot],
+            recv_sem=recv.at[slot],
+            device_id=peer(side),
+            device_id_type=MESH,
+        )
+        copy.start()
+        copies.append(copy)
+
+    put(cot_cols, cols_c.at[1], (0, -1))
+    put(cot_cols, cols_c.at[0], (0, 1))
+    put(pre_cols, cols_p.at[1], (0, -1))
+    put(pre_cols, cols_p.at[0], (0, 1))
+    put(cot_cols, cols_c.at[5], (-1, -1))
+    put(cot_cols, cols_c.at[4], (-1, 1))
+    put(cot_cols, cols_c.at[3], (1, -1))
+    put(cot_cols, cols_c.at[2], (1, 1))
+    put(pre_cols, cols_p.at[5], (-1, -1))
+    put(pre_cols, cols_p.at[4], (-1, 1))
+    put(pre_cols, cols_p.at[3], (1, -1))
+    put(pre_cols, cols_p.at[2], (1, 1))
+    put(cot_rows.at[:, 0:3], rows_c.at[1], (-1, 0))
+    put(cot_rows.at[:, 13:16], rows_c.at[0], (1, 0))
+    put(pre_rows.at[:, 0], rows_p.at[1], (-1, 0))
+    put(pre_rows.at[:, 7], rows_p.at[0], (1, 0))
+    for copy in copies:
+        copy.wait()
+
+
+def halo(cot_rows, cot_cols, pre_rows, pre_cols):
+    vmem = pl.BlockSpec(memory_space=pltpu.VMEM)
+    half = jnp.bfloat16
+    return pl.pallas_call(
+        halo_kernel,
+        out_shape=(
+            jax.ShapeDtypeStruct((2, 2, 3, 16, 256), half),
+            jax.ShapeDtypeStruct((2, 2, 64, 128), half),
+            jax.ShapeDtypeStruct((6, 2, 2, 16, 128), half),
+            jax.ShapeDtypeStruct((6, 64, 128), half),
+        ),
+        in_specs=[vmem] * 4,
+        out_specs=(vmem,) * 4,
+        scratch_shapes=[pltpu.SemaphoreType.DMA((16,)), pltpu.SemaphoreType.DMA((16,))],
+        compiler_params=pltpu.CompilerParams(collective_id=1, has_side_effects=True),
+        name="halo",
+    )(cot_rows, cot_cols, pre_rows, pre_cols)
+
+
+def gradient_kernel(
+    place,
+    live_counts,
+    index,
+    owners,
+    tokens,
+    mask_token,
+    proj,
+    first,
+    second,
+    wide,
+    narrow,
+    fine,
+    cot_rows,
+    pre_rows,
+    rows_c,
+    rows_p,
+    cols_c,
+    cols_p,
+    payload,
+    rows_out,
+    taps,
+    windows,
+    hidden,
+    deltas,
+    taps_fine,
+    windows_fine,
+):
+    half = jnp.bfloat16
+    n = place[0]
+    e = place[1]
+    north = n > 0
+    south = n < place[2] - 1
+    west = e > 0
+    east = e < place[3] - 1
+
+    def flag(condition, shape):
+        return jnp.full(shape, jnp.where(condition, 1.0, 0.0), jnp.float32)
+
+    def keep(condition, value):
+        return (value.astype(jnp.float32) * flag(condition, value.shape)).astype(half)
+
+    row_16 = lax.broadcasted_iota(jnp.int32, (16, 128), 0)
+
+    def side_cols(west_block, east_block):
+        east_part = east_block.astype(jnp.float32) * flag(east, (16, 128))
+        west_part = west_block.astype(jnp.float32) * flag(west, (16, 128))
+        return jnp.where(row_16 < 8, east_part, west_part).astype(half)
+
+    wide_map = wide[...]
+    narrow_map = narrow[...]
+    for f in range(2):
+        for part in range(2):
+            value = dot_nn(cot_rows[f, part * 8 : part * 8 + 8].reshape(128, 256), wide_map)
+            cols = side_cols(cols_c[0, f, part], cols_c[1, f, part])
+            value = value + dot_tn(cols, narrow_map)
+            taps[f, 3 + part * 8 : 11 + part * 8] = value.astype(half).reshape(8, 16, 1024)
+        value = dot_nn(rows_c[0, f].reshape(48, 256), wide_map)
+        cols = side_cols(cols_c[2, f, 1], cols_c[3, f, 1])
+        value = (value + dot_tn(cols, narrow_map)[80:128]) * flag(north, (48, 1024))
+        taps[f, 0:3] = value.astype(half).reshape(3, 16, 1024)
+        value = dot_nn(rows_c[1, f].reshape(48, 256), wide_map)
+        cols = side_cols(cols_c[4, f, 0], cols_c[5, f, 0])
+        value = (value + dot_tn(cols, narrow_map)[0:48]) * flag(south, (48, 1024))
+        taps[f, 19:22] = value.astype(half).reshape(3, 16, 1024)
+
+    lane = lax.broadcasted_iota(jnp.int32, (64, 128), 1)
+    spot = lax.rem(lax.div(lane + 1, 2), 64)
+    spot = lax.rem(spot, 10)
+    right = lax.rem(lane, 2) == 0
+    halo_pre = jnp.where(
+        spot == 0,
+        jnp.where(right, cols_p[3].astype(jnp.float32), cols_p[2].astype(jnp.float32)),
+        jnp.where(
+            spot == 9,
+            jnp.where(right, cols_p[5].astype(jnp.float32), cols_p[4].astype(jnp.float32)),
+            jnp.where(right, cols_p[1].astype(jnp.float32), cols_p[0].astype(jnp.float32)),
+        ),
+    )
+    halo_keep = jnp.where(
+        lane == 0, jnp.where(east, 1.0, 0.0), jnp.where(lane == 127, jnp.where(west, 1.0, 0.0), 0.0)
+    )
+    second_t = second[...]
+
+    for f in range(2):
+        for i in range(10):
+            column = (f * 10 + i) * 256
+            window = jnp.concatenate(
+                [
+                    taps[f, 2 * i + a, :, b * 256 : b * 256 + 256]
+                    for a in range(4)
+                    for b in range(4)
+                ],
+                axis=0,
             )
-            grad_inputs = partial_term if grad_inputs is None else grad_inputs + partial_term
-            grad_taps.append(
-                jnp.einsum("fihw,fohw->oi", inputs, window, preferred_element_type=jnp.float32)
-            )
-    grad_kernel = jnp.stack(grad_taps).reshape((4, 4) + kernel.shape[2:])
-    return (grad_inputs, grad_kernel)
+            grad = dot_nn(second_t, window)
+            if i == 0:
+                center = rows_p[0, f]
+            elif i == 9:
+                center = rows_p[1, f]
+            else:
+                center = pre_rows[f, i - 1]
+                windows[:, (f * 8 + i - 1) * 128 : (f * 8 + i) * 128] = window[:, :128]
+            center = center.astype(jnp.float32)
+            sigmoid = jax.nn.sigmoid(1.702 * center)
+            slope = sigmoid + 1.702 * center * sigmoid * (1.0 - sigmoid)
+            value = grad[:, :128] * slope
+            if 0 < i < 9:
+                hidden[:, (f * 8 + i - 1) * 128 : (f * 8 + i) * 128] = (center * sigmoid).astype(half)
+            edge_pre = halo_pre
+            if f + i > 0:
+                edge_pre = pltpu.roll(halo_pre, 128 - 2 * (f * 10 + i), 1)
+            sigmoid = jax.nn.sigmoid(1.702 * edge_pre)
+            slope = sigmoid + 1.702 * edge_pre * sigmoid * (1.0 - sigmoid)
+            edge_value = grad[:, 128:] * slope * halo_keep
+            if i == 0:
+                value = value * flag(north, value.shape)
+                edge_value = edge_value * flag(north, value.shape)
+            if i == 9:
+                value = value * flag(south, value.shape)
+                edge_value = edge_value * flag(south, value.shape)
+            deltas[f, i, :, 0:128] = value.astype(half)
+            deltas[f, i, :, 128:256] = edge_value.astype(half)
+
+    zeros_64 = jnp.zeros((64, 2048), half)
+    hidden_value = hidden[...]
+    grad_second = dot_nt(windows[0:128, :], jnp.concatenate([hidden_value, zeros_64], axis=0))
+    grad_second = grad_second + dot_nt(
+        windows[128:256, :], jnp.concatenate([zeros_64, hidden_value], axis=0)
+    )
+
+    fine_map = fine[...]
+    for f in range(2):
+        for i in range(10):
+            taps_fine[f, i] = dot_nn(deltas[f, i], fine_map).astype(half)
+    low_lane = lax.broadcasted_iota(jnp.int32, (64, 128), 1) < 64
+    for f in range(2):
+        for pair in range(2):
+            for a in range(4):
+                for b in range(4):
+                    low = taps_fine[f, 4 * pair + a, :, b * 128 : b * 128 + 128]
+                    high = taps_fine[f, 4 * pair + 2 + a, :, b * 128 : b * 128 + 128]
+                    windows_fine[
+                        (a * 4 + b) * 64 : (a * 4 + b) * 64 + 64,
+                        (f * 2 + pair) * 128 : (f * 2 + pair) * 128 + 128,
+                    ] = jnp.where(low_lane, low, high)
+
+    token_t = lax.dot_general(
+        proj[...], tokens[...], (((0,), (1,)), ((), ())), preferred_element_type=jnp.float32
+    ).astype(half)
+    mask_row = mask_token[...]
+    mask_t = lax.dot_general(
+        proj[...],
+        jnp.broadcast_to(mask_row, (8, 768)),
+        (((0,), (1,)), ((), ())),
+        preferred_element_type=jnp.float32,
+    ).astype(half)
+    mask_column = mask_t[:, 0:1].astype(jnp.float32)
+    patch = lax.broadcasted_iota(jnp.int32, (256, 64), 0)
+    slot = lax.broadcasted_iota(jnp.int32, (256, 64), 1)
+    picks = []
+    unseen = []
+    first_in = []
+    for f in range(2):
+        hit = (patch == index[f : f + 1, :]) & (slot < live_counts[f])
+        pick = jnp.where(hit, 1.0, 0.0).astype(half)
+        picks.append(pick)
+        shown = dot_nt(jnp.ones((8, 64), half), pick)
+        unseen.append(1.0 - shown)
+        placed = dot_nt(token_t[:, f * 64 : f * 64 + 64], pick)
+        placed = placed + mask_column * unseen[f][0:1, :]
+        first_in.append(placed.astype(half))
+    first_grid = jnp.concatenate(first_in, axis=1)
+    unseen = jnp.concatenate(unseen, axis=1)
+
+    window = windows_fine[...]
+    grid = dot_nn(first[...], window).astype(half)
+    zeros_fine = jnp.zeros((64, 512), half)
+    grad_first = dot_nt(window[0:512], jnp.concatenate([first_grid, zeros_fine], axis=0))
+    grad_first = grad_first + dot_nt(
+        window[512:1024], jnp.concatenate([zeros_fine, first_grid], axis=0)
+    )
+    grid_wide = grid.astype(jnp.float32)
+    mask_sum = jnp.sum(grid_wide * unseen[0:1, :], axis=1, keepdims=True)
+    mask_sum_row = dot_nt(unseen.astype(half), jnp.concatenate([grid, zeros_fine], axis=0))
+    chosen = jnp.concatenate(
+        [dot_nn(grid[:, f * 256 : f * 256 + 256], picks[f]) for f in range(2)], axis=1
+    ).astype(half)
+    grad_proj = dot_nn(chosen, tokens[...]) + mask_sum * mask_row.astype(jnp.float32)
+
+    row_second = lax.broadcasted_iota(jnp.int32, (128, 128), 0)
+    lane_second = lax.broadcasted_iota(jnp.int32, (128, 128), 1)
+    grad_second = jnp.where(
+        (row_second == 12) & (lane_second < 64), mask_sum_row[0:1, :], grad_second
+    )
+    payload[0:4] = grad_first.reshape(4, 8, 16, 128)
+    payload[4:5] = grad_second.reshape(1, 8, 16, 128)
+    for part in range(6):
+        payload[5 + part // 2, (part % 2) * 4 : (part % 2) * 4 + 4] = grad_proj[
+            :, part * 128 : part * 128 + 128
+        ].reshape(4, 16, 128)
+
+    owner_row = owners[...]
+    lane_row = lax.broadcasted_iota(jnp.int32, (1, 128), 1)
+    live_row = lane_row < jnp.where(lane_row < 64, live_counts[0], live_counts[1] + 64)
+    marked = jnp.where(live_row, owner_row, -1).astype(jnp.float32)
+    across = jnp.broadcast_to(marked, (128, 128))
+    down = across.T
+    earlier = (across == down) & (row_second < lane_second)
+    rank = jnp.sum(jnp.where(earlier, 1.0, 0.0), axis=0, keepdims=True)
+    target = jnp.where(live_row, marked * 4.0 + rank, -1.0)
+    number = lax.broadcasted_iota(jnp.int32, (96, 128), 0).astype(jnp.float32) * 2.0
+    zeros_slot = jnp.zeros((64, 128), half)
+    even = jnp.where(number == target, 1.0, 0.0).astype(half)
+    odd = jnp.where(number + 1.0 == target, 1.0, 0.0).astype(half)
+    packed = dot_nt(even, jnp.concatenate([chosen, zeros_slot], axis=0))
+    packed = packed + dot_nt(odd, jnp.concatenate([zeros_slot, chosen], axis=0))
+    rows_out[...] = packed.astype(half).reshape(6, 16, 128)
+
+
+def gradient(scalars, counts, index, owners, arrays):
+    vmem = pl.BlockSpec(memory_space=pltpu.VMEM)
+    smem = pl.BlockSpec(memory_space=pltpu.SMEM)
+    half = jnp.bfloat16
+    return pl.pallas_call(
+        gradient_kernel,
+        out_shape=(
+            jax.ShapeDtypeStruct((8, 8, 16, 128), jnp.float32),
+            jax.ShapeDtypeStruct((6, 16, 128), half),
+        ),
+        in_specs=[smem, smem] + [vmem] * (2 + len(arrays)),
+        out_specs=(vmem, vmem),
+        scratch_shapes=[
+            pltpu.VMEM((2, 22, 16, 1024), half),
+            pltpu.VMEM((256, 2048), half),
+            pltpu.VMEM((64, 2048), half),
+            pltpu.VMEM((2, 10, 64, 256), half),
+            pltpu.VMEM((2, 10, 64, 512), half),
+            pltpu.VMEM((1024, 512), half),
+        ],
+        name="gradient",
+    )(scalars, counts, index, owners, *arrays)
+
+
+def finish_kernel(
+    total, rows_in, proj, token_grad, grad_proj, grad_first, grad_second, grad_mask
+):
+    half = jnp.bfloat16
+    row = lax.broadcasted_iota(jnp.int32, (192, 128), 0)
+    column = lax.broadcasted_iota(jnp.int32, (192, 128), 1)
+    tile = lax.div(row, 4)
+    source = lax.rem(tile, 8) * 16 + lax.div(tile, 8) * 2 + lax.div(lax.rem(row, 4), 2)
+    choose = jnp.where(column == source, 1.0, 0.0).astype(half)
+    arrived = dot_nn(choose, rows_in[...].reshape(128, 128))
+    arrived = jnp.where(lax.div(column, 64) == lax.rem(row, 2), arrived, 0.0).astype(half)
+    proj_t = proj[...].astype(jnp.float32).T
+    double = jnp.concatenate([proj_t, proj_t], axis=0).astype(half)
+    token_grad[...] = dot_nn(arrived, double).astype(half)
+    packed = total[0:4].reshape(512, 128)
+    grad_first[0:512] = packed[:, 0:64]
+    grad_first[512:1024] = packed[:, 64:128]
+    for k in range(16):
+        lanes = 64 * (k // 8)
+        grad_second[k // 4, k % 4] = total[4, k % 8, 0:12, lanes : lanes + 64]
+    for part in range(6):
+        block = total[5 + part // 2, (part % 2) * 4 : (part % 2) * 4 + 4].reshape(64, 128)
+        grad_proj[part * 128 : part * 128 + 128, :] = block.T
+    mask_row = total[4, 0, 12:13, 0:64]
+    grad_mask[...] = lax.dot_general(
+        jnp.broadcast_to(mask_row, (8, 64)),
+        proj[...].astype(jnp.float32),
+        (((1,), (1,)), ((), ())),
+        precision=lax.Precision.HIGHEST,
+        preferred_element_type=jnp.float32,
+    )[0:1]
+
+
+def finish(total, rows_in, proj):
+    vmem = pl.BlockSpec(memory_space=pltpu.VMEM)
+    return pl.pallas_call(
+        finish_kernel,
+        out_shape=(
+            jax.ShapeDtypeStruct((192, 768), jnp.bfloat16),
+            jax.ShapeDtypeStruct((768, 64), jnp.float32),
+            jax.ShapeDtypeStruct((1024, 64), jnp.float32),
+            jax.ShapeDtypeStruct((4, 4, 12, 64), jnp.float32),
+            jax.ShapeDtypeStruct((1, 768), jnp.float32),
+        ),
+        in_specs=[vmem] * 3,
+        out_specs=(vmem,) * 5,
+        name="finish",
+    )(total, rows_in, proj)
 
 
 def exchange_kernel(
@@ -274,6 +701,47 @@
     )(payload, rows_out)
 
 
+def local_gradients(
+    tokens, vis_index, counts, owners, mask_token, proj_weight, up_first, up_second, saved_pre, cotangent
+):
+    half = jnp.bfloat16
+    wide, narrow, fine, edge, cols = tap_select()
+    cot_rows, cot_cols, pre_rows, pre_cols = prepare(cotangent, saved_pre, cols, edge)
+    rows_c, rows_p, cols_c, cols_p = halo(cot_rows, cot_cols, pre_rows, pre_cols)
+    scalars = jnp.stack(
+        [
+            lax.axis_index("ns"),
+            lax.axis_index("ew"),
+            jnp.int32(lax.axis_size("ns")),
+            jnp.int32(lax.axis_size("ew")),
+        ]
+    ).astype(jnp.int32)
+    first_t = up_first.reshape(1024, 64).T
+    second_t = jnp.pad(up_second, ((0, 0), (0, 0), (0, 4), (0, 0))).reshape(256, 64).T
+    return gradient(
+        scalars,
+        counts.reshape(2),
+        vis_index.reshape(2, 64),
+        owners.reshape(1, 128),
+        [
+            tokens.reshape(128, 768),
+            mask_token.reshape(1, 768),
+            proj_weight,
+            first_t,
+            second_t,
+            wide,
+            narrow,
+            fine,
+            cot_rows,
+            pre_rows,
+            rows_c,
+            rows_p,
+            cols_c,
+            cols_p,
+        ],
+    )
+
+
 def per_device(
     tokens,
     vis_index,
@@ -286,91 +754,18 @@
     saved_pre,
     cotangent,
 ):
-    tile_tokens = tokens[0, 0]
-    tile_index = vis_index[0, 0]
-    tile_counts = counts[0, 0]
-    tile_owners = owners[0, 0, :, :, 0]
-    frames, slots, features = tile_tokens.shape
-    channels = proj_weight.shape[1]
-    tok_rows = saved_pre.shape[2] // 2
-    tok_cols = saved_pre.shape[3] // 2
-    patches = tok_rows * tok_cols
-    is_live = jnp.arange(slots, dtype=jnp.int32)[None, :] < tile_counts[:, None]
-    picks = (
-        tile_index[:, :, None] == jnp.arange(patches, dtype=jnp.int32)[None, None, :]
-    ) & is_live[:, :, None]
-    picks_half = picks.astype(jnp.bfloat16)
-    hidden_mask = 1.0 - jnp.sum(picks.astype(jnp.float32), axis=1)
-    token_proj = jnp.einsum(
-        "fvd,dc->fvc", tile_tokens, proj_weight, preferred_element_type=jnp.float32
-    ).astype(jnp.bfloat16)
-    mask_proj = jnp.dot(
-        mask_token[None, :], proj_weight, preferred_element_type=jnp.float32
-    ).astype(jnp.bfloat16)[0]
-    placed = jnp.einsum("fvp,fvc->fcp", picks_half, token_proj, preferred_element_type=jnp.float32)
-    placed = placed + hidden_mask[:, None, :] * mask_proj.astype(jnp.float32)[None, :, None]
-    first_in = placed.astype(jnp.bfloat16).reshape(frames, channels, tok_rows, tok_cols)
-    padded_cot = padded_2(cotangent, (("ew", 3), ("ns", 2)), 1)
-    pre_wide = saved_pre.astype(jnp.float32)
-    hidden = gelu_value(pre_wide).astype(jnp.bfloat16)
-    grad_hidden, grad_second = transpose_back(hidden, padded_cot, up_second)
-    deltas = (grad_hidden * gelu_slope(pre_wide)).astype(jnp.bfloat16)
-    padded_deltas = padded_2(deltas, (("ew", 3), ("ns", 2)), 1)
-    grad_grid, grad_first = transpose_back(first_in, padded_deltas, up_first)
-    grad_grid = grad_grid.astype(jnp.bfloat16).reshape(frames, channels, patches)
-    chosen = jnp.einsum(
-        "fvp,fcp->fvc", picks_half, grad_grid, preferred_element_type=jnp.float32
-    ).astype(jnp.bfloat16)
-    mask_sum = jnp.einsum(
-        "fp,fcp->c", hidden_mask, grad_grid.astype(jnp.float32), precision=lax.Precision.HIGHEST
-    )
-    grad_proj = jnp.einsum("fvd,fvc->dc", tile_tokens, chosen, preferred_element_type=jnp.float32)
-    grad_proj = grad_proj + mask_token.astype(jnp.float32)[:, None] * mask_sum[None, :]
-    owner_count = lax.axis_size("ns")
-    row_count = frames * slots
-    capacity = 3 * row_count // (2 * owner_count)
-    owner_rows = tile_owners.reshape(row_count)
-    live_rows = is_live.reshape(row_count)
-    owner_hits = (
-        (owner_rows[:, None] == jnp.arange(owner_count, dtype=jnp.int32)[None, :])
-        & live_rows[:, None]
-    ).astype(jnp.int32)
-    earlier = jnp.cumsum(owner_hits, axis=0, dtype=jnp.int32) - owner_hits
-    place = jnp.sum(earlier * owner_hits, axis=1, dtype=jnp.int32)
-    target = jnp.where(live_rows, owner_rows * capacity + place, owner_count * capacity)
-    slot_hot = (
-        target[:, None] == jnp.arange(owner_count * capacity, dtype=jnp.int32)[None, :]
-    ).astype(jnp.bfloat16)
-    narrow = jnp.einsum(
-        "rs,rc->sc", slot_hot, chosen.reshape(row_count, channels),
-        preferred_element_type=jnp.float32,
-    ).astype(jnp.bfloat16)
-    rows_out = narrow.reshape(Z_LOW, 16, 128)
-
-    left = grad_first.reshape(1024, channels)
-    right = jnp.concatenate(
-        [
-            grad_proj,
-            grad_second.reshape(192, channels),
-            mask_sum[None, :],
-            jnp.zeros((63, channels), jnp.float32),
-        ],
-        axis=0,
-    )
-    payload = jnp.concatenate([left, right], axis=1).reshape(GROUP_A, GROUP_Y, 16, 128)
+    payload, rows_out = local_gradients(
+        tokens, vis_index, counts, owners, mask_token, proj_weight, up_first, up_second, saved_pre, cotangent
+    )
     total, rows_in = exchange(payload, rows_out)
-    total = total.reshape(1024, 128)
-    grad_first = total[:, :channels].reshape(4, 4, channels, channels)
-    grad_proj = total[:768, channels:]
-    grad_second = total[768:960, channels:].reshape(4, 4, 12, channels)
-    mask_sum = total[960, channels:]
-    grad_mask = jnp.dot(proj_weight.astype(jnp.float32), mask_sum, precision=lax.Precision.HIGHEST)
-    arrived = rows_in[:, : 2 * Z_LOW].reshape(GROUP_A, Z_LOW, 2, 128).transpose(1, 0, 2, 3)
-    arrived = arrived.reshape(owner_count * capacity, channels)
-    token_grad = jnp.einsum(
-        "rc,dc->rd", arrived, proj_weight, preferred_element_type=jnp.float32
-    ).astype(jnp.bfloat16)
-    return (token_grad[None, None], grad_proj, grad_first, grad_second, grad_mask)
+    token_grad, grad_proj, grad_first, grad_second, grad_mask = finish(total, rows_in, proj_weight)
+    return (
+        token_grad[None, None],
+        grad_proj,
+        grad_first.reshape(4, 4, 64, 64),
+        grad_second,
+        grad_mask.reshape(768),
+    )
 
 
 def solution(mesh):

time: 288 us -> 96 us (0.33)
  local copies, waits for them, and re-layouts: 150 us -> 9.73 us
  starting transfers between devices: 26.3 us -> 0 us
  matrix products: 22.7 us -> 0 us
  Pallas kernels: 75.5 us -> 82.5 us
  waiting for transfers between devices: 4.66 us -> 0 us
  other arithmetic: 6.35 us -> 2.6 us
    slice x40 -> x0, local copies, waits for them, and re-layouts: 140 us -> none  [the longest x32 138 us: transpose_back(): padded[:, :, tap_y:tap_y + 2 * height:2, tap_x:tap_x + 2 * breadth:2]]
    pallas_call x0 -> x4, Pallas kernels: none -> 43.6 us  [the longest x1 32.2 us: halo(): pl.pallas_call(halo_kernel, out_shape=(jax.ShapeDtypeStruct((2, 2, 3, 16,...]
    pallas_call x1, Pallas kernels: 75.5 us -> 38.9 us  [exchange(): pl.pallas_call(exchange_kernel, out_shape=(jax.ShapeDtypeStruct((GROUP_A,...]
    ppermute x8 -> x0, starting transfers between devices: 26.3 us -> none  [the longest x4 14.2 us: padded_2(): lax.ppermute(lax.slice_in_dim(block, block.shape[dim] - width, None, axis...]
    dot_general x72 -> x0, matrix products: 22.7 us -> none  [the longest x32 14.1 us: transpose_back(): jnp.einsum('oi,fohw->fihw', kernel[tap_y, tap_x], window, preferred_eleme...]
    ppermute x8 -> x0, waiting for transfers between devices: 4.66 us -> none  [the longest x4 4.09 us: padded_2(): lax.ppermute(lax.slice_in_dim(block, 0, width, axis=dim), axis, backward)]
    concatenate x6 -> x0, other arithmetic: 3.15 us -> none  [the longest x4 2.07 us: padded_2(): block = jnp.concatenate([low, block, high], axis=dim)]
    unnamed x112 -> x11, local copies, waits for them, and re-layouts: 7.68 us -> 6.32 us
  transfers between devices with their start and end apart: 8 -> 0, of which waited for: 2 -> 0; matrix products, arithmetic and copies ran while one was open for 8% -> 0% of each run, Pallas kernels for 0% -> 0%
where the time goes in v2:
time: 96 us; the launch traced here: 95.5 us
  Pallas kernels  82.5 us (86%)
  local copies, waits for them, and re-layouts  9.73 us (10%)
  other arithmetic  2.6 us (3%)
    pallas_call x1, Pallas kernels, exchange(): pl.pallas_call(exchange_kernel, out_shape=(jax.ShapeDtypeStruct((GROUP_A,...  38.9 us
    pallas_call x1, Pallas kernels, halo(): pl.pallas_call(halo_kernel, out_shape=(jax.ShapeDtypeStruct((2, 2, 3, 16,...  32.2 us
    pallas_call x1, Pallas kernels, gradient(): pl.pallas_call(gradient_kernel, out_shape=(jax.ShapeDtypeStruct((8, 8, 16...  6.43 us
    unnamed x11, local copies, waits for them, and re-layouts  6.32 us
    pallas_call x1, Pallas kernels, finish(): pl.pallas_call(finish_kernel, out_shape=(jax.ShapeDtypeStruct((192, 768),...  2.6 us
    pallas_call x1, Pallas kernels, prepare(): pl.pallas_call(prepare_kernel, out_shape=(jax.ShapeDtypeStruct((2, 16, 16...  2.38 us

profile of v2, /device:TPU:1, one launch (start us, length us, event | category | flops | bytes accessed | tf_op | source)
XLA Modules:
  0.0 95.5 jit_solution(11592458319938405299)
XLA Ops:
  0.6 0.0 copy-start
  0.7 0.7 pad_add_fusion.place
  1.3 0.5 broadcast.6
  1.8 1.3 %reduce.4 = s32[2,64]{1,0:T(2,128)S(1)} reduce(s32[1,1,2,64,1]{3,4,2,1,0:T(1,128)} %param.18, s32[]{:T(128)} %broadcast.6), dimensions={0,1,4}, to_apply=%param.18.reduce_sub_computation.3 | reduce | bytes 1028 | tf_op args[3]
  3.2 0.6 reshape.39.owners
  3.8 1.3 %reshape.41.mask_token = bf16[1,768]{1,0:T(2,128)(2,1)} reshape(bf16[768]{0:T(1024)(128)(2,1)} %param.19) | data formatting | bytes 3072 | tf_op jit(solution)/shard_map/reshape | solution.py:728
  5.0 0.8 copy.34
  5.9 0.7 copy.28
  6.6 0.0 copy-done
  6.6 0.0 copy-start.1
  6.6 0.8 copy.33
  7.4 0.1 copy-done.1
  7.5 0.8 copy.29.proj
  8.3 2.4 %prepare.1 = (bf16[2,16,16,256]{3,2,1,0:T(8,128)(2,1)}, bf16[2,2,16,128]{3,2,1,0:T(8,128)(2,1)}, bf16[2,8,64,128]{3,2,1,0:T(8,128)(2,1)}, bf16[64,128]{1,0:T(8,128)(2,1)}) custom-call(bf16[2,12,16,256]{3,2,1,0:T(8,128)(2,1)} %cot.1, bf16[2,64,8,128]{3,2,1,0:T(8,128)(2,1)} %pre.1, bf16[16,256]{1,0:T(8,128)(2,1)} %constant.27.clone.cols, ...), custom_call_target="tpu_custom_call" | custom-call | tf_op jit(solution)/shard_map/prepare/pallas_call | solution.py:103
  10.7 32.2 %halo.1 = (bf16[2,2,3,16,256]{4,3,2,1,0:T(8,128)(2,1)}, bf16[2,2,64,128]{3,2,1,0:T(8,128)(2,1)}, bf16[6,2,2,16,128]{4,3,2,1,0:T(8,128)(2,1)}, bf16[6,64,128]{2,1,0:T(8,128)(2,1)}) custom-call(bf16[2,16,16,256]{3,2,1,0:T(8,128)(2,1)} %get-tuple-element.22.cot_rows, bf16[2,2,16,128]{3,2,1,0:T(8,128)(2,1)} %get-tuple-element.24.cot_cols, ...), custom_call_target="tpu_custom_call" | custom-call | tf_op jit(solution)/shard_map/halo/pallas_call | solution.py:175
  42.8 6.4 %gradient.1 = (f32[8,8,16,128]{3,2,1,0:T(8,128)}, bf16[6,16,128]{2,1,0:T(8,128)(2,1)}) custom-call(s32[4]{0:T(128)} %pad_add_fusion.place, s32[2]{0:T(128)} %bitcast.18, s32[2,64]{1,0:T(2,128)} %bitcast.17, s32[1,128]{1,0:T(1,128)} %reshape.39.owners, bf16[128,768]{1,0:T(8,128)(2,1)} %bitcast.15, bf16[1,768]{1,0:T(2,128)(2,1)} %reshape.41.mask_token, ...), custom_call_target="tpu_custom_call" | custom-call | tf_op jit(solution)/shard_map/gradient/pallas_call | solution.py:415
  49.3 38.9 %exchange.1 = (f32[8,8,16,128]{3,2,1,0:T(8,128)}, bf16[8,16,128]{2,1,0:T(8,128)(2,1)}) custom-call(f32[8,8,16,128]{3,2,1,0:T(8,128)} %get-tuple-element.30.payload, bf16[6,16,128]{2,1,0:T(8,128)(2,1)} %get-tuple-element.31.rows_out), custom_call_target="tpu_custom_call" | custom-call | tf_op jit(solution)/shard_map/exchange/pallas_call | solution.py:666
  88.2 2.6 %finish.1 = (bf16[192,768]{1,0:T(8,128)(2,1)}, f32[768,64]{1,0:T(8,128)}, f32[1024,64]{1,0:T(8,128)}, f32[4,4,12,64]{3,2,1,0:T(8,128)}, f32[1,768]{1,0:T(1,128)}) custom-call(f32[8,8,16,128]{3,2,1,0:T(8,128)} %get-tuple-element.32.total, bf16[8,16,128]{2,1,0:T(8,128)(2,1)} %get-tuple-element.33.rows_in, bf16[768,64]{1,0:T(8,128)(2,1)} %copy.29.proj), custom_call_target="tpu_custom_call" | custom-call | tf_op jit(solution)/shard_map/finish/pallas_call | solution.py:470
  90.8 0.0 copy-start.2
  90.8 0.7 copy-done.2
  91.5 0.6 reduce.1
  92.1 1.6 %copy.32 = f32[4,4,12,64]{3,1,2,0:T(4,128)} copy(f32[4,4,12,64]{3,2,1,0:T(8,128)} %get-tuple-element.47) | data formatting | bytes 98304
  93.7 1.8 %copy.31 = f32[768,64]{0,1:T(8,128)} copy(f32[768,64]{1,0:T(8,128)} %get-tuple-element.45) | data formatting | bytes 393216
  (1 shorter events, 0.0 us)
Async XLA Ops:
  0.6 6.0 %copy-start = (bf16[4,4,64,64]{3,2,1,0:T(8,128)(2,1)S(1)}, bf16[4,4,64,64]{3,2,1,0:T(8,128)(2,1)}, u32[]{:S(2)}) copy-start(bf16[4,4,64,64]{3,2,1,0:T(8,128)(2,1)} %param.21) | copy-start | bytes 393220
  6.6 0.9 copy-start.1
  90.8 0.7 copy-start.2

commit v3 on v0

v3 whole, which is shorter than its diff:
```python
import jax
import jax.numpy as jnp
import numpy as np
from jax import lax
from jax.experimental import pallas as pl
from jax.experimental.pallas import tpu as pltpu
from jax.sharding import PartitionSpec as P

MESH = pl.DeviceIdType.MESH
GROUP_A = 8
GROUP_Y = 8
Z_LOW = 6
Z_HIGH = 2


BANDS_PAD = 16
LANES = 128


def tap_select():
    wide = np.zeros((256, 4, 256), np.float32)
    halo = np.zeros((16, 4, 256), np.float32)
    for tap in range(4):
        for lane, cell in [(j, j) for j in range(128)] + [(128, 128), (255, -1)]:
            col = 2 * cell + tap - 1
            if col < 0:
                halo[8 + col + 3, tap, lane] = 1
            elif col < 256:
                wide[col, tap, lane] = 1
            else:
                halo[col - 256, tap, lane] = 1
    fine = np.zeros((256, 4, 2, 64), np.float32)
    for tap in range(4):
        for cell in range(64):
            col = 2 * cell + tap - 1
            fine[col if col >= 0 else 255, tap, :, cell] = 1
    edge = np.zeros((2, 8, 128, 128), np.float32)
    for frame in range(2):
        for row in range(8):
            spots = [row + 1] + ([0] if row == 7 else []) + ([9] if row == 0 else [])
            for spot in spots:
                pair = 2 * (frame * 10 + spot)
                edge[frame, row, 0, pair] = 1
                edge[frame, row, 127, (pair - 1) % 128] = 1
    cols = np.zeros((16, 256), np.float32)
    for k in range(3):
        cols[k, k] = 1
        cols[8 + k, 253 + k] = 1
    order = np.zeros((4, 12, 4, 4, 4, 16), np.float32)
    for a in range(4):
        for o in range(12):
            for b in range(4):
                order[a, o, b, a, b, o] = 1
    half = jnp.bfloat16
    return (
        jnp.asarray(wide.reshape(256, 1024), half),
        jnp.asarray(halo.reshape(16, 1024), half),
        jnp.asarray(fine.reshape(256, 512), half),
        jnp.asarray(edge.reshape(2048, 128), half),
        jnp.asarray(cols, half),
        jnp.asarray(order.reshape(192, 256), half),
    )


def dot_nn(a, b):
    return jnp.dot(a, b, preferred_element_type=jnp.float32)


def dot_nt(a, b):
    return lax.dot_general(a, b, (((1,), (1,)), ((), ())), preferred_element_type=jnp.float32)


def dot_tn(a, b):
    return lax.dot_general(a, b, (((0,), (0,)), ((), ())), preferred_element_type=jnp.float32)


SIDES = ((-1, 0), (1, 0), (0, -1), (0, 1), (-1, -1), (-1, 1), (1, -1), (1, 1))
STREAMS = 2
Z_COUNT = Z_LOW * Z_HIGH


def main_kernel(
    live_counts,
    index,
    owners,
    tokens,
    mask_token,
    proj_t,
    first,
    second,
    cot,
    pre,
    wide,
    narrow,
    fine,
    edge,
    cols,
    order,
    total_out,
    rows_in,
    wide_c,
    wide_p,
    cot_rows,
    cot_cols,
    pre_rows,
    pre_cols,
    rows_c,
    rows_p,
    cols_c,
    cols_p,
    taps,
    windows,
    hidden,
    deltas,
    taps_fine,
    windows_fine,
    payload,
    buf_a,
    red_a,
    buf_b,
    buf_c,
    buf_d,
    rows_out,
    tok_z,
    tok_s,
    buf_s,
    send,
    recv,
    local_sem,
):
    half = jnp.bfloat16
    n = lax.axis_index("ns")
    e = lax.axis_index("ew")
    n_count = lax.axis_size("ns")
    e_count = lax.axis_size("ew")
    g = lax.rem(n, GROUP_A)
    zl = lax.div(n, GROUP_A)
    zh = lax.div(e, GROUP_Y)
    y = lax.rem(e, GROUP_Y)
    zi = zh * Z_LOW + zl

    def peer_side(side):
        return {
            "ew": lax.rem(e + side[1] + e_count, e_count),
            "ns": lax.rem(n + side[0] + n_count, n_count),
        }

    def peer_a(k):
        other = lax.rem(g + k, GROUP_A)
        return other, {"ew": e, "ns": zl * GROUP_A + other}

    def peer_b(k):
        other = lax.rem(y + k, GROUP_Y)
        return other, {"ew": zh * GROUP_Y + other, "ns": n}

    def peer_c(k):
        other = lax.rem(zi + k, Z_COUNT)
        return other, {
            "ew": lax.div(other, Z_LOW) * GROUP_Y + y,
            "ns": lax.rem(other, Z_LOW) * GROUP_A + g,
        }

    def peer_z(k):
        other = lax.rem(zl + k, Z_LOW)
        return other, {"ew": e, "ns": other * GROUP_A + g}

    barrier = pltpu.get_barrier_semaphore()
    for side in SIDES:
        pl.semaphore_signal(barrier, inc=1, device_id=peer_side(side), device_id_type=MESH)
    for count, peer in ((GROUP_A, peer_a), (GROUP_Y, peer_b), (Z_COUNT, peer_c)):
        for k in range(1, count):
            pl.semaphore_signal(barrier, inc=1, device_id=peer(k)[1], device_id_type=MESH)

    used = [0]

    def put(src, dst, target):
        slot = used[0]
        used[0] += 1
        copy = pltpu.make_async_remote_copy(
            src_ref=src,
            dst_ref=dst,
            send_sem=send.at[slot],
            recv_sem=recv.at[slot],
            device_id=target,
            device_id_type=MESH,
        )
        copy.start()
        return copy

    def wait_all(copies):
        for copy in copies:
            copy.wait()

    for f in range(2):
        for o in range(12):
            for part in range(2):
                wide_c[part, pl.ds((f * 16 + o) * 16, 16), :] = cot[
                    f, o, :, part * 128 : part * 128 + 128
                ].astype(jnp.float32)
        for part in range(2):
            wide_c[part, pl.ds((f * 16 + 12) * 16, 64), :] = jnp.zeros((64, 128), jnp.float32)
        for r in range(16):
            for part in range(2):
                cot_rows[f, r, :, part * 128 : part * 128 + 128] = wide_c[
                    part, pl.ds(f * 256 + r, 16, stride=16), :
                ].astype(half)
        for part in range(2):
            block = cot_rows[f, part * 8 : part * 8 + 8].reshape(128, 256)
            cot_cols[f, part] = dot_nt(cols[...], block).astype(half)
    for f in range(2):
        wide_p[pl.ds(f * 512, 512), :] = pre[f].reshape(512, 128).astype(jnp.float32)
    packed = jnp.zeros((64, 128), jnp.float32)
    for f in range(2):
        for i in range(8):
            slab = wide_p[pl.ds(f * 512 + i, 64, stride=8), :].astype(half)
            pre_rows[f, i] = slab
            packed = packed + dot_nn(slab, edge[pl.ds((f * 8 + i) * 128, 128), :])
    pre_cols[...] = packed.astype(half)

    pl.semaphore_wait(barrier, len(SIDES) + GROUP_A + GROUP_Y + Z_COUNT - 3)

    halo = []
    halo.append(put(cot_cols, cols_c.at[1], peer_side((0, -1))))
    halo.append(put(cot_cols, cols_c.at[0], peer_side((0, 1))))
    halo.append(put(pre_cols, cols_p.at[1], peer_side((0, -1))))
    halo.append(put(pre_cols, cols_p.at[0], peer_side((0, 1))))
    halo.append(put(cot_cols, cols_c.at[5], peer_side((-1, -1))))
    halo.append(put(cot_cols, cols_c.at[4], peer_side((-1, 1))))
    halo.append(put(cot_cols, cols_c.at[3], peer_side((1, -1))))
    halo.append(put(cot_cols, cols_c.at[2], peer_side((1, 1))))
    halo.append(put(pre_cols, cols_p.at[5], peer_side((-1, -1))))
    halo.append(put(pre_cols, cols_p.at[4], peer_side((-1, 1))))
    halo.append(put(pre_cols, cols_p.at[3], peer_side((1, -1))))
    halo.append(put(pre_cols, cols_p.at[2], peer_side((1, 1))))
    halo.append(put(cot_rows.at[:, 0:3], rows_c.at[1], peer_side((-1, 0))))
    halo.append(put(cot_rows.at[:, 13:16], rows_c.at[0], peer_side((1, 0))))
    halo.append(put(pre_rows.at[:, 0], rows_p.at[1], peer_side((-1, 0))))
    halo.append(put(pre_rows.at[:, 7], rows_p.at[0], peer_side((1, 0))))

    token_t = dot_nt(proj_t[...], tokens[...]).astype(half)
    mask_row = mask_token[...].astype(jnp.float32).reshape(1, 768)
    mask_t = dot_nt(proj_t[...], jnp.broadcast_to(mask_row, (8, 768)).astype(half)).astype(half)
    mask_column = mask_t[:, 0:1].astype(jnp.float32)
    patch = lax.broadcasted_iota(jnp.int32, (256, 64), 0)
    slot = lax.broadcasted_iota(jnp.int32, (256, 64), 1)
    picks = []
    unseen = []
    first_in = []
    for f in range(2):
        hit = (patch == index[f : f + 1, :]) & (slot < live_counts[f])
        pick = jnp.where(hit, 1.0, 0.0).astype(half)
        picks.append(pick)
        shown = dot_nt(jnp.ones((8, 64), half), pick)
        unseen.append(1.0 - shown)
        placed = dot_nt(token_t[:, f * 64 : f * 64 + 64], pick)
        placed = placed + mask_column * unseen[f][0:1, :]
        first_in.append(placed.astype(half))
    first_grid = jnp.concatenate(first_in, axis=1)
    unseen = jnp.concatenate(unseen, axis=1)
    second_t = dot_tn(
        second[...].astype(jnp.float32).reshape(192, 64).astype(half), order[...]
    ).astype(half)

    row_second = lax.broadcasted_iota(jnp.int32, (128, 128), 0)
    lane_second = lax.broadcasted_iota(jnp.int32, (128, 128), 1)
    owner_row = jnp.concatenate([owners[0], owners[1]], axis=1)
    lane_row = lax.broadcasted_iota(jnp.int32, (1, 128), 1)
    live_row = lane_row < jnp.where(lane_row < 64, live_counts[0], live_counts[1] + 64)
    marked = jnp.where(live_row, owner_row, -1).astype(jnp.float32)
    across = jnp.broadcast_to(marked, (128, 128))
    down = across.T
    earlier = (across == down) & (row_second < lane_second)
    rank = jnp.sum(jnp.where(earlier, 1.0, 0.0), axis=0, keepdims=True)
    target = jnp.where(live_row, marked * 4.0 + rank, -1.0)
    number = lax.broadcasted_iota(jnp.int32, (96, 128), 0).astype(jnp.float32) * 2.0
    even = jnp.where(number == target, 1.0, 0.0).astype(half)
    odd = jnp.where(number + 1.0 == target, 1.0, 0.0).astype(half)

    wait_all(halo)

    north = n > 0
    south = n < n_count - 1
    west = e > 0
    east = e < e_count - 1

    def flag(condition, shape):
        return jnp.full(shape, jnp.where(condition, 1.0, 0.0), jnp.float32)

    row_16 = lax.broadcasted_iota(jnp.int32, (16, 128), 0)

    def side_cols(west_block, east_block):
        east_part = east_block.astype(jnp.float32) * flag(east, (16, 128))
        west_part = west_block.astype(jnp.float32) * flag(west, (16, 128))
        return jnp.where(row_16 < 8, east_part, west_part).astype(half)

    wide_map = wide[...]
    narrow_map = narrow[...]
    for f in range(2):
        for part in range(2):
            value = dot_nn(cot_rows[f, part * 8 : part * 8 + 8].reshape(128, 256), wide_map)
            side = side_cols(cols_c[0, f, part], cols_c[1, f, part])
            value = value + dot_tn(side, narrow_map)
            taps[f, 3 + part * 8 : 11 + part * 8] = value.astype(half).reshape(8, 16, 1024)
        value = dot_nn(rows_c[0, f].reshape(48, 256), wide_map)
        side = side_cols(cols_c[2, f, 1], cols_c[3, f, 1])
        value = (value + dot_tn(side, narrow_map)[80:128]) * flag(north, (48, 1024))
        taps[f, 0:3] = value.astype(half).reshape(3, 16, 1024)
        value = dot_nn(rows_c[1, f].reshape(48, 256), wide_map)
        side = side_cols(cols_c[4, f, 0], cols_c[5, f, 0])
        value = (value + dot_tn(side, narrow_map)[0:48]) * flag(south, (48, 1024))
        taps[f, 19:22] = value.astype(half).reshape(3, 16, 1024)

    lane = lax.broadcasted_iota(jnp.int32, (64, 128), 1)
    spot = lax.rem(lax.rem(lax.div(lane + 1, 2), 64), 10)
    right = lax.rem(lane, 2) == 0
    halo_pre = jnp.where(
        spot == 0,
        jnp.where(right, cols_p[3].astype(jnp.float32), cols_p[2].astype(jnp.float32)),
        jnp.where(
            spot == 9,
            jnp.where(right, cols_p[5].astype(jnp.float32), cols_p[4].astype(jnp.float32)),
            jnp.where(right, cols_p[1].astype(jnp.float32), cols_p[0].astype(jnp.float32)),
        ),
    )
    halo_keep = jnp.where(
        lane == 0, jnp.where(east, 1.0, 0.0), jnp.where(lane == 127, jnp.where(west, 1.0, 0.0), 0.0)
    )
    sigmoid = jax.nn.sigmoid(1.702 * halo_pre)
    halo_slope = sigmoid + 1.702 * halo_pre * sigmoid * (1.0 - sigmoid)

    for f in range(2):
        for i in range(10):
            window = jnp.concatenate(
                [
                    taps[f, 2 * i + a, :, b * 256 : b * 256 + 256]
                    for a in range(4)
                    for b in range(4)
                ],
                axis=0,
            )
            grad = dot_nn(second_t, window)
            if i == 0:
                center = rows_p[0, f]
            elif i == 9:
                center = rows_p[1, f]
            else:
                center = pre_rows[f, i - 1]
                windows[:, (f * 8 + i - 1) * 128 : (f * 8 + i) * 128] = window[:, :128]
            center = center.astype(jnp.float32)
            sigmoid = jax.nn.sigmoid(1.702 * center)
            slope = sigmoid + 1.702 * center * sigmoid * (1.0 - sigmoid)
            value = grad[:, :128] * slope
            if 0 < i < 9:
                hidden[:, (f * 8 + i - 1) * 128 : (f * 8 + i) * 128] = (center * sigmoid).astype(half)
            edge_slope = halo_slope
            if f + i > 0:
                edge_slope = pltpu.roll(halo_slope, 128 - 2 * (f * 10 + i), 1)
            edge_value = grad[:, 128:] * edge_slope * halo_keep
            if i == 0:
                value = value * flag(north, value.shape)
                edge_value = edge_value * flag(north, value.shape)
            if i == 9:
                value = value * flag(south, value.shape)
                edge_value = edge_value * flag(south, value.shape)
            deltas[f, i, :, 0:128] = value.astype(half)
            deltas[f, i, :, 128:256] = edge_value.astype(half)

    fine_map = fine[...]
    for f in range(2):
        for i in range(10):
            taps_fine[f, i] = dot_nn(deltas[f, i], fine_map).astype(half)
    low_lane = lane < 64
    for f in range(2):
        for pair in range(2):
            for a in range(4):
                for b in range(4):
                    low = taps_fine[f, 4 * pair + a, :, b * 128 : b * 128 + 128]
                    high = taps_fine[f, 4 * pair + 2 + a, :, b * 128 : b * 128 + 128]
                    windows_fine[
                        (a * 4 + b) * 64 : (a * 4 + b) * 64 + 64,
                        (f * 2 + pair) * 128 : (f * 2 + pair) * 128 + 128,
                    ] = jnp.where(low_lane, low, high)

    zeros_fine = jnp.zeros((64, 512), half)
    grad_first = dot_nt(windows_fine[0:512], jnp.concatenate([first_grid, zeros_fine], axis=0))
    grad_first = grad_first + dot_nt(
        windows_fine[512:1024], jnp.concatenate([zeros_fine, first_grid], axis=0)
    )
    payload[0] = grad_first.reshape(GROUP_A, GROUP_Y, 8, 128)

    def scatter_a(s):
        copies = []
        for k in range(1, GROUP_A):
            other, target_device = peer_a(k)
            copies.append(put(payload.at[s, other], buf_a.at[s, k - 1], target_device))
        return copies

    copies_a = [scatter_a(0)]

    grid = dot_tn(first[...], windows_fine[...]).astype(half)
    chosen = jnp.concatenate(
        [dot_nn(grid[:, f * 256 : f * 256 + 256], picks[f]) for f in range(2)], axis=1
    ).astype(half)
    zeros_slot = jnp.zeros((64, 128), half)
    outgoing = dot_nt(even, jnp.concatenate([chosen, zeros_slot], axis=0))
    outgoing = outgoing + dot_nt(odd, jnp.concatenate([zeros_slot, chosen], axis=0))
    rows_out[...] = outgoing.astype(half).reshape(Z_LOW, 16, 128)
    copies_z = []
    for k in range(1, Z_LOW):
        other, target_device = peer_z(k)
        copies_z.append(put(rows_out.at[other], tok_z.at[zl], target_device))
    tok_z[zl] = rows_out[zl]

    zeros_64 = jnp.zeros((64, 2048), half)
    hidden_value = hidden[...]
    grad_second = dot_nt(windows[0:128, :], jnp.concatenate([hidden_value, zeros_64], axis=0))
    grad_second = grad_second + dot_nt(
        windows[128:256, :], jnp.concatenate([zeros_64, hidden_value], axis=0)
    )
    mask_sum = jnp.sum(grid.astype(jnp.float32) * unseen[0:1, :], axis=1, keepdims=True)
    mask_sum_row = dot_nt(unseen.astype(half), jnp.concatenate([grid, zeros_fine], axis=0))
    grad_proj = dot_nn(chosen, tokens[...]) + mask_sum * mask_row
    grad_second = jnp.where(
        (row_second == 12) & (lane_second < 64), mask_sum_row[0:1, :], grad_second
    )
    payload[1, 0:2] = grad_second.reshape(2, GROUP_Y, 8, 128)
    for part in range(6):
        payload[1, 2 + part] = grad_proj[:, part * 128 : part * 128 + 128].reshape(GROUP_Y, 8, 128)
    copies_a.append(scatter_a(1))

    copies_b = []
    for s in range(STREAMS):
        wait_all(copies_a[s])
        summed = payload[s, g]
        for k in range(1, GROUP_A):
            summed = summed + buf_a[s, k - 1]
        red_a[s] = summed
        copies = []
        for k in range(1, GROUP_Y):
            other, target_device = peer_b(k)
            copies.append(put(red_a.at[s, other], buf_b.at[s, k - 1], target_device))
        copies_b.append(copies)

    wait_all(copies_z)
    stacked = tok_z[...].reshape(Z_LOW * 16, 128)
    picked = lax.broadcasted_iota(jnp.int32, (GROUP_A * 16, Z_LOW * 16), 0)
    column = lax.broadcasted_iota(jnp.int32, (GROUP_A * 16, Z_LOW * 16), 1)
    wanted = ((picked % 16) // 2) * 16 + (picked // 16) * 2 + picked % 2
    choose = jnp.where(column == wanted, 1.0, 0.0).astype(half)
    tok_s[...] = dot_nn(choose, stacked).astype(half).reshape(GROUP_A, 16, 128)
    copies_t = []
    for k in range(1, GROUP_A):
        other, target_device = peer_a(k)
        copies_t.append(put(tok_s.at[other], buf_s.at[g], target_device))
    buf_s[g] = tok_s[g]

    copies_c = []
    for s in range(STREAMS):
        wait_all(copies_b[s])
        summed = red_a[s, y]
        for k in range(1, GROUP_Y):
            summed = summed + buf_b[s, k - 1]
        buf_c[s, zi] = summed
        copies = []
        for k in range(1, Z_COUNT):
            copies.append(put(buf_c.at[s, zi], buf_c.at[s, zi], peer_c(k)[1]))
        copies_c.append(copies)

    row_8 = lax.broadcasted_iota(jnp.int32, (8, 128), 0)
    copies_d = []
    for s in range(STREAMS):
        wait_all(copies_c[s])
        summed = buf_c[s, 0]
        for k in range(1, Z_COUNT):
            summed = summed + buf_c[s, k]
        if s == 1:
            rounded = summed.astype(half).astype(jnp.float32)
            rest = jnp.broadcast_to((summed - rounded)[4:5], (8, 128))
            here = jnp.where((g == 0) & (y == 1), 5, -1)
            summed = jnp.where(row_8 == here, rest, summed)
        buf_d[s, y] = summed.astype(half)
        copies = []
        for k in range(1, GROUP_Y):
            copies.append(put(buf_d.at[s, y], buf_d.at[s, y], peer_b(k)[1]))
        copies_d.append(copies)

    copies_e = []
    own = []
    for s in range(STREAMS):
        wait_all(copies_d[s])
        for k in range(1, GROUP_A):
            copies_e.append(put(buf_d.at[s], total_out.at[s, g], peer_a(k)[1]))
        copy = pltpu.make_async_copy(buf_d.at[s], total_out.at[s, g], local_sem.at[s])
        copy.start()
        own.append(copy)
    wait_all(copies_t)
    rows_in[...] = buf_s[...]
    wait_all(own)
    wait_all(copies_e)


COPIES = 16 + 2 * (2 * (GROUP_A - 1) + 2 * (GROUP_Y - 1) + Z_COUNT - 1) + Z_LOW - 1 + GROUP_A - 1


def main(counts, index, owners, arrays):
    vmem = pl.BlockSpec(memory_space=pltpu.VMEM)
    smem = pl.BlockSpec(memory_space=pltpu.SMEM)
    half = jnp.bfloat16
    wide = jnp.float32
    dma = pltpu.SemaphoreType.DMA
    return pl.pallas_call(
        main_kernel,
        out_shape=(
            jax.ShapeDtypeStruct((STREAMS, GROUP_A, GROUP_Y, 8, 128), half),
            jax.ShapeDtypeStruct((GROUP_A, 16, 128), half),
        ),
        in_specs=[smem] + [vmem] * (2 + len(arrays)),
        out_specs=(pl.BlockSpec(memory_space=pl.ANY), vmem),
        scratch_shapes=[
            pltpu.VMEM((2, 512, 128), wide),
            pltpu.VMEM((1024, 128), wide),
            pltpu.VMEM((2, 16, 16, 256), half),
            pltpu.VMEM((2, 2, 16, 128), half),
            pltpu.VMEM((2, 8, 64, 128), half),
            pltpu.VMEM((64, 128), half),
            pltpu.VMEM((2, 2, 3, 16, 256), half),
            pltpu.VMEM((2, 2, 64, 128), half),
            pltpu.VMEM((6, 2, 2, 16, 128), half),
            pltpu.VMEM((6, 64, 128), half),
            pltpu.VMEM((2, 22, 16, 1024), half),
            pltpu.VMEM((256, 2048), half),
            pltpu.VMEM((64, 2048), half),
            pltpu.VMEM((2, 10, 64, 256), half),
            pltpu.VMEM((2, 10, 64, 512), half),
            pltpu.VMEM((1024, 512), half),
            pltpu.VMEM((STREAMS, GROUP_A, GROUP_Y, 8, 128), wide),
            pltpu.VMEM((STREAMS, GROUP_A - 1, GROUP_Y, 8, 128), wide),
            pltpu.VMEM((STREAMS, GROUP_Y, 8, 128), wide),
            pltpu.VMEM((STREAMS, GROUP_Y - 1, 8, 128), wide),
            pltpu.VMEM((STREAMS, Z_COUNT, 8, 128), wide),
            pltpu.VMEM((STREAMS, GROUP_Y, 8, 128), half),
            pltpu.VMEM((Z_LOW, 16, 128), half),
            pltpu.VMEM((Z_LOW, 16, 128), half),
            pltpu.VMEM((GROUP_A, 16, 128), half),
            pltpu.VMEM((GROUP_A, 16, 128), half),
            dma((COPIES,)),
            dma((COPIES,)),
            dma((STREAMS,)),
        ],
        compiler_params=pltpu.CompilerParams(collective_id=0, has_side_effects=True),
        name="main",
    )(counts, index, owners, *arrays)


def finish_kernel(
    total, rows_in, proj_t, token_grad, grad_proj, grad_first, grad_second, grad_mask
):
    half = jnp.bfloat16
    row = lax.broadcasted_iota(jnp.int32, (192, 128), 0)
    column = lax.broadcasted_iota(jnp.int32, (192, 128), 1)
    tile = lax.div(row, 4)
    source = lax.rem(tile, 8) * 16 + lax.div(tile, 8) * 2 + lax.div(lax.rem(row, 4), 2)
    choose = jnp.where(column == source, 1.0, 0.0).astype(half)
    arrived = dot_nn(choose, rows_in[...].reshape(128, 128))
    arrived = jnp.where(lax.div(column, 64) == lax.rem(row, 2), arrived, 0.0).astype(half)
    double = jnp.concatenate([proj_t[...], proj_t[...]], axis=0)
    token_grad[...] = dot_nn(arrived, double).astype(half)
    packed = total[0].astype(jnp.float32).reshape(512, 128)
    grad_first[0:512] = packed[:, 0:64]
    grad_first[512:1024] = packed[:, 64:128]
    other = total[1].astype(jnp.float32).reshape(512, 128)
    for k in range(16):
        lanes = 64 * (k // 8)
        start = (k % 8) * 16
        grad_second[k // 4, :, k % 4, :] = other[start : start + 12, lanes : lanes + 64]
    for part in range(6):
        grad_proj[:, part * 128 : part * 128 + 128] = other[128 + part * 64 : 192 + part * 64]
    mask_row = other[12:13, 0:64] + other[13:14, 0:64]
    grad_mask[...] = jnp.dot(
        jnp.broadcast_to(mask_row, (8, 64)),
        proj_t[...].astype(jnp.float32),
        precision=lax.Precision.HIGHEST,
        preferred_element_type=jnp.float32,
    )[0:1].reshape(768)


def finish(total, rows_in, proj_t):
    vmem = pl.BlockSpec(memory_space=pltpu.VMEM)
    return pl.pallas_call(
        finish_kernel,
        out_shape=(
            jax.ShapeDtypeStruct((192, 768), jnp.bfloat16),
            jax.ShapeDtypeStruct((64, 768), jnp.float32),
            jax.ShapeDtypeStruct((1024, 64), jnp.float32),
            jax.ShapeDtypeStruct((4, 12, 4, 64), jnp.float32),
            jax.ShapeDtypeStruct((768,), jnp.float32),
        ),
        in_specs=[vmem] * 3,
        out_specs=(vmem,) * 5,
        name="finish",
    )(total, rows_in, proj_t)


def per_device(
    tokens,
    vis_index,
    counts,
    owners,
    mask_token,
    proj_weight,
    up_first,
    up_second,
    saved_pre,
    cotangent,
):
    wide, narrow, fine, edge, cols, order = tap_select()
    proj_t = proj_weight.T
    total, rows_in = main(
        counts.reshape(2),
        vis_index.reshape(2, 64),
        owners.reshape(2, 1, 64),
        [
            tokens.reshape(128, 768),
            mask_token,
            proj_t,
            up_first.reshape(1024, 64),
            up_second.transpose(0, 2, 1, 3),
            cotangent,
            saved_pre,
            wide,
            narrow,
            fine,
            edge,
            cols,
            order,
        ],
    )
    token_grad, grad_proj, grad_first, grad_second, grad_mask = finish(total, rows_in, proj_t)
    return (
        token_grad[None, None],
        grad_proj.T,
        grad_first.reshape(4, 4, 64, 64),
        grad_second.transpose(0, 2, 1, 3),
        grad_mask,
    )


def solution(mesh):
    return jax.shard_map(
        per_device,
        mesh=mesh,
        in_specs=(
            P("ns", "ew", None, None, None),
            P("ns", "ew", None, None),
            P("ns", "ew", None),
            P("ns", "ew", None, None, None),
            P(),
            P(),
            P(),
            P(),
            P(None, None, "ns", "ew"),
            P(None, None, "ns", "ew"),
        ),
        out_specs=(P("ns", "ew", None, None), P(), P(), P(), P()),
        check_vma=False,
    )
```

time: 745 us -> 68.8 us (0.09)
  waiting for transfers between devices: 373 us -> 0 us
  blocking collectives: 143 us -> 0 us
  local copies, waits for them, and re-layouts: 142 us -> 0 us
  Pallas kernels: 0 us -> 68 us
  starting transfers between devices: 39.1 us -> 0 us
  matrix products: 24.1 us -> 0 us
  between operations: 15.2 us -> 0.64 us
    psum x1 -> x0, waiting for transfers between devices: 366 us -> none  [per_device(): lax.psum((grad_proj, grad_first, grad_second, mask_sum), ('ew', 'ns'))]
    psum x1 -> x0, blocking collectives: 143 us -> none  [per_device(): lax.psum((grad_proj, grad_first, grad_second, mask_sum), ('ew', 'ns'))]
    slice x37 -> x0, local copies, waits for them, and re-layouts: 129 us -> none  [the longest x32 128 us: transpose_back(): padded[:, :, tap_y:tap_y + 2 * height:2, tap_x:tap_x + 2 * breadth:2]]
    pallas_call x0 -> x2, Pallas kernels: none -> 68 us  [the longest x1 65.7 us: main(): pl.pallas_call(main_kernel, out_shape=(jax.ShapeDtypeStruct((STREAMS, GRO...]
    ppermute x8 -> x0, starting transfers between devices: 26.4 us -> none  [the longest x4 14.2 us: padded_2(): lax.ppermute(lax.slice_in_dim(block, block.shape[dim] - width, None, axis...]
    dot_general x71 -> x0, matrix products: 24.1 us -> none  [the longest x32 15.2 us: transpose_back(): jnp.einsum('oi,fohw->fihw', kernel[tap_y, tap_x], window, preferred_eleme...]
    all_to_all x1 -> x0, starting transfers between devices: 12.7 us -> none  [per_device(): lax.all_to_all(outgoing.reshape(owner_count, capacity, features), 'ns', s...]
    unnamed x103 -> x0, local copies, waits for them, and re-layouts: 9.44 us -> none
  transfers between devices with their start and end apart: 10 -> 0, of which waited for: 3 -> 0; matrix products, arithmetic and copies ran while one was open for 3% -> 0% of each run, Pallas kernels for 0% -> 0%
where the time goes in v3:
time: 68.8 us; the launch traced here: 68.6 us
  Pallas kernels  68 us (99%)
    pallas_call x1, Pallas kernels, main(): pl.pallas_call(main_kernel, out_shape=(jax.ShapeDtypeStruct((STREAMS, GRO...  65.7 us
    pallas_call x1, Pallas kernels, finish(): pl.pallas_call(finish_kernel, out_shape=(jax.ShapeDtypeStruct((192, 768),...  2.33 us

profile of v3, /device:TPU:1, one launch (start us, length us, event | category | flops | bytes accessed | tf_op | source)
XLA Modules:
  0.0 68.6 jit_solution(3880030062799291074)
XLA Ops:
  0.6 65.7 %main.1 = (bf16[2,8,8,8,128]{4,3,2,1,0:T(8,128)(2,1)}, bf16[8,16,128]{2,1,0:T(8,128)(2,1)}) custom-call(s32[2]{0:T(128)} %bitcast.20, s32[2,64]{1,0:T(2,128)} %bitcast.18, s32[2,1,64]{2,1,0:T(1,128)} %bitcast.19, bf16[128,768]{1,0:T(8,128)(2,1)} %bitcast.16, bf16[768]{0:T(1024)(128)(2,1)} %mask_token.1, bf16[64,768]{1,0:T(8,128)(2,1)} %bitcast.13, ...), custom_call_target="tpu_custom_call" | custom-call | tf_op jit(solution)/shard_map/main/pallas_call | solution.py:511
  66.3 2.3 %finish.1 = (bf16[192,768]{1,0:T(8,128)(2,1)}, f32[64,768]{1,0:T(8,128)}, f32[1024,64]{1,0:T(8,128)}, f32[4,12,4,64]{3,2,1,0:T(4,128)}, f32[768]{0:T(1024)}) custom-call(bf16[2,8,8,8,128]{4,3,2,1,0:T(8,128)(2,1)} %get-tuple-element.12.total, bf16[8,16,128]{2,1,0:T(8,128)(2,1)} %get-tuple-element.13.rows_in, bf16[64,768]{1,0:T(8,128)(2,1)} %bitcast.14), custom_call_target="tpu_custom_call" | custom-call | tf_op jit(solution)/shard_map/finish/pallas_call | solution.py:589

commit v4 on v3

--- a/solution.py
+++ b/solution.py
@@ -79,65 +79,48 @@
 Z_COUNT = Z_LOW * Z_HIGH
 
 
-def main_kernel(
-    live_counts,
-    index,
-    owners,
-    tokens,
-    mask_token,
-    proj_t,
-    first,
-    second,
-    cot,
-    pre,
-    wide,
-    narrow,
-    fine,
-    edge,
-    cols,
-    order,
-    total_out,
-    rows_in,
-    wide_c,
-    wide_p,
+def fetch_all(pairs, sem):
+    copies = []
+    for k, (src, dst) in enumerate(pairs):
+        copy = pltpu.make_async_copy(src, dst, sem.at[k])
+        copy.start()
+        copies.append(copy)
+    return copies
+
+
+def wait_all(copies):
+    for copy in copies:
+        copy.wait()
+
+
+def halo_kernel(
+    cot_in,
+    pre_in,
+    cols_in,
+    edge_in,
     cot_rows,
-    cot_cols,
     pre_rows,
-    pre_cols,
     rows_c,
     rows_p,
     cols_c,
     cols_p,
-    taps,
-    windows,
-    hidden,
-    deltas,
-    taps_fine,
-    windows_fine,
-    payload,
-    buf_a,
-    red_a,
-    buf_b,
-    buf_c,
-    buf_d,
-    rows_out,
-    tok_z,
-    tok_s,
-    buf_s,
+    cot,
+    pre,
+    cols,
+    edge,
+    wide_c,
+    wide_p,
+    cot_cols,
+    pre_cols,
     send,
     recv,
-    local_sem,
+    fetch,
 ):
     half = jnp.bfloat16
     n = lax.axis_index("ns")
     e = lax.axis_index("ew")
     n_count = lax.axis_size("ns")
     e_count = lax.axis_size("ew")
-    g = lax.rem(n, GROUP_A)
-    zl = lax.div(n, GROUP_A)
-    zh = lax.div(e, GROUP_Y)
-    y = lax.rem(e, GROUP_Y)
-    zi = zh * Z_LOW + zl
 
     def peer_side(side):
         return {
@@ -145,31 +128,10 @@
             "ns": lax.rem(n + side[0] + n_count, n_count),
         }
 
-    def peer_a(k):
-        other = lax.rem(g + k, GROUP_A)
-        return other, {"ew": e, "ns": zl * GROUP_A + other}
-
-    def peer_b(k):
-        other = lax.rem(y + k, GROUP_Y)
-        return other, {"ew": zh * GROUP_Y + other, "ns": n}
-
-    def peer_c(k):
-        other = lax.rem(zi + k, Z_COUNT)
-        return other, {
-            "ew": lax.div(other, Z_LOW) * GROUP_Y + y,
-            "ns": lax.rem(other, Z_LOW) * GROUP_A + g,
-        }
-
-    def peer_z(k):
-        other = lax.rem(zl + k, Z_LOW)
-        return other, {"ew": e, "ns": other * GROUP_A + g}
-
     barrier = pltpu.get_barrier_semaphore()
     for side in SIDES:
         pl.semaphore_signal(barrier, inc=1, device_id=peer_side(side), device_id_type=MESH)
-    for count, peer in ((GROUP_A, peer_a), (GROUP_Y, peer_b), (Z_COUNT, peer_c)):
-        for k in range(1, count):
-            pl.semaphore_signal(barrier, inc=1, device_id=peer(k)[1], device_id_type=MESH)
+    fetched = fetch_all(((cot_in, cot), (cols_in, cols), (pre_in, pre), (edge_in, edge)), fetch)
 
     used = [0]
 
@@ -187,10 +149,7 @@
         copy.start()
         return copy
 
-    def wait_all(copies):
-        for copy in copies:
-            copy.wait()
-
+    wait_all(fetched)
     for f in range(2):
         for o in range(12):
             for part in range(2):
@@ -217,7 +176,7 @@
             packed = packed + dot_nn(slab, edge[pl.ds((f * 8 + i) * 128, 128), :])
     pre_cols[...] = packed.astype(half)
 
-    pl.semaphore_wait(barrier, len(SIDES) + GROUP_A + GROUP_Y + Z_COUNT - 3)
+    pl.semaphore_wait(barrier, len(SIDES))
 
     halo = []
     halo.append(put(cot_cols, cols_c.at[1], peer_side((0, -1))))
@@ -236,6 +195,144 @@
     halo.append(put(cot_rows.at[:, 13:16], rows_c.at[0], peer_side((1, 0))))
     halo.append(put(pre_rows.at[:, 0], rows_p.at[1], peer_side((-1, 0))))
     halo.append(put(pre_rows.at[:, 7], rows_p.at[0], peer_side((1, 0))))
+
+    wait_all(halo)
+
+
+def halo(cotangent, saved_pre, cols, edge):
+    vmem = pl.BlockSpec(memory_space=pltpu.VMEM)
+    hbm = pl.BlockSpec(memory_space=pl.ANY)
+    half = jnp.bfloat16
+    wide = jnp.float32
+    dma = pltpu.SemaphoreType.DMA
+    return pl.pallas_call(
+        halo_kernel,
+        out_shape=(
+            jax.ShapeDtypeStruct((2, 16, 16, 256), half),
+            jax.ShapeDtypeStruct((2, 8, 64, 128), half),
+            jax.ShapeDtypeStruct((2, 2, 3, 16, 256), half),
+            jax.ShapeDtypeStruct((2, 2, 64, 128), half),
+            jax.ShapeDtypeStruct((6, 2, 2, 16, 128), half),
+            jax.ShapeDtypeStruct((6, 64, 128), half),
+        ),
+        in_specs=[hbm] * 4,
+        out_specs=(vmem,) * 6,
+        scratch_shapes=[pltpu.VMEM(x.shape, x.dtype) for x in (cotangent, saved_pre, cols, edge)]
+        + [
+            pltpu.VMEM((2, 512, 128), wide),
+            pltpu.VMEM((1024, 128), wide),
+            pltpu.VMEM((2, 2, 16, 128), half),
+            pltpu.VMEM((64, 128), half),
+            dma((16,)),
+            dma((16,)),
+            dma((4,)),
+        ],
+        compiler_params=pltpu.CompilerParams(collective_id=1, has_side_effects=True),
+        name="halo",
+    )(cotangent, saved_pre, cols, edge)
+
+
+OPERANDS = tuple(range(17))
+
+
+def main_kernel(live_counts, *refs):
+    sources = refs[: len(OPERANDS)]
+    (total_out, rows_in) = refs[len(OPERANDS) : len(OPERANDS) + 2]
+    held = refs[len(OPERANDS) + 2 : 2 * len(OPERANDS) + 2]
+    (
+        index,
+        owners,
+        tokens,
+        mask_token,
+        proj_t,
+        first,
+        second,
+        wide,
+        narrow,
+        fine,
+        order,
+        cot_rows,
+        pre_rows,
+        rows_c,
+        rows_p,
+        cols_c,
+        cols_p,
+    ) = held
+    (
+        taps,
+        windows,
+        hidden,
+        deltas,
+        taps_fine,
+        windows_fine,
+        payload,
+        buf_a,
+        red_a,
+        buf_b,
+        buf_c,
+        buf_d,
+        rows_out,
+        tok_z,
+        tok_s,
+        buf_s,
+        send,
+        recv,
+        local_sem,
+        fetch,
+    ) = refs[2 * len(OPERANDS) + 2 :]
+    half = jnp.bfloat16
+    n = lax.axis_index("ns")
+    e = lax.axis_index("ew")
+    n_count = lax.axis_size("ns")
+    e_count = lax.axis_size("ew")
+    g = lax.rem(n, GROUP_A)
+    zl = lax.div(n, GROUP_A)
+    zh = lax.div(e, GROUP_Y)
+    y = lax.rem(e, GROUP_Y)
+    zi = zh * Z_LOW + zl
+
+    def peer_a(k):
+        other = lax.rem(g + k, GROUP_A)
+        return other, {"ew": e, "ns": zl * GROUP_A + other}
+
+    def peer_b(k):
+        other = lax.rem(y + k, GROUP_Y)
+        return other, {"ew": zh * GROUP_Y + other, "ns": n}
+
+    def peer_c(k):
+        other = lax.rem(zi + k, Z_COUNT)
+        return other, {
+            "ew": lax.div(other, Z_LOW) * GROUP_Y + y,
+            "ns": lax.rem(other, Z_LOW) * GROUP_A + g,
+        }
+
+    def peer_z(k):
+        other = lax.rem(zl + k, Z_LOW)
+        return other, {"ew": e, "ns": other * GROUP_A + g}
+
+    barrier = pltpu.get_barrier_semaphore()
+    for count, peer in ((GROUP_A, peer_a), (GROUP_Y, peer_b), (Z_COUNT, peer_c)):
+        for k in range(1, count):
+            pl.semaphore_signal(barrier, inc=1, device_id=peer(k)[1], device_id_type=MESH)
+
+    fetched = fetch_all(tuple(zip(sources, held)), fetch)
+    used = [0]
+
+    def put(src, dst, target):
+        slot = used[0]
+        used[0] += 1
+        copy = pltpu.make_async_remote_copy(
+            src_ref=src,
+            dst_ref=dst,
+            send_sem=send.at[slot],
+            recv_sem=recv.at[slot],
+            device_id=target,
+            device_id_type=MESH,
+        )
+        copy.start()
+        return copy
+
+    wait_all(fetched)
 
     token_t = dot_nt(proj_t[...], tokens[...]).astype(half)
     mask_row = mask_token[...].astype(jnp.float32).reshape(1, 768)
@@ -275,8 +372,6 @@
     number = lax.broadcasted_iota(jnp.int32, (96, 128), 0).astype(jnp.float32) * 2.0
     even = jnp.where(number == target, 1.0, 0.0).astype(half)
     odd = jnp.where(number + 1.0 == target, 1.0, 0.0).astype(half)
-
-    wait_all(halo)
 
     north = n > 0
     south = n < n_count - 1
@@ -386,7 +481,8 @@
     grad_first = grad_first + dot_nt(
         windows_fine[512:1024], jnp.concatenate([zeros_fine, first_grid], axis=0)
     )
-    payload[0] = grad_first.reshape(GROUP_A, GROUP_Y, 8, 128)
+    payload[0] = grad_first.astype(half).reshape(GROUP_A, GROUP_Y, 8, 128)
+    pl.semaphore_wait(barrier, GROUP_A + GROUP_Y + Z_COUNT - 3)
 
     def scatter_a(s):
         copies = []
@@ -420,20 +516,25 @@
     mask_sum = jnp.sum(grid.astype(jnp.float32) * unseen[0:1, :], axis=1, keepdims=True)
     mask_sum_row = dot_nt(unseen.astype(half), jnp.concatenate([grid, zeros_fine], axis=0))
     grad_proj = dot_nn(chosen, tokens[...]) + mask_sum * mask_row
+    mask_sum_row = mask_sum_row[0:1, :]
+    mask_rest = mask_sum_row - mask_sum_row.astype(half).astype(jnp.float32)
     grad_second = jnp.where(
-        (row_second == 12) & (lane_second < 64), mask_sum_row[0:1, :], grad_second
-    )
-    payload[1, 0:2] = grad_second.reshape(2, GROUP_Y, 8, 128)
+        (row_second == 12) & (lane_second < 64),
+        mask_sum_row,
+        jnp.where((row_second == 13) & (lane_second < 64), mask_rest, grad_second),
+    )
+    payload[1, 0:2] = grad_second.astype(half).reshape(2, GROUP_Y, 8, 128)
     for part in range(6):
-        payload[1, 2 + part] = grad_proj[:, part * 128 : part * 128 + 128].reshape(GROUP_Y, 8, 128)
+        block = grad_proj[:, part * 128 : part * 128 + 128].astype(half)
+        payload[1, 2 + part] = block.reshape(GROUP_Y, 8, 128)
     copies_a.append(scatter_a(1))
 
     copies_b = []
     for s in range(STREAMS):
         wait_all(copies_a[s])
-        summed = payload[s, g]
+        summed = payload[s, g].astype(jnp.float32)
         for k in range(1, GROUP_A):
-            summed = summed + buf_a[s, k - 1]
+            summed = summed + buf_a[s, k - 1].astype(jnp.float32)
         red_a[s] = summed
         copies = []
         for k in range(1, GROUP_Y):
@@ -474,10 +575,11 @@
         for k in range(1, Z_COUNT):
             summed = summed + buf_c[s, k]
         if s == 1:
-            rounded = summed.astype(half).astype(jnp.float32)
-            rest = jnp.broadcast_to((summed - rounded)[4:5], (8, 128))
-            here = jnp.where((g == 0) & (y == 1), 5, -1)
-            summed = jnp.where(row_8 == here, rest, summed)
+            mask_total = summed[4:5] + summed[5:6]
+            rest = mask_total - mask_total.astype(half).astype(jnp.float32)
+            here = jnp.where((g == 0) & (y == 1), 4, -2)
+            summed = jnp.where(row_8 == here, mask_total, summed)
+            summed = jnp.where(row_8 == here + 1, rest, summed)
         buf_d[s, y] = summed.astype(half)
         copies = []
         for k in range(1, GROUP_Y):
@@ -499,12 +601,13 @@
     wait_all(copies_e)
 
 
-COPIES = 16 + 2 * (2 * (GROUP_A - 1) + 2 * (GROUP_Y - 1) + Z_COUNT - 1) + Z_LOW - 1 + GROUP_A - 1
-
-
-def main(counts, index, owners, arrays):
+COPIES = 2 * (2 * (GROUP_A - 1) + 2 * (GROUP_Y - 1) + Z_COUNT - 1) + Z_LOW - 1 + GROUP_A - 1
+
+
+def main(counts, arrays):
     vmem = pl.BlockSpec(memory_space=pltpu.VMEM)
     smem = pl.BlockSpec(memory_space=pltpu.SMEM)
+    hbm = pl.BlockSpec(memory_space=pl.ANY)
     half = jnp.bfloat16
     wide = jnp.float32
     dma = pltpu.SemaphoreType.DMA
@@ -514,27 +617,18 @@
             jax.ShapeDtypeStruct((STREAMS, GROUP_A, GROUP_Y, 8, 128), half),
             jax.ShapeDtypeStruct((GROUP_A, 16, 128), half),
         ),
-        in_specs=[smem] + [vmem] * (2 + len(arrays)),
-        out_specs=(pl.BlockSpec(memory_space=pl.ANY), vmem),
-        scratch_shapes=[
-            pltpu.VMEM((2, 512, 128), wide),
-            pltpu.VMEM((1024, 128), wide),
-            pltpu.VMEM((2, 16, 16, 256), half),
-            pltpu.VMEM((2, 2, 16, 128), half),
-            pltpu.VMEM((2, 8, 64, 128), half),
-            pltpu.VMEM((64, 128), half),
-            pltpu.VMEM((2, 2, 3, 16, 256), half),
-            pltpu.VMEM((2, 2, 64, 128), half),
-            pltpu.VMEM((6, 2, 2, 16, 128), half),
-            pltpu.VMEM((6, 64, 128), half),
+        in_specs=[smem] + [hbm] * len(arrays),
+        out_specs=(hbm, vmem),
+        scratch_shapes=[pltpu.VMEM(x.shape, x.dtype) for x in arrays]
+        + [
             pltpu.VMEM((2, 22, 16, 1024), half),
             pltpu.VMEM((256, 2048), half),
             pltpu.VMEM((64, 2048), half),
             pltpu.VMEM((2, 10, 64, 256), half),
             pltpu.VMEM((2, 10, 64, 512), half),
             pltpu.VMEM((1024, 512), half),
-            pltpu.VMEM((STREAMS, GROUP_A, GROUP_Y, 8, 128), wide),
-            pltpu.VMEM((STREAMS, GROUP_A - 1, GROUP_Y, 8, 128), wide),
+            pltpu.VMEM((STREAMS, GROUP_A, GROUP_Y, 8, 128), half),
+            pltpu.VMEM((STREAMS, GROUP_A - 1, GROUP_Y, 8, 128), half),
             pltpu.VMEM((STREAMS, GROUP_Y, 8, 128), wide),
             pltpu.VMEM((STREAMS, GROUP_Y - 1, 8, 128), wide),
             pltpu.VMEM((STREAMS, Z_COUNT, 8, 128), wide),
@@ -546,10 +640,11 @@
             dma((COPIES,)),
             dma((COPIES,)),
             dma((STREAMS,)),
+            dma((len(arrays),)),
         ],
         compiler_params=pltpu.CompilerParams(collective_id=0, has_side_effects=True),
         name="main",
-    )(counts, index, owners, *arrays)
+    )(counts, *arrays)
 
 
 def finish_kernel(
@@ -615,24 +710,22 @@
 ):
     wide, narrow, fine, edge, cols, order = tap_select()
     proj_t = proj_weight.T
+    parts = halo(cotangent, saved_pre, cols, edge)
     total, rows_in = main(
         counts.reshape(2),
-        vis_index.reshape(2, 64),
-        owners.reshape(2, 1, 64),
         [
+            vis_index.reshape(2, 64),
+            owners.reshape(2, 1, 64),
             tokens.reshape(128, 768),
             mask_token,
             proj_t,
             up_first.reshape(1024, 64),
             up_second.transpose(0, 2, 1, 3),
-            cotangent,
-            saved_pre,
             wide,
             narrow,
             fine,
-            edge,
-            cols,
             order,
+            *parts,
         ],
     )
     token_grad, grad_proj, grad_first, grad_second, grad_mask = finish(total, rows_in, proj_t)

time: 68.8 us -> 70.3 us (1.022)
  Pallas kernels: 68 us -> 69.4 us
    pallas_call x0 -> x1, Pallas kernels: none -> 31.4 us  [halo(): pl.pallas_call(halo_kernel, out_shape=(jax.ShapeDtypeStruct((2, 16, 16, 2...]
    pallas_call x1, Pallas kernels: 65.7 us -> 35.6 us  [main(): pl.pallas_call(main_kernel, out_shape=(jax.ShapeDtypeStruct((STREAMS, GRO...]
where the time goes in v4:
time: 70.3 us; the launch traced here: 70.1 us
  Pallas kernels  69.4 us (99%)
    pallas_call x1, Pallas kernels, main(): pl.pallas_call(main_kernel, out_shape=(jax.ShapeDtypeStruct((STREAMS, GRO...  35.6 us
    pallas_call x1, Pallas kernels, halo(): pl.pallas_call(halo_kernel, out_shape=(jax.ShapeDtypeStruct((2, 16, 16, 2...  31.4 us
    pallas_call x1, Pallas kernels, finish(): pl.pallas_call(finish_kernel, out_shape=(jax.ShapeDtypeStruct((192, 768),...  2.33 us

profile of v4, /device:TPU:1, one launch (start us, length us, event | category | flops | bytes accessed | tf_op | source)
XLA Modules:
  0.0 70.1 jit_solution(18050547305746109013)
XLA Ops:
  0.6 31.4 %halo.1 = (bf16[2,16,16,256]{3,2,1,0:T(8,128)(2,1)}, bf16[2,8,64,128]{3,2,1,0:T(8,128)(2,1)}, bf16[2,2,3,16,256]{4,3,2,1,0:T(8,128)(2,1)}, bf16[2,2,64,128]{3,2,...) custom-call(bf16[2,12,16,256]{3,2,1,0:T(8,128)(2,1)} %cot_in.1, ...), custom_call_target="tpu_custom_call" | custom-call | tf_op jit(solution)/shard_map/halo/pallas_call | solution.py:208
  32.1 35.6 %main.1 = (bf16[2,8,8,8,128]{4,3,2,1,0:T(8,128)(2,1)}, bf16[8,16,128]{2,1,0:T(8,128)(2,1)}) custom-call(s32[2]{0:T(128)} %bitcast.20, s32[2,64]{1,0:T(2,128)} %bitcast.18, s32[2,1,64]{2,1,0:T(1,128)} %bitcast.19, bf16[128,768]{1,0:T(8,128)(2,1)} %bitcast.16, bf16[768]{0:T(1024)(128)(2,1)} %refs_3_.1, bf16[64,768]{1,0:T(8,128)(2,1)} %bitcast.13, ...), custom_call_target="tpu_custom_call" | custom-call | tf_op jit(solution)/shard_map/main/pallas_call | solution.py:614
  67.7 2.3 %finish.1 = (bf16[192,768]{1,0:T(8,128)(2,1)}, f32[64,768]{1,0:T(8,128)}, f32[1024,64]{1,0:T(8,128)}, f32[4,12,4,64]{3,2,1,0:T(4,128)}, f32[768]{0:T(1024)}) custom-call(bf16[2,8,8,8,128]{4,3,2,1,0:T(8,128)(2,1)} %get-tuple-element.24.total, bf16[8,16,128]{2,1,0:T(8,128)(2,1)} %get-tuple-element.25.rows_in, bf16[64,768]{1,0:T(8,128)(2,1)} %bitcast.14), custom_call_target="tpu_custom_call" | custom-call | tf_op jit(solution)/shard_map/finish/pallas_call | solution.py:684

commit v5 on v3

--- a/solution.py
+++ b/solution.py
@@ -79,55 +79,81 @@
 Z_COUNT = Z_LOW * Z_HIGH
 
 
-def main_kernel(
-    live_counts,
-    index,
-    owners,
-    tokens,
-    mask_token,
-    proj_t,
-    first,
-    second,
-    cot,
-    pre,
-    wide,
-    narrow,
-    fine,
-    edge,
-    cols,
-    order,
-    total_out,
-    rows_in,
-    wide_c,
-    wide_p,
-    cot_rows,
-    cot_cols,
-    pre_rows,
-    pre_cols,
-    rows_c,
-    rows_p,
-    cols_c,
-    cols_p,
-    taps,
-    windows,
-    hidden,
-    deltas,
-    taps_fine,
-    windows_fine,
-    payload,
-    buf_a,
-    red_a,
-    buf_b,
-    buf_c,
-    buf_d,
-    rows_out,
-    tok_z,
-    tok_s,
-    buf_s,
-    send,
-    recv,
-    local_sem,
-):
+def fetch_all(pairs, sem, first):
+    copies = []
+    for k, (src, dst) in enumerate(pairs):
+        copy = pltpu.make_async_copy(src, dst, sem.at[first + k])
+        copy.start()
+        copies.append(copy)
+    return copies
+
+
+def wait_all(copies):
+    for copy in copies:
+        copy.wait()
+
+
+EARLY = 4
+MAIN_VMEM = 24 * 1024 * 1024
+FINISH_VMEM = 8 * 1024 * 1024
+OPERANDS = tuple(range(16))
+
+
+def main_kernel(*refs):
+    sources = refs[: len(OPERANDS)]
+    (total_out, rows_in) = refs[len(OPERANDS) : len(OPERANDS) + 2]
+    held = refs[len(OPERANDS) + 2 : 2 * len(OPERANDS) + 2]
+    (
+        cot,
+        cols,
+        pre,
+        edge,
+        live_counts,
+        index,
+        owners,
+        tokens,
+        mask_token,
+        proj_t,
+        first,
+        second,
+        wide,
+        narrow,
+        fine,
+        order,
+    ) = held
+    (
+        wide_c,
+        wide_p,
+        cot_rows,
+        cot_cols,
+        pre_rows,
+        pre_cols,
+        rows_c,
+        rows_p,
+        cols_c,
+        cols_p,
+        slopes,
+        taps,
+        windows,
+        hidden,
+        deltas,
+        taps_fine,
+        windows_fine,
+        payload,
+        buf_a,
+        red_a,
+        buf_b,
+        buf_c,
+        buf_d,
+        rows_out,
+        tok_z,
+        tok_s,
+        buf_s,
+        send,
+        recv,
+        local_sem,
+        fetch,
+    ) = refs[2 * len(OPERANDS) + 2 :]
     half = jnp.bfloat16
     n = lax.axis_index("ns")
     e = lax.axis_index("ew")
@@ -164,6 +190,8 @@
         other = lax.rem(zl + k, Z_LOW)
         return other, {"ew": e, "ns": other * GROUP_A + g}
 
+    pairs = tuple(zip(sources, held))
+    early = fetch_all(pairs[:EARLY], fetch, 0)
     barrier = pltpu.get_barrier_semaphore()
     for side in SIDES:
         pl.semaphore_signal(barrier, inc=1, device_id=peer_side(side), device_id_type=MESH)
@@ -171,6 +199,7 @@
         for k in range(1, count):
             pl.semaphore_signal(barrier, inc=1, device_id=peer(k)[1], device_id_type=MESH)
 
+    later = fetch_all(pairs[EARLY:], fetch, EARLY)
     used = [0]
 
     def put(src, dst, target):
@@ -187,10 +216,7 @@
         copy.start()
         return copy
 
-    def wait_all(copies):
-        for copy in copies:
-            copy.wait()
-
+    wait_all(early)
     for f in range(2):
         for o in range(12):
             for part in range(2):
@@ -237,6 +263,15 @@
     halo.append(put(pre_rows.at[:, 0], rows_p.at[1], peer_side((-1, 0))))
     halo.append(put(pre_rows.at[:, 7], rows_p.at[0], peer_side((1, 0))))
 
+    wait_all(later)
+
+    for f in range(2):
+        for i in range(8):
+            center = wide_p[pl.ds(f * 512 + i, 64, stride=8), :]
+            sigmoid = jax.nn.sigmoid(1.702 * center)
+            slopes[f, i] = sigmoid + 1.702 * center * sigmoid * (1.0 - sigmoid)
+            hidden[:, (f * 8 + i) * 128 : (f * 8 + i + 1) * 128] = (center * sigmoid).astype(half)
+
     token_t = dot_nt(proj_t[...], tokens[...]).astype(half)
     mask_row = mask_token[...].astype(jnp.float32).reshape(1, 768)
     mask_t = dot_nt(proj_t[...], jnp.broadcast_to(mask_row, (8, 768)).astype(half)).astype(half)
@@ -339,19 +374,14 @@
                 axis=0,
             )
             grad = dot_nn(second_t, window)
-            if i == 0:
-                center = rows_p[0, f]
-            elif i == 9:
-                center = rows_p[1, f]
+            if 0 < i < 9:
+                windows[:, (f * 8 + i - 1) * 128 : (f * 8 + i) * 128] = window[:, :128]
+                slope = slopes[f, i - 1]
             else:
-                center = pre_rows[f, i - 1]
-                windows[:, (f * 8 + i - 1) * 128 : (f * 8 + i) * 128] = window[:, :128]
-            center = center.astype(jnp.float32)
-            sigmoid = jax.nn.sigmoid(1.702 * center)
-            slope = sigmoid + 1.702 * center * sigmoid * (1.0 - sigmoid)
+                center = rows_p[i // 9, f].astype(jnp.float32)
+                sigmoid = jax.nn.sigmoid(1.702 * center)
+                slope = sigmoid + 1.702 * center * sigmoid * (1.0 - sigmoid)
             value = grad[:, :128] * slope
-            if 0 < i < 9:
-                hidden[:, (f * 8 + i - 1) * 128 : (f * 8 + i) * 128] = (center * sigmoid).astype(half)
             edge_slope = halo_slope
             if f + i > 0:
                 edge_slope = pltpu.roll(halo_slope, 128 - 2 * (f * 10 + i), 1)
@@ -386,7 +416,7 @@
     grad_first = grad_first + dot_nt(
         windows_fine[512:1024], jnp.concatenate([zeros_fine, first_grid], axis=0)
     )
-    payload[0] = grad_first.reshape(GROUP_A, GROUP_Y, 8, 128)
+    payload[0] = grad_first.astype(half).reshape(GROUP_A, GROUP_Y, 8, 128)
 
     def scatter_a(s):
         copies = []
@@ -420,20 +450,25 @@
     mask_sum = jnp.sum(grid.astype(jnp.float32) * unseen[0:1, :], axis=1, keepdims=True)
     mask_sum_row = dot_nt(unseen.astype(half), jnp.concatenate([grid, zeros_fine], axis=0))
     grad_proj = dot_nn(chosen, tokens[...]) + mask_sum * mask_row
+    mask_sum_row = mask_sum_row[0:1, :]
+    mask_rest = mask_sum_row - mask_sum_row.astype(half).astype(jnp.float32)
     grad_second = jnp.where(
-        (row_second == 12) & (lane_second < 64), mask_sum_row[0:1, :], grad_second
-    )
-    payload[1, 0:2] = grad_second.reshape(2, GROUP_Y, 8, 128)
+        (row_second == 12) & (lane_second < 64),
+        mask_sum_row,
+        jnp.where((row_second == 13) & (lane_second < 64), mask_rest, grad_second),
+    )
+    payload[1, 0:2] = grad_second.astype(half).reshape(2, GROUP_Y, 8, 128)
     for part in range(6):
-        payload[1, 2 + part] = grad_proj[:, part * 128 : part * 128 + 128].reshape(GROUP_Y, 8, 128)
+        block = grad_proj[:, part * 128 : part * 128 + 128].astype(half)
+        payload[1, 2 + part] = block.reshape(GROUP_Y, 8, 128)
     copies_a.append(scatter_a(1))
 
     copies_b = []
     for s in range(STREAMS):
         wait_all(copies_a[s])
-        summed = payload[s, g]
+        summed = payload[s, g].astype(jnp.float32)
         for k in range(1, GROUP_A):
-            summed = summed + buf_a[s, k - 1]
+            summed = summed + buf_a[s, k - 1].astype(jnp.float32)
         red_a[s] = summed
         copies = []
         for k in range(1, GROUP_Y):
@@ -474,10 +509,11 @@
         for k in range(1, Z_COUNT):
             summed = summed + buf_c[s, k]
         if s == 1:
-            rounded = summed.astype(half).astype(jnp.float32)
-            rest = jnp.broadcast_to((summed - rounded)[4:5], (8, 128))
-            here = jnp.where((g == 0) & (y == 1), 5, -1)
-            summed = jnp.where(row_8 == here, rest, summed)
+            mask_total = summed[4:5] + summed[5:6]
+            rest = mask_total - mask_total.astype(half).astype(jnp.float32)
+            here = jnp.where((g == 0) & (y == 1), 4, -2)
+            summed = jnp.where(row_8 == here, mask_total, summed)
+            summed = jnp.where(row_8 == here + 1, rest, summed)
         buf_d[s, y] = summed.astype(half)
         copies = []
         for k in range(1, GROUP_Y):
@@ -502,9 +538,9 @@
 COPIES = 16 + 2 * (2 * (GROUP_A - 1) + 2 * (GROUP_Y - 1) + Z_COUNT - 1) + Z_LOW - 1 + GROUP_A - 1
 
 
-def main(counts, index, owners, arrays):
+def main(arrays):
     vmem = pl.BlockSpec(memory_space=pltpu.VMEM)
-    smem = pl.BlockSpec(memory_space=pltpu.SMEM)
+    hbm = pl.BlockSpec(memory_space=pl.ANY)
     half = jnp.bfloat16
     wide = jnp.float32
     dma = pltpu.SemaphoreType.DMA
@@ -514,9 +550,13 @@
             jax.ShapeDtypeStruct((STREAMS, GROUP_A, GROUP_Y, 8, 128), half),
             jax.ShapeDtypeStruct((GROUP_A, 16, 128), half),
         ),
-        in_specs=[smem] + [vmem] * (2 + len(arrays)),
-        out_specs=(pl.BlockSpec(memory_space=pl.ANY), vmem),
+        in_specs=[pl.BlockSpec(memory_space=pltpu.HBM)] * len(arrays),
+        out_specs=(hbm, vmem),
         scratch_shapes=[
+            (pltpu.SMEM if x.ndim == 1 and x.dtype == jnp.int32 else pltpu.VMEM)(x.shape, x.dtype)
+            for x in arrays
+        ]
+        + [
             pltpu.VMEM((2, 512, 128), wide),
             pltpu.VMEM((1024, 128), wide),
             pltpu.VMEM((2, 16, 16, 256), half),
@@ -527,14 +567,15 @@
             pltpu.VMEM((2, 2, 64, 128), half),
             pltpu.VMEM((6, 2, 2, 16, 128), half),
             pltpu.VMEM((6, 64, 128), half),
+            pltpu.VMEM((2, 8, 64, 128), wide),
             pltpu.VMEM((2, 22, 16, 1024), half),
             pltpu.VMEM((256, 2048), half),
             pltpu.VMEM((64, 2048), half),
             pltpu.VMEM((2, 10, 64, 256), half),
             pltpu.VMEM((2, 10, 64, 512), half),
             pltpu.VMEM((1024, 512), half),
-            pltpu.VMEM((STREAMS, GROUP_A, GROUP_Y, 8, 128), wide),
-            pltpu.VMEM((STREAMS, GROUP_A - 1, GROUP_Y, 8, 128), wide),
+            pltpu.VMEM((STREAMS, GROUP_A, GROUP_Y, 8, 128), half),
+            pltpu.VMEM((STREAMS, GROUP_A - 1, GROUP_Y, 8, 128), half),
             pltpu.VMEM((STREAMS, GROUP_Y, 8, 128), wide),
             pltpu.VMEM((STREAMS, GROUP_Y - 1, 8, 128), wide),
             pltpu.VMEM((STREAMS, Z_COUNT, 8, 128), wide),
@@ -546,10 +587,13 @@
             dma((COPIES,)),
             dma((COPIES,)),
             dma((STREAMS,)),
+            dma((len(arrays),)),
         ],
-        compiler_params=pltpu.CompilerParams(collective_id=0, has_side_effects=True),
+        compiler_params=pltpu.CompilerParams(
+            collective_id=0, has_side_effects=True, vmem_limit_bytes=MAIN_VMEM
+        ),
         name="main",
-    )(counts, index, owners, *arrays)
+    )(*[pltpu.with_memory_space_constraint(x, pltpu.HBM) for x in arrays])
 
 
 def finish_kernel(
@@ -597,6 +641,7 @@
         ),
         in_specs=[vmem] * 3,
         out_specs=(vmem,) * 5,
+        compiler_params=pltpu.CompilerParams(vmem_limit_bytes=FINISH_VMEM),
         name="finish",
     )(total, rows_in, proj_t)
 
@@ -616,22 +661,22 @@
     wide, narrow, fine, edge, cols, order = tap_select()
     proj_t = proj_weight.T
     total, rows_in = main(
-        counts.reshape(2),
-        vis_index.reshape(2, 64),
-        owners.reshape(2, 1, 64),
         [
+            cotangent,
+            cols,
+            saved_pre,
+            edge,
+            counts.reshape(2),
+            vis_index.reshape(2, 64),
+            owners.reshape(2, 1, 64),
             tokens.reshape(128, 768),
             mask_token,
             proj_t,
             up_first.reshape(1024, 64),
             up_second.transpose(0, 2, 1, 3),
-            cotangent,
-            saved_pre,
             wide,
             narrow,
             fine,
-            edge,
-            cols,
             order,
         ],
     )

time: 68.8 us -> 64.2 us (0.933)
  Pallas kernels: 68 us -> 63.4 us
    pallas_call x1, Pallas kernels: 65.7 us -> 62 us  [main(): pl.pallas_call(main_kernel, out_shape=(jax.ShapeDtypeStruct((STREAMS, GRO...]
    pallas_call x1, Pallas kernels: 2.33 us -> 1.33 us  [finish(): pl.pallas_call(finish_kernel, out_shape=(jax.ShapeDtypeStruct((192, 768),...]
where the time goes in v5:
time: 64.2 us; the launch traced here: 64 us
  Pallas kernels  63.4 us (99%)
  between operations  0.66 us (1%)
    pallas_call x1, Pallas kernels, main(): pl.pallas_call(main_kernel, out_shape=(jax.ShapeDtypeStruct((STREAMS, GRO...  62 us
    pallas_call x1, Pallas kernels, finish(): pl.pallas_call(finish_kernel, out_shape=(jax.ShapeDtypeStruct((192, 768),...  1.33 us

profile of v5, /device:TPU:1, one launch (start us, length us, event | category | flops | bytes accessed | tf_op | source)
XLA Modules:
  0.0 64.0 jit_solution(10062624308077025952)
XLA Ops:
  0.6 0.0 copy-start
  0.6 62.0 %main.1 = (bf16[2,8,8,8,128]{4,3,2,1,0:T(8,128)(2,1)S(1)}, bf16[8,16,128]{2,1,0:T(8,128)(2,1)S(1)}) custom-call(bf16[2,12,16,256]{3,2,1,0:T(8,128)(2,1)} %refs_0_.1, bf16[16,256]{1,0:T(8,128)(2,1)} %constant.16.clone.refs_1_, bf16[2,64,8,128]{3,2,1,0:T(8,128)(2,1)} %refs_2_.1, bf16[2048,128]{1,0:T(8,128)(2,1)} %constant.15.clone.refs_3_, s32[2]{0:T(128)} %bitcast.20, ...), custom_call_target="tpu_custom_call" | custom-call | tf_op jit(solution)/shard_map/main/pallas_call | solution.py:547
  62.7 0.0 copy-done
  62.7 1.3 %finish.1 = (bf16[192,768]{1,0:T(8,128)(2,1)}, f32[64,768]{1,0:T(8,128)}, f32[1024,64]{1,0:T(8,128)}, f32[4,12,4,64]{3,2,1,0:T(4,128)}, f32[768]{0:T(1024)}) custom-call(bf16[2,8,8,8,128]{4,3,2,1,0:T(8,128)(2,1)S(1)} %get-tuple-element.12.total, bf16[8,16,128]{2,1,0:T(8,128)(2,1)S(1)} %get-tuple-element.13.rows_in, bf16[64,768]{1,0:T(8,128)(2,1)S(1)} %bitcast.14), custom_call_target="tpu_custom_call" | custom-call | tf_op jit(solution)/shard_map/finish/pallas_call | solution.py:633
Async XLA Ops:
  0.6 62.1 %copy-start = (bf16[768,64]{0,1:T(8,128)(2,1)S(1)}, bf16[768,64]{0,1:T(8,128)(2,1)}, u32[]{:S(2)}) copy-start(bf16[768,64]{0,1:T(8,128)(2,1)} %param.21) | copy-start | bytes 294916

commit v6 on v5

--- a/solution.py
+++ b/solution.py
@@ -34,14 +34,17 @@
         for cell in range(64):
             col = 2 * cell + tap - 1
             fine[col if col >= 0 else 255, tap, :, cell] = 1
-    edge = np.zeros((2, 8, 128, 128), np.float32)
+    edge = np.zeros((8, 2, 16, 128), np.float32)
+    place = np.zeros((2, 16, 2, 128), np.float32)
+    for row in range(8):
+        for spot in [row + 1] + ([0] if row == 7 else []) + ([9] if row == 0 else []):
+            edge[row, 0, spot, 0] = 1
+            edge[row, 1, spot, 127] = 1
     for frame in range(2):
-        for row in range(8):
-            spots = [row + 1] + ([0] if row == 7 else []) + ([9] if row == 0 else [])
-            for spot in spots:
-                pair = 2 * (frame * 10 + spot)
-                edge[frame, row, 0, pair] = 1
-                edge[frame, row, 127, (pair - 1) % 128] = 1
+        for spot in range(10):
+            pair = 2 * (frame * 10 + spot)
+            place[0, spot, frame, pair] = 1
+            place[1, spot, frame, (pair - 1) % 128] = 1
     cols = np.zeros((16, 256), np.float32)
     for k in range(3):
         cols[k, k] = 1
@@ -56,7 +59,8 @@
         jnp.asarray(wide.reshape(256, 1024), half),
         jnp.asarray(halo.reshape(16, 1024), half),
         jnp.asarray(fine.reshape(256, 512), half),
-        jnp.asarray(edge.reshape(2048, 128), half),
+        jnp.asarray(edge.reshape(8, 32, 128), half),
+        jnp.asarray(place.reshape(32, 256), half),
         jnp.asarray(cols, half),
         jnp.asarray(order.reshape(192, 256), half),
     )
@@ -96,7 +100,7 @@
 EARLY = 4
 MAIN_VMEM = 24 * 1024 * 1024
 FINISH_VMEM = 8 * 1024 * 1024
-OPERANDS = tuple(range(16))
+OPERANDS = tuple(range(17))
 
 
 def main_kernel(*refs):
@@ -120,6 +124,7 @@
         narrow,
         fine,
         order,
+        place,
     ) = held
     (
         wide_c,
@@ -131,6 +136,7 @@
         rows_c,
         rows_p,
         cols_c,
+        corners_c,
         cols_p,
         slopes,
         taps,
@@ -201,6 +207,7 @@
 
     later = fetch_all(pairs[EARLY:], fetch, EARLY)
     used = [0]
+    sent = []
 
     def put(src, dst, target):
         slot = used[0]
@@ -214,7 +221,12 @@
             device_id_type=MESH,
         )
         copy.start()
+        sent.append(copy)
         return copy
+
+    def wait_here(copies):
+        for copy in copies:
+            copy.wait_recv()
 
     wait_all(early)
     for f in range(2):
@@ -232,36 +244,74 @@
                 ].astype(half)
         for part in range(2):
             block = cot_rows[f, part * 8 : part * 8 + 8].reshape(128, 256)
-            cot_cols[f, part] = dot_nt(cols[...], block).astype(half)
+            packed = dot_nt(cols[...], block).astype(half)
+            cot_cols[0, f, part] = packed[0:8]
+            cot_cols[1, f, part] = packed[8:16]
     for f in range(2):
         wide_p[pl.ds(f * 512, 512), :] = pre[f].reshape(512, 128).astype(jnp.float32)
-    packed = jnp.zeros((64, 128), jnp.float32)
-    for f in range(2):
-        for i in range(8):
-            slab = wide_p[pl.ds(f * 512 + i, 64, stride=8), :].astype(half)
-            pre_rows[f, i] = slab
-            packed = packed + dot_nn(slab, edge[pl.ds((f * 8 + i) * 128, 128), :])
-    pre_cols[...] = packed.astype(half)
+    packed = jnp.zeros((32, 128), jnp.float32)
+    for i in range(8):
+        slabs = [wide_p[pl.ds(f * 512 + i, 64, stride=8), :].astype(half) for f in range(2)]
+        for f in range(2):
+            pre_rows[f, i] = slabs[f]
+        packed = packed + dot_nt(edge[i], jnp.concatenate(slabs, axis=0))
+    pre_cols[...] = packed.astype(half).reshape(2, 16, 128)
 
     pl.semaphore_wait(barrier, len(SIDES) + GROUP_A + GROUP_Y + Z_COUNT - 3)
 
     halo = []
-    halo.append(put(cot_cols, cols_c.at[1], peer_side((0, -1))))
-    halo.append(put(cot_cols, cols_c.at[0], peer_side((0, 1))))
-    halo.append(put(pre_cols, cols_p.at[1], peer_side((0, -1))))
-    halo.append(put(pre_cols, cols_p.at[0], peer_side((0, 1))))
-    halo.append(put(cot_cols, cols_c.at[5], peer_side((-1, -1))))
-    halo.append(put(cot_cols, cols_c.at[4], peer_side((-1, 1))))
-    halo.append(put(cot_cols, cols_c.at[3], peer_side((1, -1))))
-    halo.append(put(cot_cols, cols_c.at[2], peer_side((1, 1))))
-    halo.append(put(pre_cols, cols_p.at[5], peer_side((-1, -1))))
-    halo.append(put(pre_cols, cols_p.at[4], peer_side((-1, 1))))
-    halo.append(put(pre_cols, cols_p.at[3], peer_side((1, -1))))
-    halo.append(put(pre_cols, cols_p.at[2], peer_side((1, 1))))
-    halo.append(put(cot_rows.at[:, 0:3], rows_c.at[1], peer_side((-1, 0))))
-    halo.append(put(cot_rows.at[:, 13:16], rows_c.at[0], peer_side((1, 0))))
-    halo.append(put(pre_rows.at[:, 0], rows_p.at[1], peer_side((-1, 0))))
-    halo.append(put(pre_rows.at[:, 7], rows_p.at[0], peer_side((1, 0))))
+
+    def edge_put(src, dst, side):
+        slot = used[0]
+        used[0] += 1
+        copy = pltpu.make_async_remote_copy(
+            src_ref=src,
+            dst_ref=dst,
+            send_sem=send.at[slot],
+            recv_sem=recv.at[slot],
+            device_id=peer_side(side),
+            device_id_type=MESH,
+        )
+        halo.append((side, copy))
+
+    edge_put(cot_cols.at[0], cols_c.at[1], (0, -1))
+    edge_put(pre_cols.at[0], cols_p.at[1], (0, -1))
+    edge_put(cot_cols.at[1], cols_c.at[0], (0, 1))
+    edge_put(pre_cols.at[1], cols_p.at[0], (0, 1))
+    edge_put(cot_cols.at[0, :, 0], corners_c.at[3], (-1, -1))
+    edge_put(pre_cols.at[0], cols_p.at[5], (-1, -1))
+    edge_put(cot_cols.at[1, :, 0], corners_c.at[2], (-1, 1))
+    edge_put(pre_cols.at[1], cols_p.at[4], (-1, 1))
+    edge_put(cot_cols.at[0, :, 1], corners_c.at[1], (1, -1))
+    edge_put(pre_cols.at[0], cols_p.at[3], (1, -1))
+    edge_put(cot_cols.at[1, :, 1], corners_c.at[0], (1, 1))
+    edge_put(pre_cols.at[1], cols_p.at[2], (1, 1))
+    edge_put(cot_rows.at[:, 0:3], rows_c.at[1], (-1, 0))
+    edge_put(pre_rows.at[:, 0], rows_p.at[1], (-1, 0))
+    edge_put(cot_rows.at[:, 13:16], rows_c.at[0], (1, 0))
+    edge_put(pre_rows.at[:, 7], rows_p.at[0], (1, 0))
+
+    north = n > 0
+    south = n < n_count - 1
+    west = e > 0
+    east = e < e_count - 1
+
+    def inside(side):
+        by_row = {-1: north, 0: None, 1: south}[side[0]]
+        by_column = {-1: west, 0: None, 1: east}[side[1]]
+        if by_row is None:
+            return by_column
+        if by_column is None:
+            return by_row
+        return jnp.logical_and(by_row, by_column)
+
+    for way in ((0, -1), (0, 1), (-1, -1), (-1, 1), (1, -1), (1, 1), (-1, 0), (1, 0)):
+
+        @pl.when(inside(way))
+        def _(way=way):
+            for side, copy in halo:
+                if side == way:
+                    copy.start()
 
     wait_all(later)
 
@@ -311,22 +361,20 @@
     even = jnp.where(number == target, 1.0, 0.0).astype(half)
     odd = jnp.where(number + 1.0 == target, 1.0, 0.0).astype(half)
 
-    wait_all(halo)
-
-    north = n > 0
-    south = n < n_count - 1
-    west = e > 0
-    east = e < e_count - 1
-
-    def flag(condition, shape):
-        return jnp.full(shape, jnp.where(condition, 1.0, 0.0), jnp.float32)
-
-    row_16 = lax.broadcasted_iota(jnp.int32, (16, 128), 0)
+    for way in SIDES:
+
+        @pl.when(inside((-way[0], -way[1])))
+        def _(way=way):
+            for side, copy in halo:
+                if side == way:
+                    copy.wait_recv()
+
+    def only(condition, value):
+        chosen_lanes = jnp.full(value.shape, jnp.where(condition, 1.0, 0.0), jnp.float32) > 0.5
+        return jnp.where(chosen_lanes, value.astype(jnp.float32), 0.0)
 
     def side_cols(west_block, east_block):
-        east_part = east_block.astype(jnp.float32) * flag(east, (16, 128))
-        west_part = west_block.astype(jnp.float32) * flag(west, (16, 128))
-        return jnp.where(row_16 < 8, east_part, west_part).astype(half)
+        return jnp.concatenate([only(east, east_block), only(west, west_block)], axis=0).astype(half)
 
     wide_map = wide[...]
     narrow_map = narrow[...]
@@ -337,26 +385,27 @@
             value = value + dot_tn(side, narrow_map)
             taps[f, 3 + part * 8 : 11 + part * 8] = value.astype(half).reshape(8, 16, 1024)
         value = dot_nn(rows_c[0, f].reshape(48, 256), wide_map)
-        side = side_cols(cols_c[2, f, 1], cols_c[3, f, 1])
-        value = (value + dot_tn(side, narrow_map)[80:128]) * flag(north, (48, 1024))
+        side = side_cols(corners_c[0, f], corners_c[1, f])
+        value = only(north, value + dot_tn(side, narrow_map)[80:128])
         taps[f, 0:3] = value.astype(half).reshape(3, 16, 1024)
         value = dot_nn(rows_c[1, f].reshape(48, 256), wide_map)
-        side = side_cols(cols_c[4, f, 0], cols_c[5, f, 0])
-        value = (value + dot_tn(side, narrow_map)[0:48]) * flag(south, (48, 1024))
+        side = side_cols(corners_c[2, f], corners_c[3, f])
+        value = only(south, value + dot_tn(side, narrow_map)[0:48])
         taps[f, 19:22] = value.astype(half).reshape(3, 16, 1024)
 
     lane = lax.broadcasted_iota(jnp.int32, (64, 128), 1)
-    spot = lax.rem(lax.rem(lax.div(lane + 1, 2), 64), 10)
-    right = lax.rem(lane, 2) == 0
-    halo_pre = jnp.where(
-        spot == 0,
-        jnp.where(right, cols_p[3].astype(jnp.float32), cols_p[2].astype(jnp.float32)),
-        jnp.where(
-            spot == 9,
-            jnp.where(right, cols_p[5].astype(jnp.float32), cols_p[4].astype(jnp.float32)),
-            jnp.where(right, cols_p[1].astype(jnp.float32), cols_p[0].astype(jnp.float32)),
-        ),
-    )
+    spot = lax.broadcasted_iota(jnp.int32, (16, 128), 0)
+
+    def side_rows(condition, upper, middle, lower):
+        value = jnp.where(spot == 9, only(south, lower), middle.astype(jnp.float32))
+        return only(condition, jnp.where(spot == 0, only(north, upper), value))
+
+    side = jnp.concatenate(
+        [side_rows(east, cols_p[3], cols_p[1], cols_p[5]), side_rows(west, cols_p[2], cols_p[0], cols_p[4])],
+        axis=0,
+    ).astype(half)
+    placed = dot_tn(side, place[...])
+    halo_pre = placed[0:64, 0:128] + placed[64:128, 128:256]
     halo_keep = jnp.where(
         lane == 0, jnp.where(east, 1.0, 0.0), jnp.where(lane == 127, jnp.where(west, 1.0, 0.0), 0.0)
     )
@@ -387,11 +436,11 @@
                 edge_slope = pltpu.roll(halo_slope, 128 - 2 * (f * 10 + i), 1)
             edge_value = grad[:, 128:] * edge_slope * halo_keep
             if i == 0:
-                value = value * flag(north, value.shape)
-                edge_value = edge_value * flag(north, value.shape)
+                value = only(north, value)
+                edge_value = only(north, edge_value)
             if i == 9:
-                value = value * flag(south, value.shape)
-                edge_value = edge_value * flag(south, value.shape)
+                value = only(south, value)
+                edge_value = only(south, edge_value)
             deltas[f, i, :, 0:128] = value.astype(half)
             deltas[f, i, :, 128:256] = edge_value.astype(half)
 
@@ -465,7 +514,7 @@
 
     copies_b = []
     for s in range(STREAMS):
-        wait_all(copies_a[s])
+        wait_here(copies_a[s])
         summed = payload[s, g].astype(jnp.float32)
         for k in range(1, GROUP_A):
             summed = summed + buf_a[s, k - 1].astype(jnp.float32)
@@ -476,7 +525,7 @@
             copies.append(put(red_a.at[s, other], buf_b.at[s, k - 1], target_device))
         copies_b.append(copies)
 
-    wait_all(copies_z)
+    wait_here(copies_z)
     stacked = tok_z[...].reshape(Z_LOW * 16, 128)
     picked = lax.broadcasted_iota(jnp.int32, (GROUP_A * 16, Z_LOW * 16), 0)
     column = lax.broadcasted_iota(jnp.int32, (GROUP_A * 16, Z_LOW * 16), 1)
@@ -491,7 +540,7 @@
 
     copies_c = []
     for s in range(STREAMS):
-        wait_all(copies_b[s])
+        wait_here(copies_b[s])
         summed = red_a[s, y]
         for k in range(1, GROUP_Y):
             summed = summed + buf_b[s, k - 1]
@@ -504,7 +553,7 @@
     row_8 = lax.broadcasted_iota(jnp.int32, (8, 128), 0)
     copies_d = []
     for s in range(STREAMS):
-        wait_all(copies_c[s])
+        wait_here(copies_c[s])
         summed = buf_c[s, 0]
         for k in range(1, Z_COUNT):
             summed = summed + buf_c[s, k]
@@ -523,16 +572,25 @@
     copies_e = []
     own = []
     for s in range(STREAMS):
-        wait_all(copies_d[s])
+        wait_here(copies_d[s])
         for k in range(1, GROUP_A):
             copies_e.append(put(buf_d.at[s], total_out.at[s, g], peer_a(k)[1]))
         copy = pltpu.make_async_copy(buf_d.at[s], total_out.at[s, g], local_sem.at[s])
         copy.start()
         own.append(copy)
-    wait_all(copies_t)
+    wait_here(copies_t)
     rows_in[...] = buf_s[...]
+    wait_here(copies_e)
     wait_all(own)
-    wait_all(copies_e)
+    for copy in sent:
+        copy.wait_send()
+    for way in SIDES:
+
+        @pl.when(inside(way))
+        def _(way=way):
+            for side, copy in halo:
+                if side == way:
+                    copy.wait_send()
 
 
 COPIES = 16 + 2 * (2 * (GROUP_A - 1) + 2 * (GROUP_Y - 1) + Z_COUNT - 1) + Z_LOW - 1 + GROUP_A - 1
@@ -560,13 +618,14 @@
             pltpu.VMEM((2, 512, 128), wide),
             pltpu.VMEM((1024, 128), wide),
             pltpu.VMEM((2, 16, 16, 256), half),
-            pltpu.VMEM((2, 2, 16, 128), half),
+            pltpu.VMEM((2, 2, 2, 8, 128), half),
             pltpu.VMEM((2, 8, 64, 128), half),
-            pltpu.VMEM((64, 128), half),
+            pltpu.VMEM((2, 16, 128), half),
             pltpu.VMEM((2, 2, 3, 16, 256), half),
             pltpu.VMEM((2, 2, 64, 128), half),
-            pltpu.VMEM((6, 2, 2, 16, 128), half),
-            pltpu.VMEM((6, 64, 128), half),
+            pltpu.VMEM((2, 2, 2, 8, 128), half),
+            pltpu.VMEM((4, 2, 8, 128), half),
+            pltpu.VMEM((6, 16, 128), half),
             pltpu.VMEM((2, 8, 64, 128), wide),
             pltpu.VMEM((2, 22, 16, 1024), half),
             pltpu.VMEM((256, 2048), half),
@@ -658,7 +717,7 @@
     saved_pre,
     cotangent,
 ):
-    wide, narrow, fine, edge, cols, order = tap_select()
+    wide, narrow, fine, edge, place, cols, order = tap_select()
     proj_t = proj_weight.T
     total, rows_in = main(
         [
@@ -678,6 +737,7 @@
             narrow,
             fine,
             order,
+            place,
         ],
     )
     token_grad, grad_proj, grad_first, grad_second, grad_mask = finish(total, rows_in, proj_t)

time: 64.2 us -> 58.1 us (0.905)
  Pallas kernels: 63.4 us -> 57.3 us
    pallas_call x1, Pallas kernels: 62 us -> 56 us  [main(): pl.pallas_call(main_kernel, out_shape=(jax.ShapeDtypeStruct((STREAMS, GRO...]
where the time goes in v6:
time: 58.1 us; the launch traced here: 58 us
  Pallas kernels  57.3 us (99%)
  between operations  0.66 us (1%)
    pallas_call x1, Pallas kernels, main(): pl.pallas_call(main_kernel, out_shape=(jax.ShapeDtypeStruct((STREAMS, GRO...  56 us
    pallas_call x1, Pallas kernels, finish(): pl.pallas_call(finish_kernel, out_shape=(jax.ShapeDtypeStruct((192, 768),...  1.33 us

profile of v6, /device:TPU:1, one launch (start us, length us, event | category | flops | bytes accessed | tf_op | source)
XLA Modules:
  0.0 58.0 jit_solution(17296065482609810824)
XLA Ops:
  0.6 0.0 copy-start
  0.6 56.0 %main.1 = (bf16[2,8,8,8,128]{4,3,2,1,0:T(8,128)(2,1)S(1)}, bf16[8,16,128]{2,1,0:T(8,128)(2,1)S(1)}) custom-call(bf16[2,12,16,256]{3,2,1,0:T(8,128)(2,1)} %refs_0_.1, bf16[16,256]{1,0:T(8,128)(2,1)} %constant.19.clone.refs_1_, bf16[2,64,8,128]{3,2,1,0:T(8,128)(2,1)} %refs_2_.1, bf16[8,32,128]{2,1,0:T(8,128)(2,1)} %constant.17.clone.refs_3_, s32[2]{0:T(128)} %bitcast.20, ...), custom_call_target="tpu_custom_call" | custom-call | tf_op jit(solution)/shard_map/main/pallas_call | solution.py:605
  56.6 0.0 copy-done
  56.7 1.3 %finish.1 = (bf16[192,768]{1,0:T(8,128)(2,1)}, f32[64,768]{1,0:T(8,128)}, f32[1024,64]{1,0:T(8,128)}, f32[4,12,4,64]{3,2,1,0:T(4,128)}, f32[768]{0:T(1024)}) custom-call(bf16[2,8,8,8,128]{4,3,2,1,0:T(8,128)(2,1)S(1)} %get-tuple-element.12.total, bf16[8,16,128]{2,1,0:T(8,128)(2,1)S(1)} %get-tuple-element.13.rows_in, bf16[64,768]{1,0:T(8,128)(2,1)S(1)} %bitcast.14), custom_call_target="tpu_custom_call" | custom-call | tf_op jit(solution)/shard_map/finish/pallas_call | solution.py:692
Async XLA Ops:
  0.6 56.0 %copy-start = (bf16[768,64]{0,1:T(8,128)(2,1)S(1)}, bf16[768,64]{0,1:T(8,128)(2,1)}, u32[]{:S(2)}) copy-start(bf16[768,64]{0,1:T(8,128)(2,1)} %param.22) | copy-start | bytes 294916

commit v7 on v6

--- a/solution.py
+++ b/solution.py
@@ -19,16 +19,18 @@
 
 def tap_select():
     wide = np.zeros((256, 4, 256), np.float32)
-    halo = np.zeros((16, 4, 256), np.float32)
+    halo = np.zeros((2, 16, 4, 256), np.float32)
     for tap in range(4):
         for lane, cell in [(j, j) for j in range(128)] + [(128, 128), (255, -1)]:
             col = 2 * cell + tap - 1
             if col < 0:
-                halo[8 + col + 3, tap, lane] = 1
+                for frame in range(2):
+                    halo[frame, 8 + frame * 3 + col + 3, tap, lane] = 1
             elif col < 256:
                 wide[col, tap, lane] = 1
             else:
-                halo[col - 256, tap, lane] = 1
+                for frame in range(2):
+                    halo[frame, frame * 3 + col - 256, tap, lane] = 1
     fine = np.zeros((256, 4, 2, 64), np.float32)
     for tap in range(4):
         for cell in range(64):
@@ -37,18 +39,20 @@
     edge = np.zeros((8, 2, 16, 128), np.float32)
     place = np.zeros((2, 16, 2, 128), np.float32)
     for row in range(8):
-        for spot in [row + 1] + ([0] if row == 7 else []) + ([9] if row == 0 else []):
-            edge[row, 0, spot, 0] = 1
-            edge[row, 1, spot, 127] = 1
+        for line in [row] + ([8] if row == 7 else []) + ([9] if row == 0 else []):
+            edge[row, 0, line, 0] = 1
+            edge[row, 1, line, 127] = 1
     for frame in range(2):
         for spot in range(10):
             pair = 2 * (frame * 10 + spot)
-            place[0, spot, frame, pair] = 1
-            place[1, spot, frame, (pair - 1) % 128] = 1
-    cols = np.zeros((16, 256), np.float32)
-    for k in range(3):
-        cols[k, k] = 1
-        cols[8 + k, 253 + k] = 1
+            line = {0: 8, 9: 9}.get(spot, spot - 1)
+            place[0, line, frame, pair] = 1
+            place[1, line, frame, (pair - 1) % 128] = 1
+    cols = np.zeros((2, 16, 256), np.float32)
+    for frame in range(2):
+        for k in range(3):
+            cols[frame, frame * 3 + k, k] = 1
+            cols[frame, 8 + frame * 3 + k, 253 + k] = 1
     order = np.zeros((4, 12, 4, 4, 4, 16), np.float32)
     for a in range(4):
         for o in range(12):
@@ -57,7 +61,7 @@
     half = jnp.bfloat16
     return (
         jnp.asarray(wide.reshape(256, 1024), half),
-        jnp.asarray(halo.reshape(16, 1024), half),
+        jnp.asarray(halo.reshape(2, 16, 1024), half),
         jnp.asarray(fine.reshape(256, 512), half),
         jnp.asarray(edge.reshape(8, 32, 128), half),
         jnp.asarray(place.reshape(32, 256), half),
@@ -130,14 +134,12 @@
         wide_c,
         wide_p,
         cot_rows,
-        cot_cols,
+        packs,
         pre_rows,
-        pre_cols,
         rows_c,
         rows_p,
         cols_c,
-        corners_c,
-        cols_p,
+        corners,
         slopes,
         taps,
         windows,
@@ -199,9 +201,11 @@
     pairs = tuple(zip(sources, held))
     early = fetch_all(pairs[:EARLY], fetch, 0)
     barrier = pltpu.get_barrier_semaphore()
-    for side in SIDES:
+    for k in (6, 5, 7, 4, 8, 3, 9, 2, 10, 1, 11):
+        pl.semaphore_signal(barrier, inc=1, device_id=peer_c(k)[1], device_id_type=MESH)
+    for side in reversed(SIDES):
         pl.semaphore_signal(barrier, inc=1, device_id=peer_side(side), device_id_type=MESH)
-    for count, peer in ((GROUP_A, peer_a), (GROUP_Y, peer_b), (Z_COUNT, peer_c)):
+    for count, peer in ((GROUP_Y, peer_b), (GROUP_A, peer_a)):
         for k in range(1, count):
             pl.semaphore_signal(barrier, inc=1, device_id=peer(k)[1], device_id_type=MESH)
 
@@ -242,11 +246,13 @@
                 cot_rows[f, r, :, part * 128 : part * 128 + 128] = wide_c[
                     part, pl.ds(f * 256 + r, 16, stride=16), :
                 ].astype(half)
-        for part in range(2):
+    for part in range(2):
+        packed = jnp.zeros((16, 128), jnp.float32)
+        for f in range(2):
             block = cot_rows[f, part * 8 : part * 8 + 8].reshape(128, 256)
-            packed = dot_nt(cols[...], block).astype(half)
-            cot_cols[0, f, part] = packed[0:8]
-            cot_cols[1, f, part] = packed[8:16]
+            packed = packed + dot_nt(cols[f], block)
+        for side in range(2):
+            packs[side, 1 + 2 * part] = packed[side * 8 : side * 8 + 8].astype(half)
     for f in range(2):
         wide_p[pl.ds(f * 512, 512), :] = pre[f].reshape(512, 128).astype(jnp.float32)
     packed = jnp.zeros((32, 128), jnp.float32)
@@ -255,7 +261,11 @@
         for f in range(2):
             pre_rows[f, i] = slabs[f]
         packed = packed + dot_nt(edge[i], jnp.concatenate(slabs, axis=0))
-    pre_cols[...] = packed.astype(half).reshape(2, 16, 128)
+    for side in range(2):
+        packs[side, 2] = packed[side * 16 : side * 16 + 8].astype(half)
+        corner = packed[side * 16 + 8 : side * 16 + 16].astype(half)
+        packs[side, 0] = corner
+        packs[side, 4] = corner
 
     pl.semaphore_wait(barrier, len(SIDES) + GROUP_A + GROUP_Y + Z_COUNT - 3)
 
@@ -274,18 +284,12 @@
         )
         halo.append((side, copy))
 
-    edge_put(cot_cols.at[0], cols_c.at[1], (0, -1))
-    edge_put(pre_cols.at[0], cols_p.at[1], (0, -1))
-    edge_put(cot_cols.at[1], cols_c.at[0], (0, 1))
-    edge_put(pre_cols.at[1], cols_p.at[0], (0, 1))
-    edge_put(cot_cols.at[0, :, 0], corners_c.at[3], (-1, -1))
-    edge_put(pre_cols.at[0], cols_p.at[5], (-1, -1))
-    edge_put(cot_cols.at[1, :, 0], corners_c.at[2], (-1, 1))
-    edge_put(pre_cols.at[1], cols_p.at[4], (-1, 1))
-    edge_put(cot_cols.at[0, :, 1], corners_c.at[1], (1, -1))
-    edge_put(pre_cols.at[0], cols_p.at[3], (1, -1))
-    edge_put(cot_cols.at[1, :, 1], corners_c.at[0], (1, 1))
-    edge_put(pre_cols.at[1], cols_p.at[2], (1, 1))
+    edge_put(packs.at[0, 1:4], cols_c.at[1], (0, -1))
+    edge_put(packs.at[1, 1:4], cols_c.at[0], (0, 1))
+    edge_put(packs.at[0, 0:2], corners.at[3], (-1, -1))
+    edge_put(packs.at[1, 0:2], corners.at[2], (-1, 1))
+    edge_put(packs.at[0, 3:5], corners.at[1], (1, -1))
+    edge_put(packs.at[1, 3:5], corners.at[0], (1, 1))
     edge_put(cot_rows.at[:, 0:3], rows_c.at[1], (-1, 0))
     edge_put(pre_rows.at[:, 0], rows_p.at[1], (-1, 0))
     edge_put(cot_rows.at[:, 13:16], rows_c.at[0], (1, 0))
@@ -377,31 +381,33 @@
         return jnp.concatenate([only(east, east_block), only(west, west_block)], axis=0).astype(half)
 
     wide_map = wide[...]
-    narrow_map = narrow[...]
     for f in range(2):
+        narrow_map = narrow[f]
         for part in range(2):
             value = dot_nn(cot_rows[f, part * 8 : part * 8 + 8].reshape(128, 256), wide_map)
-            side = side_cols(cols_c[0, f, part], cols_c[1, f, part])
+            side = side_cols(cols_c[0, 2 * part], cols_c[1, 2 * part])
             value = value + dot_tn(side, narrow_map)
             taps[f, 3 + part * 8 : 11 + part * 8] = value.astype(half).reshape(8, 16, 1024)
         value = dot_nn(rows_c[0, f].reshape(48, 256), wide_map)
-        side = side_cols(corners_c[0, f], corners_c[1, f])
+        side = side_cols(corners[0, 0], corners[1, 0])
         value = only(north, value + dot_tn(side, narrow_map)[80:128])
         taps[f, 0:3] = value.astype(half).reshape(3, 16, 1024)
         value = dot_nn(rows_c[1, f].reshape(48, 256), wide_map)
-        side = side_cols(corners_c[2, f], corners_c[3, f])
+        side = side_cols(corners[2, 1], corners[3, 1])
         value = only(south, value + dot_tn(side, narrow_map)[0:48])
         taps[f, 19:22] = value.astype(half).reshape(3, 16, 1024)
 
     lane = lax.broadcasted_iota(jnp.int32, (64, 128), 1)
-    spot = lax.broadcasted_iota(jnp.int32, (16, 128), 0)
+    line = lax.broadcasted_iota(jnp.int32, (8, 128), 0)
 
     def side_rows(condition, upper, middle, lower):
-        value = jnp.where(spot == 9, only(south, lower), middle.astype(jnp.float32))
-        return only(condition, jnp.where(spot == 0, only(north, upper), value))
+        corner = jnp.where(line == 0, only(north, upper), 0.0)
+        corner = jnp.where(line == 1, only(south, lower), corner)
+        return [only(condition, middle), only(condition, corner)]
 
     side = jnp.concatenate(
-        [side_rows(east, cols_p[3], cols_p[1], cols_p[5]), side_rows(west, cols_p[2], cols_p[0], cols_p[4])],
+        side_rows(east, corners[1, 1], cols_c[1, 1], corners[3, 0])
+        + side_rows(west, corners[0, 1], cols_c[0, 1], corners[2, 0]),
         axis=0,
     ).astype(half)
     placed = dot_tn(side, place[...])
@@ -593,7 +599,7 @@
                     copy.wait_send()
 
 
-COPIES = 16 + 2 * (2 * (GROUP_A - 1) + 2 * (GROUP_Y - 1) + Z_COUNT - 1) + Z_LOW - 1 + GROUP_A - 1
+COPIES = 10 + 2 * (2 * (GROUP_A - 1) + 2 * (GROUP_Y - 1) + Z_COUNT - 1) + Z_LOW - 1 + GROUP_A - 1
 
 
 def main(arrays):
@@ -618,14 +624,12 @@
             pltpu.VMEM((2, 512, 128), wide),
             pltpu.VMEM((1024, 128), wide),
             pltpu.VMEM((2, 16, 16, 256), half),
-            pltpu.VMEM((2, 2, 2, 8, 128), half),
+            pltpu.VMEM((2, 5, 8, 128), half),
             pltpu.VMEM((2, 8, 64, 128), half),
-            pltpu.VMEM((2, 16, 128), half),
             pltpu.VMEM((2, 2, 3, 16, 256), half),
             pltpu.VMEM((2, 2, 64, 128), half),
-            pltpu.VMEM((2, 2, 2, 8, 128), half),
+            pltpu.VMEM((2, 3, 8, 128), half),
             pltpu.VMEM((4, 2, 8, 128), half),
-            pltpu.VMEM((6, 16, 128), half),
             pltpu.VMEM((2, 8, 64, 128), wide),
             pltpu.VMEM((2, 22, 16, 1024), half),
             pltpu.VMEM((256, 2048), half),

time: 58.1 us -> 57.6 us (level)
  no operation moved by 1% of the time
where the time goes in v7:
time: 57.6 us; the launch traced here: 57.5 us
  Pallas kernels  56.8 us (99%)
  between operations  0.66 us (1%)
    pallas_call x1, Pallas kernels, main(): pl.pallas_call(main_kernel, out_shape=(jax.ShapeDtypeStruct((STREAMS, GRO...  55.5 us
    pallas_call x1, Pallas kernels, finish(): pl.pallas_call(finish_kernel, out_shape=(jax.ShapeDtypeStruct((192, 768),...  1.33 us

profile of v7, /device:TPU:1, one launch (start us, length us, event | category | flops | bytes accessed | tf_op | source)
XLA Modules:
  0.0 57.5 jit_solution(3302176095203289480)
XLA Ops:
  0.6 0.0 copy-start
  0.6 55.5 %main.1 = (bf16[2,8,8,8,128]{4,3,2,1,0:T(8,128)(2,1)S(1)}, bf16[8,16,128]{2,1,0:T(8,128)(2,1)S(1)}) custom-call(bf16[2,12,16,256]{3,2,1,0:T(8,128)(2,1)} %refs_0_.1, bf16[2,16,256]{2,1,0:T(8,128)(2,1)} %constant.19.clone.refs_1_, bf16[2,64,8,128]{3,2,1,0:T(8,128)(2,1)} %refs_2_.1, bf16[8,32,128]{2,1,0:T(8,128)(2,1)} %constant.17.clone.refs_3_, s32[2]{0:T(128)} %bitcast.20, ...), custom_call_target="tpu_custom_call" | custom-call | tf_op jit(solution)/shard_map/main/pallas_call | solution.py:611
  56.1 0.0 copy-done
  56.1 1.3 %finish.1 = (bf16[192,768]{1,0:T(8,128)(2,1)}, f32[64,768]{1,0:T(8,128)}, f32[1024,64]{1,0:T(8,128)}, f32[4,12,4,64]{3,2,1,0:T(4,128)}, f32[768]{0:T(1024)}) custom-call(bf16[2,8,8,8,128]{4,3,2,1,0:T(8,128)(2,1)S(1)} %get-tuple-element.12.total, bf16[8,16,128]{2,1,0:T(8,128)(2,1)S(1)} %get-tuple-element.13.rows_in, bf16[64,768]{1,0:T(8,128)(2,1)S(1)} %bitcast.14), custom_call_target="tpu_custom_call" | custom-call | tf_op jit(solution)/shard_map/finish/pallas_call | solution.py:696
Async XLA Ops:
  0.6 55.5 %copy-start = (bf16[768,64]{0,1:T(8,128)(2,1)S(1)}, bf16[768,64]{0,1:T(8,128)(2,1)}, u32[]{:S(2)}) copy-start(bf16[768,64]{0,1:T(8,128)(2,1)} %param.22) | copy-start | bytes 294916

commit v8 on v7

--- a/solution.py
+++ b/solution.py
@@ -365,13 +365,16 @@
     even = jnp.where(number == target, 1.0, 0.0).astype(half)
     odd = jnp.where(number + 1.0 == target, 1.0, 0.0).astype(half)
 
-    for way in SIDES:
-
-        @pl.when(inside((-way[0], -way[1])))
-        def _(way=way):
-            for side, copy in halo:
-                if side == way:
-                    copy.wait_recv()
+    def wait_sides(ways):
+        for way in ways:
+
+            @pl.when(inside((-way[0], -way[1])))
+            def _(way=way):
+                for side, copy in halo:
+                    if side == way:
+                        copy.wait_recv()
+
+    wait_sides(SIDES[:2])
 
     def only(condition, value):
         chosen_lanes = jnp.full(value.shape, jnp.where(condition, 1.0, 0.0), jnp.float32) > 0.5
@@ -382,20 +385,32 @@
 
     wide_map = wide[...]
     for f in range(2):
-        narrow_map = narrow[f]
         for part in range(2):
             value = dot_nn(cot_rows[f, part * 8 : part * 8 + 8].reshape(128, 256), wide_map)
-            side = side_cols(cols_c[0, 2 * part], cols_c[1, 2 * part])
-            value = value + dot_tn(side, narrow_map)
             taps[f, 3 + part * 8 : 11 + part * 8] = value.astype(half).reshape(8, 16, 1024)
-        value = dot_nn(rows_c[0, f].reshape(48, 256), wide_map)
-        side = side_cols(corners[0, 0], corners[1, 0])
-        value = only(north, value + dot_tn(side, narrow_map)[80:128])
+        value = only(north, dot_nn(rows_c[0, f].reshape(48, 256), wide_map))
         taps[f, 0:3] = value.astype(half).reshape(3, 16, 1024)
-        value = dot_nn(rows_c[1, f].reshape(48, 256), wide_map)
-        side = side_cols(corners[2, 1], corners[3, 1])
-        value = only(south, value + dot_tn(side, narrow_map)[0:48])
+        value = only(south, dot_nn(rows_c[1, f].reshape(48, 256), wide_map))
         taps[f, 19:22] = value.astype(half).reshape(3, 16, 1024)
+
+    wait_sides(SIDES[2:])
+
+    blocks = [(3, 11, 0, None, side_cols(cols_c[0, 0], cols_c[1, 0]))]
+    blocks.append((11, 19, 0, None, side_cols(cols_c[0, 2], cols_c[1, 2])))
+    blocks.append((0, 3, 80, north, side_cols(corners[0, 0], corners[1, 0])))
+    blocks.append((19, 22, 0, south, side_cols(corners[2, 1], corners[3, 1])))
+    for f in range(2):
+        for low, high, start, condition, side in blocks:
+            count = high - low
+            for first_lane, last_lane in ((0, 256), (384, 512), (640, 1024)):
+                width = last_lane - first_lane
+                value = dot_tn(side, narrow[f, :, first_lane:last_lane])
+                value = value[start : start + count * 16]
+                if condition is not None:
+                    value = only(condition, value)
+                held_taps = taps[f, low:high, :, first_lane:last_lane].astype(jnp.float32)
+                value = held_taps + value.reshape(count, 16, width)
+                taps[f, low:high, :, first_lane:last_lane] = value.astype(half)
 
     lane = lax.broadcasted_iota(jnp.int32, (64, 128), 1)
     line = lax.broadcasted_iota(jnp.int32, (8, 128), 0)

time: 57.6 us -> 57.3 us (level)
  no operation moved by 1% of the time
where the time goes in v8:
time: 57.3 us; the launch traced here: 57.2 us
  Pallas kernels  56.5 us (99%)
  between operations  0.66 us (1%)
    pallas_call x1, Pallas kernels, main(): pl.pallas_call(main_kernel, out_shape=(jax.ShapeDtypeStruct((STREAMS, GRO...  55.2 us
    pallas_call x1, Pallas kernels, finish(): pl.pallas_call(finish_kernel, out_shape=(jax.ShapeDtypeStruct((192, 768),...  1.33 us

profile of v8, /device:TPU:1, one launch (start us, length us, event | category | flops | bytes accessed | tf_op | source)
XLA Modules:
  0.0 57.2 jit_solution(16298154050244774231)
XLA Ops:
  0.6 0.0 copy-start
  0.6 55.2 %main.1 = (bf16[2,8,8,8,128]{4,3,2,1,0:T(8,128)(2,1)S(1)}, bf16[8,16,128]{2,1,0:T(8,128)(2,1)S(1)}) custom-call(bf16[2,12,16,256]{3,2,1,0:T(8,128)(2,1)} %refs_0_.1, bf16[2,16,256]{2,1,0:T(8,128)(2,1)} %constant.19.clone.refs_1_, bf16[2,64,8,128]{3,2,1,0:T(8,128)(2,1)} %refs_2_.1, bf16[8,32,128]{2,1,0:T(8,128)(2,1)} %constant.17.clone.refs_3_, s32[2]{0:T(128)} %bitcast.20, ...), custom_call_target="tpu_custom_call" | custom-call | tf_op jit(solution)/shard_map/main/pallas_call | solution.py:626
  55.8 0.0 copy-done
  55.8 1.3 %finish.1 = (bf16[192,768]{1,0:T(8,128)(2,1)}, f32[64,768]{1,0:T(8,128)}, f32[1024,64]{1,0:T(8,128)}, f32[4,12,4,64]{3,2,1,0:T(4,128)}, f32[768]{0:T(1024)}) custom-call(bf16[2,8,8,8,128]{4,3,2,1,0:T(8,128)(2,1)S(1)} %get-tuple-element.12.total, bf16[8,16,128]{2,1,0:T(8,128)(2,1)S(1)} %get-tuple-element.13.rows_in, bf16[64,768]{1,0:T(8,128)(2,1)S(1)} %bitcast.14), custom_call_target="tpu_custom_call" | custom-call | tf_op jit(solution)/shard_map/finish/pallas_call | solution.py:711
Async XLA Ops:
  0.6 55.2 %copy-start = (bf16[768,64]{0,1:T(8,128)(2,1)S(1)}, bf16[768,64]{0,1:T(8,128)(2,1)}, u32[]{:S(2)}) copy-start(bf16[768,64]{0,1:T(8,128)(2,1)} %param.22) | copy-start | bytes 294916
